TPU v7x, 256 devices: a whole 4x4x8 slice. The times are simulated.
256 devices in a mesh: rx: 32 (over z, x), tb: 8 (over y, core).
Axes of the slice: x: 4, y: 4, z: 8, core: 2. Of those that a mesh axis runs over, the one named last changes fastest.
Arguments:
- raw_samples: bfloat16 [32, 2, 8192], P('rx', None, 'tb'), may hold values from -3.5 to 3.5
- block_scales: float32 [32, 32], P('rx', 'tb'), may hold values from 0.5 to 2
- lag_window_start: int32 [512, 16], P('rx'), may hold values from 0 to 1008
- doppler_window_start: int32 [512, 16], P('rx'), may hold values from 0 to 31
- peak_owner: int32 [512, 16, 1], P(('rx', 'tb')), may hold values from 0 to 31; in each aligned block of 32 rows (0 to 31, 32 to 63, ..., all dimensions but the last counted through in order) at most 2 rows name the same one
- peak_emitter: int32 [512, 16], P(('rx', 'tb')), may hold values from 0 to 3
- gn_steps: int32 [128], P('rx'), may hold values from 3 to 6
- receiver_pos: float32 [3, 32], replicated, may hold values from -4 to 4
- emitter_start: float32 [3, 128], P(None, 'rx'), may hold values from -4 to 4
Outputs:
- ambiguity: float32 [32, 512, 2, 1024], P('tb', 'rx')
- emitter_pos: float32 [3, 128], P(None, 'rx')
- emitter_vel: float32 [3, 128], P(None, 'rx')
- receiver_clock_bias: float32 [32], replicated
Inputs may be any that keep to these rules, and one draw needn't show every extreme that they name: `peak_owner`: within the aligned blocks of 32 peaks of one device (consecutive pair slots, peaks in order), no owner is named more than 2 times, and in some block an owner is named exactly 2 times.
All inputs are finite; a program needn't handle non-finite values.
Results may differ from a plain program's by a relative error of at most 0.0037.
Values may be sent and summed in bfloat16 or wider, within the bound.
A program may use at most 128 MiB of HBM per device.

v0:
```python
import math

import jax
import jax.numpy as jnp
from jax import lax
from jax.sharding import PartitionSpec as P

SEG = 256
DOPPLER_BINS = 32
LAG_COUNT = 1024
BLK = 256
WL = 16
WD = 4
GN_MAX = 6


highest = lax.Precision.HIGHEST
two_pi = 2.0 * math.pi
damping = 2.0
delay_extent = 16.0
doppler_extent = 4.0


def from_behind(value, axis, steps):
    count = lax.axis_size(axis)
    leading, last = (max(0, -steps), min(count, count - steps))
    return lax.ppermute(value, axis, [(source, source + steps) for source in range(leading, last)])


def passed_along(block, axis, distance):
    devices = range(lax.axis_size(axis))
    route = [((i - distance) % len(devices), i) for i in devices]
    return lax.ppermute(block, axis, route)


def angle_table(row_count, col_count, length):
    index_grid = (
        jnp.arange(row_count, dtype=jnp.int32)[:, None]
        * jnp.arange(col_count, dtype=jnp.int32)[None, :]
        % length
    )
    phase_grid = index_grid.astype(jnp.float32) * (two_pi / length)
    return (jnp.cos(phase_grid), jnp.sin(phase_grid))


def spectra(segments, length):
    seg_rows = segments.shape[0]
    seg_width = segments.shape[2]
    cosine, sine_part = angle_table(seg_width, length, length)
    product = jnp.dot(
        segments.reshape(seg_rows * 2, seg_width),
        jnp.concatenate([cosine, sine_part], axis=1),
        precision=highest,
        preferred_element_type=jnp.float32,
    )
    product = product.reshape(seg_rows, 2, 2 * length)
    real_part = product[:, 0, :length] + product[:, 1, length:]
    imag_part = product[:, 1, :length] - product[:, 0, length:]
    return jnp.stack([real_part, imag_part], axis=1)


def doppler_mix(near_spec, far_part, mix_cos, mix_sin):
    cross_real = near_spec[:, 0] * far_part[:, 0] + near_spec[:, 1] * far_part[:, 1]
    cross_imag = near_spec[:, 1] * far_part[:, 0] - near_spec[:, 0] * far_part[:, 1]
    mixed_real = jnp.dot(mix_cos, cross_real, precision=highest) + jnp.dot(
        mix_sin, cross_imag, precision=highest
    )
    mixed_imag = jnp.dot(mix_cos, cross_imag, precision=highest) - jnp.dot(
        mix_sin, cross_real, precision=highest
    )
    return jnp.stack([mixed_real, mixed_imag], axis=1)


def lag_transform(spectra_in, lag_coeff, lag_count):
    length = spectra_in.shape[-1]
    lead_shape = spectra_in.shape[:-2]
    product = jnp.dot(
        spectra_in.reshape(-1, length),
        lag_coeff,
        precision=None,
        preferred_element_type=jnp.float32,
    )
    product = product.reshape(lead_shape + (2, 2 * lag_count))
    real_part = product[..., 0, :lag_count] + product[..., 1, lag_count:]
    imag_part = product[..., 1, :lag_count] - product[..., 0, lag_count:]
    return jnp.stack([real_part, imag_part], axis=-2) * (1.0 / length)


def pick_slot_first(surface, dop_start, lag_start):
    slot_count = surface.shape[0]
    dop_index = (
        dop_start[:, :, None, None] + jnp.arange(WD, dtype=jnp.int32)[:, None]
    ) % surface.shape[1]
    lag_index = lag_start[:, :, None, None] + jnp.arange(WL, dtype=jnp.int32)[None, :]
    slot_index = jnp.arange(slot_count, dtype=jnp.int32)[:, None, None, None]
    picked = surface[slot_index, dop_index, :, lag_index]
    return picked.reshape(slot_count, dop_start.shape[1], WD * WL * 2)


def solve_three(normals, damp_term):
    entry_xx = normals[0] + damp_term
    entry_xy = normals[1]
    entry_xz = normals[2]
    entry_yy = normals[3] + damp_term
    entry_yz = normals[4]
    entry_zz = normals[5] + damp_term
    minor_xx = entry_yy * entry_zz - entry_yz * entry_yz
    minor_xy = entry_xz * entry_yz - entry_xy * entry_zz
    minor_xz = entry_xy * entry_yz - entry_xz * entry_yy
    minor_yy = entry_xx * entry_zz - entry_xz * entry_xz
    minor_yz = entry_xy * entry_xz - entry_xx * entry_yz
    minor_zz = entry_xx * entry_yy - entry_xy * entry_xy
    determinant = entry_xx * minor_xx + entry_xy * minor_xy + entry_xz * minor_xz
    step_x = minor_xx * normals[6] + minor_xy * normals[7] + minor_xz * normals[8]
    step_y = minor_xy * normals[6] + minor_yy * normals[7] + minor_yz * normals[8]
    step_z = minor_xz * normals[6] + minor_yz * normals[7] + minor_zz * normals[8]
    return jnp.stack([step_x, step_y, step_z]) / determinant


def normal_rows(sensitivity_matrix, misfit_vector):
    return [
        sensitivity_matrix[0] * sensitivity_matrix[0],
        sensitivity_matrix[0] * sensitivity_matrix[1],
        sensitivity_matrix[0] * sensitivity_matrix[2],
        sensitivity_matrix[1] * sensitivity_matrix[1],
        sensitivity_matrix[1] * sensitivity_matrix[2],
        sensitivity_matrix[2] * sensitivity_matrix[2],
        sensitivity_matrix[0] * misfit_vector,
        sensitivity_matrix[1] * misfit_vector,
        sensitivity_matrix[2] * misfit_vector,
    ]


def ranges(position, onehot_emit, first_pos, second_pos):
    at_peak = jnp.dot(position, onehot_emit, precision=highest)
    diff_first = at_peak - first_pos
    diff_second = at_peak - second_pos
    range_first = jnp.sqrt(jnp.sum(diff_first * diff_first, axis=0) + 1.0)
    range_second = jnp.sqrt(jnp.sum(diff_second * diff_second, axis=0) + 1.0)
    return (range_second - range_first, diff_second / range_second - diff_first / range_first)


def local(
    raw_samples,
    block_scales,
    lag_window_start,
    doppler_window_start,
    peak_owner,
    peak_emitter,
    gn_steps,
    receiver_pos,
    emitter_start,
):
    cycle_size = lax.axis_size("rx")
    block_count = lax.axis_size("tb")
    cycle_index = lax.axis_index("rx")
    block_index = lax.axis_index("tb")
    sample_count = raw_samples.shape[2]
    seg_count = sample_count // SEG
    length = SEG + LAG_COUNT
    reach = LAG_COUNT // SEG
    half_cycle = lag_window_start.shape[0]
    slot_block = half_cycle // block_count
    peaks_slot = lag_window_start.shape[1]
    signal = raw_samples[0].astype(jnp.float32) * jnp.repeat(block_scales[0], BLK)[None, :]
    beyond = from_behind(signal, "tb", -1)
    extended = jnp.concatenate([signal, beyond], axis=1)
    piece_count = seg_count + reach
    piece_spec = spectra(jnp.transpose(extended.reshape(2, piece_count, SEG), (1, 0, 2)), length)
    near_spec = piece_spec[:seg_count]
    freq_ids = jnp.arange(length, dtype=jnp.int32)
    far_real = near_spec[:, 0]
    far_imag = near_spec[:, 1]
    for offset_id in range(1, reach + 1):
        turn = (freq_ids * (offset_id * SEG) % length).astype(jnp.float32) * (two_pi / length)
        turn_cos = jnp.cos(turn)[None, :]
        turn_sin = jnp.sin(turn)[None, :]
        later = piece_spec[offset_id : offset_id + seg_count]
        far_real = far_real + later[:, 0] * turn_cos + later[:, 1] * turn_sin
        far_imag = far_imag + later[:, 1] * turn_cos - later[:, 0] * turn_sin
    far_spec = jnp.stack([far_real, far_imag], axis=1)
    global_seg = block_index * seg_count + jnp.arange(seg_count, dtype=jnp.int32)
    mix_phase = (
        jnp.arange(DOPPLER_BINS, dtype=jnp.int32)[:, None] * global_seg[None, :] % DOPPLER_BINS
    ).astype(jnp.float32) * (two_pi / DOPPLER_BINS)
    mix_cos = jnp.cos(mix_phase)
    mix_sin = jnp.sin(mix_phase)

    def cycle_step(moving, unused_item):
        moving = passed_along(moving, "rx", -1)
        return (moving, doppler_mix(near_spec, moving, mix_cos, mix_sin))

    mixed_all = lax.scan(cycle_step, far_spec, None, length=half_cycle)[1]
    block_spec = mixed_all.astype(jnp.bfloat16)
    cosine, sine_part = angle_table(length, LAG_COUNT, length)
    lag_coeff = jnp.concatenate([cosine, sine_part], axis=1).astype(jnp.bfloat16)
    local_lag = lax.dynamic_slice_in_dim(lag_window_start, block_index * slot_block, slot_block, 0)
    local_doppler = lax.dynamic_slice_in_dim(
        doppler_window_start, block_index * slot_block, slot_block, 0
    )
    block_surf = lag_transform(block_spec, lag_coeff, LAG_COUNT)
    window_part = jnp.transpose(
        pick_slot_first(block_surf, doppler_window_start, lag_window_start), (1, 0, 2)
    )
    surface_part, window_sum = (
        lax.psum_scatter(block_surf, "tb", scatter_dimension=1, tiled=True),
        lax.psum_scatter(window_part, "tb", scatter_dimension=1, tiled=True),
    )
    windows = jnp.transpose(window_sum, (1, 0, 2))
    surface = jnp.transpose(surface_part, (1, 0, 2, 3))
    ambiguity = surface * (1.0 / math.sqrt(SEG * DOPPLER_BINS))
    window_five = windows.reshape(slot_block, peaks_slot, WD, WL, 2)
    window_power = jnp.sum(window_five * window_five, axis=4) * (1.0 / (SEG * DOPPLER_BINS))
    total_power = jnp.mean(window_power, axis=(2, 3)) + 1e-06
    lag_average = (
        jnp.mean(window_power * jnp.arange(WL, dtype=jnp.float32), axis=(2, 3)) / total_power
    )
    doppler_average = (
        jnp.mean(window_power * jnp.arange(WD, dtype=jnp.float32)[:, None], axis=(2, 3))
        / total_power
    )
    measured_delay = (local_lag.astype(jnp.float32) + lag_average) * (delay_extent / LAG_COUNT)
    measured_doppler = (local_doppler.astype(jnp.float32) + doppler_average) * (
        doppler_extent / DOPPLER_BINS
    )
    peak_weight_sum = slot_block * peaks_slot
    capacity = max(2, peak_weight_sum // cycle_size * 2)
    slot_local = block_index * slot_block + jnp.arange(slot_block, dtype=jnp.int32)
    second_ids = (cycle_index + slot_local + 1) % cycle_size
    first_float = jnp.full((peak_weight_sum,), cycle_index.astype(jnp.float32), jnp.float32)
    second_float = (
        jnp.broadcast_to(second_ids[:, None], (slot_block, peaks_slot))
        .reshape(peak_weight_sum)
        .astype(jnp.float32)
    )
    emit_float = peak_emitter.reshape(peak_weight_sum).astype(jnp.float32)
    owner_flat = peak_owner.reshape(peak_weight_sum)
    owner_hot = (owner_flat[:, None] == jnp.arange(cycle_size, dtype=jnp.int32)[None, :]).astype(
        jnp.int32
    )
    earlier = jnp.cumsum(owner_hot, axis=0) - owner_hot
    rank_in = jnp.sum(earlier * owner_hot, axis=1)
    target = owner_flat * capacity + rank_in
    placing = (
        target[:, None] == jnp.arange(cycle_size * capacity, dtype=jnp.int32)[None, :]
    ).astype(jnp.float32)
    payload = jnp.stack(
        [
            measured_delay.reshape(peak_weight_sum),
            measured_doppler.reshape(peak_weight_sum),
            first_float,
            second_float,
            emit_float,
            jnp.ones((peak_weight_sum,), jnp.float32),
        ]
    )
    send_buf = jnp.dot(payload, placing, precision=highest)
    arrived = lax.all_to_all(send_buf, "rx", split_axis=1, concat_axis=1, tiled=True)
    recv_count = receiver_pos.shape[1]
    em_count = emitter_start.shape[1]
    live_mask = arrived[5]
    receiver_ids = jnp.arange(recv_count, dtype=jnp.float32)[:, None]
    onehot_first = (arrived[2][None, :] == receiver_ids).astype(jnp.float32)
    onehot_second = (arrived[3][None, :] == receiver_ids).astype(jnp.float32)
    onehot_emit = (arrived[4][None, :] == jnp.arange(em_count, dtype=jnp.float32)[:, None]).astype(
        jnp.float32
    )
    first_pos = jnp.dot(receiver_pos, onehot_first, precision=highest)
    second_pos = jnp.dot(receiver_pos, onehot_second, precision=highest)
    arrived_tau = arrived[0]
    arrived_nu = arrived[1]
    position = emitter_start
    emitter_speed = jnp.zeros((3, em_count), jnp.float32)
    receiver_clock_bias = jnp.zeros((recv_count,), jnp.float32)
    per_receiver = (1.0 + damping) * peaks_slot * cycle_size
    for gn_step in range(GN_MAX):
        peak_dispersion, sensitivity_matrix = ranges(position, onehot_emit, first_pos, second_pos)
        bias_first = jnp.dot(receiver_clock_bias, onehot_first, precision=highest)
        bias_second = jnp.dot(receiver_clock_bias, onehot_second, precision=highest)
        misfit_vector = live_mask * (arrived_tau - peak_dispersion - bias_second + bias_first)
        sensitivity_matrix = sensitivity_matrix * live_mask
        stacked_rows = jnp.stack(normal_rows(sensitivity_matrix, misfit_vector) + [live_mask])
        pos_normals = lax.psum(jnp.dot(stacked_rows, onehot_emit.T, precision=highest), "tb")
        damp_term = damping * (pos_normals[9] + 1.0)
        still_moving = (gn_step < gn_steps)[None, :]
        position = position + jnp.where(still_moving, solve_three(pos_normals, damp_term), 0.0)
        peak_dispersion, sensitivity_matrix = ranges(position, onehot_emit, first_pos, second_pos)
        sensitivity_matrix = sensitivity_matrix * live_mask
        vel_peak = jnp.dot(emitter_speed, onehot_emit, precision=highest)
        velocity_misfit = live_mask * (arrived_nu - jnp.sum(vel_peak * sensitivity_matrix, axis=0))
        vel_terms = jnp.dot(
            jnp.stack(normal_rows(sensitivity_matrix, velocity_misfit)),
            onehot_emit.T,
            precision=highest,
        )
        clock_misfit = live_mask * (arrived_tau - peak_dispersion - bias_second + bias_first)
        clock_terms = jnp.dot(onehot_second - onehot_first, clock_misfit, precision=highest)
        vel_normals = lax.psum(vel_terms, "tb")
        clock_total = lax.psum(clock_terms, ("rx", "tb"))
        emitter_speed = emitter_speed + jnp.where(
            still_moving, solve_three(vel_normals, damp_term), 0.0
        )
        receiver_clock_bias = receiver_clock_bias + clock_total / per_receiver
    return (ambiguity, position, emitter_speed, receiver_clock_bias)


def solution(mesh):
    placed = (
        P("rx", None, "tb"),
        P("rx", "tb"),
        P("rx", None),
        P("rx", None),
        P(("rx", "tb"), None, None),
        P(("rx", "tb"), None),
        P("rx"),
        P(),
        P(None, "rx"),
    )
    return jax.shard_map(
        local,
        mesh=mesh,
        in_specs=placed,
        out_specs=(P("tb", "rx", None, None), P(None, "rx"), P(None, "rx"), P()),
        check_vma=False,
    )
```

profile of v0, /device:TPU:1, one launch (start us, length us, event | category | flops | bytes accessed | tf_op | source)
XLA Modules:
  0.0 1112.6 jit_solution(10033241439755260535)
XLA Ops:
  8.6 5.1 collective-permute-start.1
  13.8 5.3 fusion.61
  19.3 22.7 %sine_convert_fusion = (bf16[1280,1024]{1,0:T(8,128)(2,1)}, bf16[1280,1024]{1,0:T(8,128)(2,1)}) fusion(), kind=kLoop, calls=%fused_computation.55 | loop fusion | flops 14417920 | bytes 5242880 | tf_op jit(solution)/shard_map/convert.2
  47.0 1.3 fusion.53
  48.6 134.8 %while.14 = (s32[]{:T(128)}, f32[4,2,1280]{2,1,0:T(2,128)S(1)}, bf16[16,32,2,1280]{3,1,2,0:T(8,128)(2,1)}, f32[4,2,1280]{2,1,0:T(2,128)S(1)}, s32[4]{0:T(128)S(1)}, /*index=5*/s32[]{:T(128)}) while((s32[]{:T(128)}, f32[4,2,1280]{2,1,0:T(2,128)S(1)}, bf16[16,32,2,1280]{3,1,2,0:T(8,128)(2,1)}, ...), condition=%wide.region_1.2_spmd.clone.clone, body=%wide.region_0.1_spmd.clone.clone.sunk | while | flops 8393730 | bytes 1597625 | solution.py:193
  48.6 6.1 collective-permute-start
  54.7 1.3 collective-permute-done
  58.1 5.3 collective-permute-start
  66.7 5.1 collective-permute-start
  71.8 1.1 collective-permute-done
  75.0 5.1 collective-permute-start
  83.3 5.1 collective-permute-start
  91.7 5.1 collective-permute-start
  100.0 5.1 collective-permute-start
  108.3 5.1 collective-permute-start
  116.6 5.1 collective-permute-start
  125.0 5.1 collective-permute-start
  133.3 5.1 collective-permute-start
  141.6 5.1 collective-permute-start
  149.9 5.1 collective-permute-start
  158.3 5.1 collective-permute-start
  166.6 5.1 collective-permute-start
  174.9 5.1 collective-permute-start
  183.4 8.1 fusion.47
  191.5 1.4 slice_add_fusion
  193.4 2.0 copy-done.1
  195.4 5.2 copy.33
  200.6 270.8 %gather_fusion = f32[16384,2]{0,1:T(2,128)S(1)} fusion(f32[16,32,2,1024]{3,2,1,0:T(2,128)} %copy.33, s32[16384]{0:T(1024)S(1)} %reshape.522), kind=kCustom, calls=%fused_computation | custom fusion | bytes 458752 | tf_op jit(solution)/shard_map/gather | solution.py:96
  471.4 5.0 copy.34
  476.4 7.4 reshape.519
  484.1 48.3 %reduce-scatter.5.cloned.1.call-done = f32[16,2,128]{2,0,1:T(8,128)} async-done(((f32[16,16,128]{2,0,1:T(8,128)}), f32[16,2,128]{2,0,1:T(8,128)}) %reduce-scatter.5.cloned.1.call-update) | async-done | bytes 16400 | tf_op jit(solution)/shard_map/reduce_scatter | solution.py:207
  535.4 9.6 all-to-all-start
  545.2 6.5 copy.32
  551.7 1.9 all-to-all-done
  555.7 16.3 %psum.126 = f32[10,4]{0,1:T(4,128)S(1)} all-reduce(f32[10,4]{0,1:T(4,128)S(1)} %fusion.167), channel_id=1, replica_groups=mesh['rx'=32,'tb'=8] {'tb'}, use_global_device_ids=true, to_apply=%region_12.13 | all-reduce | flops 40 | bytes 320 | tf_op jit(solution)/shard_map/psum | solution.py:283
  572.9 73.5 %psum.127 = f32[32]{0:T(128)S(1)} all-reduce(f32[32]{0:T(128)S(1)} %convolution_bitcast_fusion.18), channel_id=1, replica_groups=mesh['rx'=32,'tb'=8] {'rx','tb'}, use_global_device_ids=true, to_apply=%region_15.16 | all-reduce | flops 32 | bytes 256 | tf_op jit(solution)/shard_map/psum | solution.py:299
  647.3 12.4 %all-reduce.4 = (f32[10,4]{0,1:T(4,128)S(1)}, f32[9,4]{0,1:T(4,128)S(1)}) all-reduce(f32[10,4]{0,1:T(4,128)S(1)} %fusion.165, f32[9,4]{0,1:T(4,128)S(1)} %fusion.156), channel_id=1, replica_groups=mesh['rx'=32,'tb'=8] {'tb'}, use_global_device_ids=true, to_apply=%region_16.17 | all-reduce | flops 76 | bytes 608 | tf_op jit(solution)/shard_map/psum | solution.py:283
  660.5 73.3 %psum.129 = f32[32]{0:T(128)S(1)} all-reduce(f32[32]{0:T(128)S(1)} %convolution_bitcast_fusion.15), channel_id=1, replica_groups=mesh['rx'=32,'tb'=8] {'rx','tb'}, use_global_device_ids=true, to_apply=%region_19.20 | all-reduce | flops 32 | bytes 256 | tf_op jit(solution)/shard_map/psum | solution.py:299
  735.2 12.4 %all-reduce.3 = (f32[10,4]{0,1:T(4,128)S(1)}, f32[9,4]{0,1:T(4,128)S(1)}) all-reduce(f32[10,4]{0,1:T(4,128)S(1)} %fusion.163, f32[9,4]{0,1:T(4,128)S(1)} %fusion.155), channel_id=1, replica_groups=mesh['rx'=32,'tb'=8] {'tb'}, use_global_device_ids=true, to_apply=%region_20.21 | all-reduce | flops 76 | bytes 608 | tf_op jit(solution)/shard_map/psum | solution.py:283
  748.5 73.5 %psum.131 = f32[32]{0:T(128)S(1)} all-reduce(f32[32]{0:T(128)S(1)} %convolution_bitcast_fusion.12), channel_id=1, replica_groups=mesh['rx'=32,'tb'=8] {'rx','tb'}, use_global_device_ids=true, to_apply=%region_23.24 | all-reduce | flops 32 | bytes 256 | tf_op jit(solution)/shard_map/psum | solution.py:299
  823.3 12.4 %all-reduce.2 = (f32[10,4]{0,1:T(4,128)S(1)}, f32[9,4]{0,1:T(4,128)S(1)}) all-reduce(f32[10,4]{0,1:T(4,128)S(1)} %fusion.161, f32[9,4]{0,1:T(4,128)S(1)} %fusion.154), channel_id=1, replica_groups=mesh['rx'=32,'tb'=8] {'tb'}, use_global_device_ids=true, to_apply=%region_24.25 | all-reduce | flops 76 | bytes 608 | tf_op jit(solution)/shard_map/psum | solution.py:283
  836.5 74.2 %psum.133 = f32[32]{0:T(128)S(1)} all-reduce(f32[32]{0:T(128)S(1)} %convolution_bitcast_fusion.9), channel_id=1, replica_groups=mesh['rx'=32,'tb'=8] {'rx','tb'}, use_global_device_ids=true, to_apply=%region_27.28 | all-reduce | flops 32 | bytes 256 | tf_op jit(solution)/shard_map/psum | solution.py:299
  912.0 12.4 %all-reduce.1 = (f32[10,4]{0,1:T(4,128)S(1)}, f32[9,4]{0,1:T(4,128)S(1)}) all-reduce(f32[10,4]{0,1:T(4,128)S(1)} %fusion.159, f32[9,4]{0,1:T(4,128)S(1)} %fusion.153), channel_id=1, replica_groups=mesh['rx'=32,'tb'=8] {'tb'}, use_global_device_ids=true, to_apply=%region_28.29 | all-reduce | flops 76 | bytes 608 | tf_op jit(solution)/shard_map/psum | solution.py:283
  925.3 73.4 %psum.135 = f32[32]{0:T(128)S(1)} all-reduce(f32[32]{0:T(128)S(1)} %convolution_bitcast_fusion.6), channel_id=1, replica_groups=mesh['rx'=32,'tb'=8] {'rx','tb'}, use_global_device_ids=true, to_apply=%region_31.32 | all-reduce | flops 32 | bytes 256 | tf_op jit(solution)/shard_map/psum | solution.py:299
  1000.1 12.4 %all-reduce = (f32[10,4]{0,1:T(4,128)S(1)}, f32[9,4]{0,1:T(4,128)S(1)}) all-reduce(f32[10,4]{0,1:T(4,128)S(1)} %fusion.157, f32[9,4]{0,1:T(4,128)S(1)} %fusion.152), channel_id=1, replica_groups=mesh['rx'=32,'tb'=8] {'tb'}, use_global_device_ids=true, to_apply=%region_32.33 | all-reduce | flops 76 | bytes 608 | tf_op jit(solution)/shard_map/psum | solution.py:283
  1013.3 74.1 %psum.143 = f32[32]{0:T(128)S(1)} all-reduce(f32[32]{0:T(128)S(1)} %convolution_bitcast_fusion.3), channel_id=1, replica_groups=mesh['rx'=32,'tb'=8] {'rx','tb'}, use_global_device_ids=true, to_apply=%region_47.48 | all-reduce | flops 32 | bytes 256 | tf_op jit(solution)/shard_map/psum | solution.py:299
  1089.0 12.4 %psum.142 = f32[9,4]{0,1:T(4,128)S(1)} all-reduce(f32[9,4]{0,1:T(4,128)S(1)} %fusion.150), channel_id=1, replica_groups=mesh['rx'=32,'tb'=8] {'tb'}, use_global_device_ids=true, to_apply=%region_46.47 | all-reduce | flops 36 | bytes 288 | tf_op jit(solution)/shard_map/psum | solution.py:298
  1104.2 1.2 copy.38
  (363 shorter events, 77.1 us)
Async XLA Ops:
  7.2 547.2 %copy-start = (f32[3,32]{1,0:T(4,128)S(1)}, f32[3,32]{1,0:T(4,128)}, u32[]{:S(2)}) copy-start(f32[3,32]{1,0:T(4,128)} %param.18) | copy-start | bytes 1156
  7.2 525.3 %reduce-scatter.5.cloned.1.call-start = ((), (), s32[]{:S(2)}) async-start(), calls=%async_computation.4 | async-start | bytes 147456 | tf_op jit(solution)/shard_map/reduce_scatter | solution.py:207
  8.6 37.6 %collective-permute-start.1 = (f32[2,1024]{1,0:T(2,128)S(1)}, f32[2,1024]{1,0:T(2,128)}, u32[]{:S(2)}, u32[]{:S(2)}) collective-permute-start(f32[2,1024]{1,0:T(2,128)S(1)} %convert_multiply_fusion), channel_id=1, source_target_pairs={{1,0},{2,1},{3,2},{4,3},{5,4},{6,5},{7,6},{9,8},{10,9},{11,10},{12... | collective-permute-start | bytes 24584 | tf_op jit(solution)/shard_map/ppermute | solution.py:27
  19.3 23.7 %copy-start.4 = (s32[16,16]{1,0:T(8,128)S(1)}, s32[16,16]{1,0:T(8,128)}, u32[]{:S(2)}) copy-start(s32[16,16]{1,0:T(8,128)} %param.14) | copy-start | bytes 3076
  19.3 23.9 %copy-start.3 = (s32[16,16]{1,0:T(8,128)S(1)}, s32[16,16]{1,0:T(8,128)}, u32[]{:S(2)}) copy-start(s32[16,16]{1,0:T(8,128)} %param.13) | copy-start | bytes 3076
  19.3 24.5 %copy-start.8 = (s32[2,16,1]{1,2,0:T(1,128)S(1)}, s32[2,16,1]{1,2,0:T(1,128)}, u32[]{:S(2)}) copy-start(s32[2,16,1]{1,2,0:T(1,128)} %param.15) | copy-start | bytes 388
  44.6 1.3 copy-start.6
  48.3 135.1 %copy-start.2 = (bf16[1280,1024]{1,0:T(8,128)(2,1)S(1)}, bf16[1280,1024]{1,0:T(8,128)(2,1)}, u32[]{:S(2)}) copy-start(bf16[1280,1024]{1,0:T(8,128)(2,1)} %get-tuple-element.353) | copy-start | bytes 7864324
  48.6 7.4 collective-permute-start
  58.1 6.4 collective-permute-start
  66.7 6.2 collective-permute-start
  75.0 6.2 collective-permute-start
  83.3 6.2 collective-permute-start
  91.7 6.2 collective-permute-start
  100.0 6.2 collective-permute-start
  108.3 6.2 collective-permute-start
  116.6 6.2 collective-permute-start
  125.0 6.2 collective-permute-start
  133.3 6.2 collective-permute-start
  141.6 6.2 collective-permute-start
  149.9 6.2 collective-permute-start
  158.3 6.2 collective-permute-start
  166.6 6.2 collective-permute-start
  174.9 6.2 collective-permute-start
  193.4 2.0 copy-start.1
  476.4 7.7 copy-start.9
  476.4 7.8 copy-start.7
  476.4 7.8 copy-start.13
  476.4 57.1 %copy-start.10 = (f32[4]{0:T(128)S(1)}, f32[4]{0:T(128)}, u32[]{:S(2)}) copy-start(f32[4]{0:T(128)} %iota_multiply_fusion) | copy-start | bytes 52
  476.4 57.1 %copy-start.11 = (f32[16]{0:T(128)S(1)}, f32[16]{0:T(128)}, u32[]{:S(2)}) copy-start(f32[16]{0:T(128)} %iota_multiply_fusion.1) | copy-start | bytes 196
  476.4 68.7 %copy-start.12 = (s32[4]{0:T(128)S(1)}, s32[4]{0:T(128)}, u32[]{:S(2)}) copy-start(s32[4]{0:T(128)} %param.17) | copy-start | bytes 52
  476.4 68.7 %copy-start.5 = (f32[3,4]{1,0:T(4,128)S(1)}, f32[3,4]{1,0:T(4,128)}, u32[]{:S(2)}) copy-start(f32[3,4]{1,0:T(4,128)} %param.19) | copy-start | bytes 148
  535.4 18.2 %all-to-all-start = ((f32[6,32,2]{0,2,1:T(2,128)}), f32[6,32,2]{0,2,1:T(2,128)S(1)}, u32[]{:S(2)}, u32[]{:S(2)}) async-start(f32[6,32,2]{0,2,1:T(2,128)} %bitcast.10), calls=%async_computation.2 | async-start | bytes 65536 | tf_op jit(solution)/shard_map/all_to_all | solution.py:258
  545.0 558.1 %reduce-scatter.3.cloned.1.call-start = ((), (), s32[]{:S(2)}) async-start(), calls=%async_computation.3 | async-start | bytes 4718592 | tf_op jit(solution)/shard_map/reduce_scatter | solution.py:206
Sparse Core Ops, SparseCore 0:
  484.0 48.4 reduce-scatter.4
  551.8 39.8 reduce-scatter.2
where the time goes:
time: 1130 us; the launch traced here: 1110 us
  blocking collectives  533 us (47%)
  local copies, waits for them, and re-layouts  304 us (27%)
  starting transfers between devices  97.1 us (9%)
  waiting for transfers between devices  68.1 us (6%)
  other arithmetic  54.9 us (5%)
  matrix products  39.9 us (4%)
  between operations  15.2 us (1%)
    psum x6, blocking collectives, local(): clock_total = lax.psum(clock_terms, ('rx', 'tb'))  442 us
    gather x2, local copies, waits for them, and re-layouts, pick_slot_first(): picked = surface[slot_index, dop_index, :, lag_index]  276 us
    ppermute x16, starting transfers between devices, passed_along(): return lax.ppermute(block, axis, route)  82.4 us
    psum x6, blocking collectives, local(): lax.psum(jnp.dot(stacked_rows, onehot_emit.T, precision=highest), 'tb')  78.5 us
    reduce_scatter x1, waiting for transfers between devices, local(): lax.psum_scatter(window_part, 'tb', scatter_dimension=1, tiled=True)  48.3 us
    another operation x1, other arithmetic  22.7 us
  transfers between devices with their start and end apart: 20, of which 18 were waited for; matrix products, arithmetic and copies ran while one was open for 5% of the time, Pallas kernels for 0%

commit v1 on v0

v1 whole, which is shorter than its diff:
```python
import functools
import math

import jax
import jax.numpy as jnp
import numpy as np
from jax import lax
from jax.experimental import pallas as pl
from jax.experimental.pallas import tpu as pltpu
from jax.sharding import PartitionSpec as P

SEG = 256
DOPPLER_BINS = 32
LAG_COUNT = 1024
WL = 16
WD = 4
GN_MAX = 6
RX = 32
TB = 8
FFT = 512
SAMPLES = SEG * DOPPLER_BINS

MESH = pl.DeviceIdType.MESH
f32 = jnp.float32
bf16 = jnp.bfloat16
highest = lax.Precision.HIGHEST


def split_pair(table):
    high = table.astype(bf16)
    low = (table - high.astype(np.float64)).astype(bf16)
    return high, low


def tables():
    turn = 2.0 * np.pi / FFT
    t_f = np.arange(SEG)[:, None] * np.arange(FFT)[None, :] % FFT * turn
    forward = np.concatenate([np.cos(t_f), np.sin(t_f)], axis=1)
    backward = np.concatenate([np.cos(t_f.T), np.sin(t_f.T)], axis=1)
    d_m = (
        np.arange(DOPPLER_BINS)[:, None] * np.arange(DOPPLER_BINS)[None, :] % DOPPLER_BINS
    ) * (2.0 * np.pi / DOPPLER_BINS)
    mix = np.block([[np.cos(d_m), np.sin(d_m)], [-np.sin(d_m), np.cos(d_m)]])
    mix = mix / (FFT * math.sqrt(SAMPLES))
    return split_pair(forward) + split_pair(backward) + (mix.astype(np.float32),)


def gather_kernel(raw, scl, raw_all, scl_all, send_a, recv_a, send_b, recv_b, own_sem):
    r = lax.axis_index("rx")
    b = lax.axis_index("tb")
    barrier = pltpu.get_barrier_semaphore()
    targets = []
    for d in range(1, TB):
        peer = lax.rem(b + d, TB)
        pl.semaphore_signal(barrier, inc=1, device_id={"rx": r, "tb": peer}, device_id_type=MESH)
        targets.append((r, peer, 0))
    for i in (1, 2):
        source = lax.rem(r + 2 * b + i, RX)
        for t in range(TB):
            pl.semaphore_signal(
                barrier, inc=1, device_id={"rx": source, "tb": t}, device_id_type=MESH
            )
            targets.append((lax.rem(r + RX - 2 * t - i, RX), t, i))
    pl.semaphore_wait(barrier, len(targets))
    own = [
        pltpu.make_async_copy(raw, raw_all.at[b], own_sem.at[0]),
        pltpu.make_async_copy(scl, scl_all.at[b], own_sem.at[1]),
    ]
    sends = []
    for n, (to_r, to_b, i) in enumerate(targets):
        slot = i * TB + b
        for src, dst, ss, rs in (
            (raw, raw_all, send_a, recv_a),
            (scl, scl_all, send_b, recv_b),
        ):
            copy = pltpu.make_async_remote_copy(
                src_ref=src,
                dst_ref=dst.at[slot],
                send_sem=ss.at[n],
                recv_sem=rs.at[slot],
                device_id={"rx": to_r, "tb": to_b},
                device_id_type=MESH,
            )
            copy.start()
            sends.append(copy)
    for copy in own:
        copy.start()
    for copy in own:
        copy.wait()
    arrivals = [lax.rem(b + d, TB) for d in range(1, TB)]
    arrivals += [i * TB + t for i in (1, 2) for t in range(TB)]
    for slot in arrivals:
        for src, dst, rs in ((raw, raw_all, recv_a), (scl, scl_all, recv_b)):
            pltpu.make_async_remote_copy(
                src_ref=src,
                dst_ref=dst.at[slot],
                send_sem=send_a.at[0],
                recv_sem=rs.at[slot],
                device_id={"rx": r, "tb": lax.rem(b + 1, TB)},
                device_id_type=MESH,
            ).wait_recv()
    for copy in sends:
        copy.wait_send()


def gather_samples(raw, scl):
    any_spec = pl.BlockSpec(memory_space=pl.ANY)
    n = 3 * TB - 1
    return pl.pallas_call(
        gather_kernel,
        out_shape=(
            jax.ShapeDtypeStruct((3 * TB,) + raw.shape, raw.dtype),
            jax.ShapeDtypeStruct((3 * TB,) + scl.shape, scl.dtype),
        ),
        in_specs=[any_spec, any_spec],
        out_specs=(any_spec, any_spec),
        scratch_shapes=[
            pltpu.SemaphoreType.DMA((n,)),
            pltpu.SemaphoreType.DMA((3 * TB,)),
            pltpu.SemaphoreType.DMA((n,)),
            pltpu.SemaphoreType.DMA((3 * TB,)),
            pltpu.SemaphoreType.DMA((2,)),
        ],
        compiler_params=pltpu.CompilerParams(collective_id=0, has_side_effects=True),
        name="gather_samples",
    )(raw, scl)


def iota(shape, dim):
    return lax.broadcasted_iota(jnp.int32, shape, dim)


def to_column(row, count):
    eye = iota((count, count), 0) == iota((count, count), 1)
    return jnp.sum(jnp.where(eye, row, 0.0), axis=1, keepdims=True)


def surface_kernel(
    raw_ref, scl_ref, fhi_ref, flo_ref, bhi_ref, blo_ref, mix_ref,
    lag_ref, dop_ref, own_ref, em_ref, start_ref, steps_ref,
    surf_ref, pay_ref, re_ref, im_ref, rr_ref,
):
    raw = raw_ref[...].astype(f32).reshape(3 * TB * 8, SEG).astype(bf16)
    spec = jnp.dot(raw, fhi_ref[...], preferred_element_type=f32)
    spec = spec + jnp.dot(raw, flo_ref[...], preferred_element_type=f32)
    cos_part = spec[:, :FFT].reshape(3 * TB, 8, FFT)
    sin_part = spec[:, FFT:].reshape(3 * TB, 8, FFT)
    sub = iota((1, 8, 1), 1)
    sign = jnp.where(sub < 4, 1.0, -1.0).astype(f32)
    sub_l = iota((1, 8, 128), 1)
    lane_l = iota((1, 8, 128), 2)
    pick = lane_l == lax.rem(sub_l, 4)
    scale = jnp.sum(jnp.where(pick, scl_ref[...], 0.0), axis=2, keepdims=True)
    pieces = (cos_part + sign * pltpu.roll(sin_part, 4, 1)) * scale
    for i in range(3):
        re_ref[i, 32:40, :] = jnp.zeros((8, FFT), f32)
        im_ref[i, 32:40, :] = jnp.zeros((8, FFT), f32)
        for t in range(TB):
            re_ref[i, 4 * t : 4 * t + 4, :] = pieces[i * TB + t, 0:4, :]
            im_ref[i, 4 * t : 4 * t + 4, :] = pieces[i * TB + t, 4:8, :]
    near_re = re_ref[0, 0:32, :]
    near_im = im_ref[0, 0:32, :]
    alt = jnp.where(lax.rem(iota((1, FFT), 1), 2) == 0, 1.0, -1.0).astype(f32)
    for c in range(2):
        for j in range(4):
            far_re = re_ref[c + 1, j : j + 32, :] + alt * re_ref[c + 1, j + 1 : j + 33, :]
            far_im = im_ref[c + 1, j : j + 32, :] + alt * im_ref[c + 1, j + 1 : j + 33, :]
            row = (c * 4 + j) * 32
            rr_ref[row : row + 32, :] = near_re * far_re + near_im * far_im
            rr_ref[256 + row : 288 + row, :] = near_im * far_re - near_re * far_im
    cross = rr_ref[...]
    high = cross.astype(bf16)
    low = (cross - high.astype(f32)).astype(bf16)
    lagged = jnp.dot(high, bhi_ref[...], preferred_element_type=f32)
    lagged = lagged + jnp.dot(low, bhi_ref[...], preferred_element_type=f32)
    lagged = lagged + jnp.dot(high, blo_ref[...], preferred_element_type=f32)
    lag_re = lagged[0:256, 0:256] + lagged[256:512, 256:512]
    lag_im = lagged[256:512, 0:256] - lagged[0:256, 256:512]

    b = lax.axis_index("tb")
    r = lax.axis_index("rx")
    lag_rows = lag_ref[pl.ds(2 * b, 2), :].astype(f32)
    dop_rows = dop_ref[pl.ds(2 * b, 2), :].astype(f32)
    tau_cols, nu_cols, own_cols, em_cols = [], [], [], []
    for c in range(2):
        top = jnp.concatenate(
            [lag_re[(c * 4 + j) * 32 : (c * 4 + j + 1) * 32] for j in range(4)], axis=1
        )
        low_half = jnp.concatenate(
            [lag_im[(c * 4 + j) * 32 : (c * 4 + j + 1) * 32] for j in range(4)], axis=1
        )
        stacked = jnp.concatenate([top, low_half], axis=0)
        surf = jnp.dot(mix_ref[...], stacked, precision=highest, preferred_element_type=f32)
        for comp in range(2):
            for lt in range(8):
                surf_ref[pl.ds(c * 16 + lt * 2 + comp, 32, stride=32), :] = surf[
                    comp * 32 : comp * 32 + 32, lt * 128 : lt * 128 + 128
                ]
        power = surf[0:32] * surf[0:32] + surf[32:64] * surf[32:64]
        lag0 = to_column(lag_rows[c : c + 1, :], 16)
        dop0 = to_column(dop_rows[c : c + 1, :], 16)
        d_id = iota((16, DOPPLER_BINS), 1).astype(f32)
        offset = d_id - dop0
        offset = jnp.where(offset < 0.0, offset + DOPPLER_BINS, offset)
        inside = jnp.where(offset < WD, 1.0, 0.0).astype(f32)
        weights = jnp.concatenate([inside, inside * offset], axis=0)
        rows = jnp.dot(weights, power, precision=highest, preferred_element_type=f32)
        step = iota((16, LAG_COUNT), 1).astype(f32) - lag0
        within = (step >= 0.0) & (step < WL)
        plain = jnp.where(within, rows[0:16], 0.0)
        norm = 1.0 / (WL * WD)
        total = jnp.sum(plain, axis=1, keepdims=True) * norm + 1e-06
        lag_mean = jnp.sum(plain * step, axis=1, keepdims=True) * norm / total
        dop_mean = jnp.sum(jnp.where(within, rows[16:32], 0.0), axis=1, keepdims=True) * norm / total
        tau_cols.append((lag0 + lag_mean) * (16.0 / LAG_COUNT))
        nu_cols.append((dop0 + dop_mean) * (4.0 / DOPPLER_BINS))
        own_cols.append(to_column(own_ref[c : c + 1, :].astype(f32), 16))
        em_cols.append(to_column(em_ref[c : c + 1, :].astype(f32), 16) + (1.0 + 4.0 * c))
    tau = jnp.concatenate(tau_cols, axis=0)
    nu = jnp.concatenate(nu_cols, axis=0)
    owner = jnp.concatenate(own_cols, axis=0)
    code = jnp.concatenate(em_cols, axis=0)
    p_row = iota((32, 32), 0)
    p_col = iota((32, 32), 1)
    owner_row = jnp.sum(jnp.where(p_row == p_col, owner, 0.0), axis=0, keepdims=True)
    same = (owner_row == owner) & (p_col < p_row)
    rank = jnp.sum(jnp.where(same, 1.0, 0.0), axis=1, keepdims=True)
    lane = iota((32, 128), 1)
    slot = lax.rem(lane, 64).astype(f32)
    placed = (rank * 32.0 + owner) == slot
    first = lane < 64
    pay_ref[0] = jnp.sum(
        jnp.where(placed, jnp.where(first, tau, nu), 0.0), axis=0, keepdims=True
    )
    codes = jnp.sum(jnp.where(placed & first, code, 0.0), axis=0, keepdims=True)
    lane1 = iota((1, 128), 1)
    for k in range(3):
        for e in range(4):
            codes = jnp.where(lane1 == 64 + 4 * k + e, start_ref[k : k + 1, e : e + 1], codes)
    for e in range(4):
        codes = jnp.where(lane1 == 76 + e, steps_ref[0:1, e : e + 1].astype(f32), codes)
    pay_ref[1] = codes


def surfaces(raw_all, scl_all, lag, dop, own, em, start, steps, consts):
    vmem = pl.BlockSpec(memory_space=pltpu.VMEM)
    return pl.pallas_call(
        surface_kernel,
        out_shape=(
            jax.ShapeDtypeStruct((1024, 128), f32),
            jax.ShapeDtypeStruct((2, 1, 128), f32),
        ),
        in_specs=[vmem] * 13,
        out_specs=(vmem, vmem),
        scratch_shapes=[
            pltpu.VMEM((3, 40, FFT), f32),
            pltpu.VMEM((3, 40, FFT), f32),
            pltpu.VMEM((512, FFT), f32),
        ],
        name="surfaces",
    )(raw_all, scl_all, *consts, lag, dop, own, em, start, steps)


def exchange_kernel(surf, pay, amb, table, send_p, recv_p, send_s, recv_s, send_t, recv_t, own_sem):
    r = lax.axis_index("rx")
    b = lax.axis_index("tb")
    barrier = pltpu.get_barrier_semaphore()
    for d in range(1, RX):
        pl.semaphore_signal(
            barrier,
            inc=1,
            device_id={"rx": lax.rem(r + d, RX), "tb": b},
            device_id_type=MESH,
        )
    for d in range(1, TB):
        pl.semaphore_signal(
            barrier,
            inc=1,
            device_id={"rx": r, "tb": lax.rem(b + d, TB)},
            device_id_type=MESH,
        )
    pl.semaphore_wait(barrier, RX + TB - 2)
    own = [
        pltpu.make_async_copy(pay, table.at[b, :, r], own_sem.at[0]),
        pltpu.make_async_copy(surf.at[b], amb.at[:, b], own_sem.at[1]),
    ]
    own[0].start()
    first, second, third = [], [], []
    for d in range(1, RX):
        copy = pltpu.make_async_remote_copy(
            src_ref=pay,
            dst_ref=table.at[b, :, r],
            send_sem=send_p.at[d - 1],
            recv_sem=recv_p.at[d - 1],
            device_id={"rx": lax.rem(r + d, RX), "tb": b},
            device_id_type=MESH,
        )
        copy.start()
        first.append(copy)
    for d in range(1, TB):
        peer = lax.rem(b + d, TB)
        copy = pltpu.make_async_remote_copy(
            src_ref=surf.at[peer],
            dst_ref=amb.at[:, b],
            send_sem=send_s.at[d - 1],
            recv_sem=recv_s.at[d - 1],
            device_id={"rx": r, "tb": peer},
            device_id_type=MESH,
        )
        copy.start()
        second.append(copy)
    own[1].start()
    own[0].wait()
    for d in range(1, RX):
        source = lax.rem(r + RX - d, RX)
        pltpu.make_async_remote_copy(
            src_ref=pay,
            dst_ref=table.at[b, :, source],
            send_sem=send_p.at[d - 1],
            recv_sem=recv_p.at[d - 1],
            device_id={"rx": source, "tb": b},
            device_id_type=MESH,
        ).wait_recv()
    for d in range(1, TB):
        copy = pltpu.make_async_remote_copy(
            src_ref=table.at[b],
            dst_ref=table.at[b],
            send_sem=send_t.at[d - 1],
            recv_sem=recv_t.at[d - 1],
            device_id={"rx": r, "tb": lax.rem(b + d, TB)},
            device_id_type=MESH,
        )
        copy.start()
        third.append(copy)
    for d in range(1, TB):
        source = lax.rem(b + TB - d, TB)
        pltpu.make_async_remote_copy(
            src_ref=surf.at[source],
            dst_ref=amb.at[:, source],
            send_sem=send_s.at[d - 1],
            recv_sem=recv_s.at[d - 1],
            device_id={"rx": r, "tb": source},
            device_id_type=MESH,
        ).wait_recv()
        pltpu.make_async_remote_copy(
            src_ref=table.at[source],
            dst_ref=table.at[source],
            send_sem=send_t.at[d - 1],
            recv_sem=recv_t.at[d - 1],
            device_id={"rx": r, "tb": source},
            device_id_type=MESH,
        ).wait_recv()
    for copy in first + second + third:
        copy.wait_send()
    own[1].wait()


def exchange(surf, pay):
    any_spec = pl.BlockSpec(memory_space=pl.ANY)
    vmem = pl.BlockSpec(memory_space=pltpu.VMEM)
    dma = pltpu.SemaphoreType.DMA
    return pl.pallas_call(
        exchange_kernel,
        out_shape=(
            jax.ShapeDtypeStruct((4, TB, 32, 128), f32),
            jax.ShapeDtypeStruct((TB, 2, RX, 1, 128), f32),
        ),
        in_specs=[vmem, vmem],
        out_specs=(any_spec, any_spec),
        scratch_shapes=[
            dma((RX - 1,)), dma((RX - 1,)), dma((TB - 1,)), dma((TB - 1,)),
            dma((TB - 1,)), dma((TB - 1,)), dma((2,)),
        ],
        compiler_params=pltpu.CompilerParams(collective_id=1, has_side_effects=True),
        name="exchange",
    )(surf, pay)


def solve_three(normals, rhs, damp_term):
    entry_xx = normals[0] + damp_term
    entry_xy = normals[1]
    entry_xz = normals[2]
    entry_yy = normals[3] + damp_term
    entry_yz = normals[4]
    entry_zz = normals[5] + damp_term
    minor_xx = entry_yy * entry_zz - entry_yz * entry_yz
    minor_xy = entry_xz * entry_yz - entry_xy * entry_zz
    minor_xz = entry_xy * entry_yz - entry_xz * entry_yy
    minor_yy = entry_xx * entry_zz - entry_xz * entry_xz
    minor_yz = entry_xy * entry_xz - entry_xx * entry_yz
    minor_zz = entry_xx * entry_yy - entry_xy * entry_xy
    inverse = 1.0 / (entry_xx * minor_xx + entry_xy * minor_xy + entry_xz * minor_xz)
    step_x = minor_xx * rhs[0] + minor_xy * rhs[1] + minor_xz * rhs[2]
    step_y = minor_xy * rhs[0] + minor_yy * rhs[1] + minor_yz * rhs[2]
    step_z = minor_xz * rhs[0] + minor_yz * rhs[1] + minor_zz * rhs[2]
    return [step_x * inverse, step_y * inverse, step_z * inverse]


def per_receiver(x, shift):
    return pltpu.roll(x, (RX - shift) % RX, 0)


def solve_kernel(
    table_ref, rpos_ref, pos_ref, vel_ref, bias_ref,
    tau_ref, nu_ref, mask_ref, late_ref, fst_ref, snd_ref, spread_ref, jac_ref,
):
    lane = iota((RX, 128), 1)
    low = lane < 64
    own_lane = iota((RX, 128), 0) == lax.rem(lane, RX)
    halves = []
    for k in range(4):
        a0, a1 = table_ref[k, 0], table_ref[k + 4, 0]
        tau_ref[k] = jnp.where(low, a0, pltpu.roll(a1, 64, 1))
        nu_ref[k] = jnp.where(low, pltpu.roll(a0, 64, 1), a1)
        code = jnp.where(low, table_ref[k, 1], pltpu.roll(table_ref[k + 4, 1], 64, 1))
        late = code > 4.5
        late_ref[k] = jnp.where(late, 1.0, 0.0)
        emitter = jnp.where(late, code - 4.0, code)
        for e in range(4):
            mask_ref[e, k] = jnp.where(emitter == e + 1.0, 1.0, 0.0)

    info = table_ref[0, 1]

    def owner_row(col):
        value = jnp.sum(jnp.where(lane == col, info, 0.0), axis=1, keepdims=True)
        return jnp.sum(jnp.where(own_lane, value, 0.0), axis=0, keepdims=True)

    def owner_rows(base):
        return jnp.concatenate([owner_row(base + e) for e in range(4)], axis=0)

    position = [owner_rows(64 + 4 * k) for k in range(3)]
    steps = owner_rows(76)

    def second_of(x, k):
        late = late_ref[k] > 0.5
        near_half = jnp.where(late, per_receiver(x, 2 * k + 2), per_receiver(x, 2 * k + 1))
        far_half = jnp.where(late, per_receiver(x, 2 * k + 10), per_receiver(x, 2 * k + 9))
        return jnp.where(low, near_half, far_half)

    eye = iota((RX, RX), 0) == iota((RX, RX), 1)
    for comp in range(3):
        column = jnp.sum(
            jnp.where(eye, rpos_ref[comp : comp + 1, :], 0.0), axis=1, keepdims=True
        )
        column = jnp.broadcast_to(column, (RX, 128))
        fst_ref[comp] = column
        for k in range(4):
            snd_ref[comp, k] = second_of(column, k)

    def sum_rows(parts):
        rows = jnp.concatenate([jnp.sum(p, axis=0, keepdims=True) for p in parts], axis=0)
        rows = rows + pltpu.roll(rows, 32, 1)
        return rows + pltpu.roll(rows, 64, 1)

    def add_to(acc, key, k, quantity):
        for e in range(4):
            term = mask_ref[e, k] * quantity
            term = term[0:8] + term[8:16] + term[16:24] + term[24:32]
            acc[key][e] = term if k == 0 else acc[key][e] + term

    def at_peaks(rows, k):
        value = mask_ref[0, k] * rows[0:1]
        for e in range(1, 4):
            value = value + mask_ref[e, k] * rows[e : e + 1]
        return value

    def ranges(position, k):
        sq_first = jnp.ones((RX, 128), f32)
        sq_second = sq_first
        firsts, seconds = [], []
        for comp in range(3):
            at = at_peaks(position[comp], k)
            d_first = at - fst_ref[comp]
            d_second = at - snd_ref[comp, k]
            sq_first = sq_first + d_first * d_first
            sq_second = sq_second + d_second * d_second
            firsts.append(d_first)
            seconds.append(d_second)
        inv_first = lax.rsqrt(sq_first)
        inv_second = lax.rsqrt(sq_second)
        spread = sq_second * inv_second - sq_first * inv_first
        spread_ref[k] = spread
        jac = [seconds[i] * inv_second - firsts[i] * inv_first for i in range(3)]
        for i in range(3):
            jac_ref[i, k] = jac[i]
        return spread, jac

    pairs = ((0, 0), (0, 1), (0, 2), (1, 1), (1, 2), (2, 2))
    acc = {key: [None] * 4 for key in range(7)}
    for k in range(4):
        _, jac = ranges(position, k)
        for key, (x, y) in enumerate(pairs):
            add_to(acc, key, k, jac[x] * jac[y])
        add_to(acc, 6, k, jnp.ones((RX, 128), f32))
    normals = [sum_rows(acc[key]) for key in range(6)]
    damp = 2.0 * (sum_rows(acc[6]) + 1.0)
    zero = jnp.zeros((4, 128), f32)

    def gn_step(step, carry):
        position, speed, bias, normals = carry
        moving = step.astype(f32) < steps
        acc = {key: [None] * 4 for key in range(3)}
        for k in range(4):
            delta = second_of(bias, k) - bias
            resid = tau_ref[k] - spread_ref[k] - delta
            for i in range(3):
                add_to(acc, i, k, jac_ref[i, k] * resid)
        moved = solve_three(normals, [sum_rows(acc[i]) for i in range(3)], damp)
        position = [position[i] + jnp.where(moving, moved[i], 0.0) for i in range(3)]
        acc = {key: [None] * 4 for key in range(9)}
        clock = None
        for k in range(4):
            spread, jac = ranges(position, k)
            for key, (x, y) in enumerate(pairs):
                add_to(acc, key, k, jac[x] * jac[y])
            rate = nu_ref[k]
            for i in range(3):
                rate = rate - at_peaks(speed[i], k) * jac[i]
            for i in range(3):
                add_to(acc, 6 + i, k, jac[i] * rate)
            live = mask_ref[0, k] + mask_ref[1, k] + mask_ref[2, k] + mask_ref[3, k]
            delta = second_of(bias, k) - bias
            cres = live * (tau_ref[k] - spread - delta)
            late = late_ref[k] * cres
            early = cres - late
            part = -cres
            for term, keep, shift in (
                (early, low, 2 * k + 1),
                (late, low, 2 * k + 2),
                (early, jnp.logical_not(low), 2 * k + 9),
                (late, jnp.logical_not(low), 2 * k + 10),
            ):
                part = part + pltpu.roll(jnp.where(keep, term, 0.0), shift, 0)
            clock = part if clock is None else clock + part
        normals = [sum_rows(acc[key]) for key in range(6)]
        turned = solve_three(normals, [sum_rows(acc[6 + i]) for i in range(3)], damp)
        speed = [speed[i] + jnp.where(moving, turned[i], 0.0) for i in range(3)]
        total = jnp.sum(clock, axis=1, keepdims=True)
        bias = bias + jnp.broadcast_to(total, (RX, 128)) / (3.0 * 16 * RX)
        return position, speed, bias, normals

    carry = (position, [zero, zero, zero], jnp.zeros((RX, 128), f32), normals)
    position, speed, bias, _ = lax.fori_loop(0, GN_MAX, gn_step, carry)
    r = lax.axis_index("rx")
    lane4 = iota((4, 128), 1)
    sub4 = iota((4, 128), 0)
    for out, value in ((pos_ref, position), (vel_ref, speed)):
        for i in range(3):
            column = jnp.sum(jnp.where(lane4 == r, value[i], 0.0), axis=1, keepdims=True)
            row = jnp.sum(jnp.where(lane4 == sub4, column, 0.0), axis=0, keepdims=True)
            out[i : i + 1, :] = row[:, 0:4]
    bias_row = jnp.sum(jnp.where(iota((RX, 128), 0) == lane, bias, 0.0), axis=0, keepdims=True)
    bias_ref[...] = bias_row[:, 0:RX]


def solve(table, receiver_pos):
    vmem = pl.BlockSpec(memory_space=pltpu.VMEM)
    block = (4, RX, 128)
    return pl.pallas_call(
        solve_kernel,
        out_shape=(
            jax.ShapeDtypeStruct((3, 4), f32),
            jax.ShapeDtypeStruct((3, 4), f32),
            jax.ShapeDtypeStruct((1, RX), f32),
        ),
        in_specs=[vmem, vmem],
        out_specs=(vmem, vmem, vmem),
        scratch_shapes=[
            pltpu.VMEM(block, f32),
            pltpu.VMEM(block, f32),
            pltpu.VMEM((4,) + block, f32),
            pltpu.VMEM(block, f32),
            pltpu.VMEM((3, RX, 128), f32),
            pltpu.VMEM((3,) + block, f32),
            pltpu.VMEM(block, f32),
            pltpu.VMEM((3,) + block, f32),
        ],
        name="solve",
    )(table, receiver_pos)


def local(
    consts, raw_samples, block_scales, lag_window_start, doppler_window_start,
    peak_owner, peak_emitter, gn_steps, receiver_pos, emitter_start,
):
    raw = raw_samples.reshape(8, SEG)
    scl = jnp.pad(block_scales, ((0, 0), (0, 124)))
    raw_all, scl_all = gather_samples(raw, scl)
    surf, pay = surfaces(
        raw_all, scl_all, lag_window_start, doppler_window_start,
        peak_owner.reshape(2, 16), peak_emitter, emitter_start, gn_steps.reshape(1, 4), consts,
    )
    amb, table = exchange(surf.reshape(TB, 4, 32, 128), pay)
    position, speed, bias = solve(table.reshape(TB, 2, RX, 128), receiver_pos)
    amb = amb.reshape(4, 16, 8, 2, 128).transpose(0, 1, 3, 2, 4).reshape(4, 16, 2, LAG_COUNT)
    return amb, position, speed, bias.reshape(RX)


def solution(mesh):
    placed = (
        P("rx", None, "tb"),
        P("rx", "tb"),
        P("rx", None),
        P("rx", None),
        P(("rx", "tb"), None, None),
        P(("rx", "tb"), None),
        P("rx"),
        P(),
        P(None, "rx"),
    )
    return jax.shard_map(
        functools.partial(local, tables()),
        mesh=mesh,
        in_specs=placed,
        out_specs=(P("tb", "rx", None, None), P(None, "rx"), P(None, "rx"), P()),
        check_vma=False,
    )
```

time: 1130 us -> 56.3 us (0.05); the launches traced: 1110 us -> 56.1 us
  blocking collectives: 533 us -> 0 us
  local copies, waits for them, and re-layouts: 304 us -> 3.65 us
  starting transfers between devices: 97.1 us -> 0 us
  waiting for transfers between devices: 68.1 us -> 0 us
  other arithmetic: 54.9 us -> 0 us
  Pallas kernels: 0 us -> 51.8 us
  matrix products: 39.9 us -> 0 us
  between operations: 15.2 us -> 0.66 us
    psum x13 -> x0, blocking collectives: 533 us -> none  [the longest x6 442 us: local(): clock_total = lax.psum(clock_terms, ('rx', 'tb'))]
    gather x2 -> x0, local copies, waits for them, and re-layouts: 276 us -> none  [pick_slot_first(): picked = surface[slot_index, dop_index, :, lag_index]]
    ppermute x17 -> x0, starting transfers between devices: 87.5 us -> none  [the longest x16 82.4 us: passed_along(): return lax.ppermute(block, axis, route)]
    pallas_call x0 -> x4, Pallas kernels: none -> 51.8 us  [the longest x1 19.7 us: gather_samples(): pl.pallas_call(gather_kernel, out_shape=(jax.ShapeDtypeStruct((3 * TB,) +...]
    reduce_scatter x2 -> x0, waiting for transfers between devices: 48.3 us -> none  [the longest x1 48.3 us: local(): lax.psum_scatter(window_part, 'tb', scatter_dimension=1, tiled=True)]
    dot_general x112 -> x0, matrix products: 39.9 us -> none  [the longest x1 8.12 us: lag_transform(): jnp.dot(spectra_in.reshape(-1, length), lag_coeff, precision=None, prefer...]
    another operation x16 -> x0, other arithmetic: 22.9 us -> none
    ppermute x17 -> x0, waiting for transfers between devices: 17.8 us -> none  [the longest x16 17.8 us: passed_along(): return lax.ppermute(block, axis, route)]
  transfers between devices with their start and end apart: 20 -> 0, of which waited for: 18 -> 0; matrix products, arithmetic and copies ran while one was open for 5% -> 0% of each run, Pallas kernels for 0% -> 0%
where the time goes in v1:
time: 56.3 us; the launch traced here: 56.1 us
  Pallas kernels  51.8 us (92%)
  local copies, waits for them, and re-layouts  3.65 us (6%)
  between operations  0.66 us (1%)
    pallas_call x1, Pallas kernels, gather_samples(): pl.pallas_call(gather_kernel, out_shape=(jax.ShapeDtypeStruct((3 * TB,) +...  19.7 us
    pallas_call x1, Pallas kernels, exchange(): pl.pallas_call(exchange_kernel, out_shape=(jax.ShapeDtypeStruct((4, TB, 3...  19.1 us
    pallas_call x1, Pallas kernels, solve(): pl.pallas_call(solve_kernel, out_shape=(jax.ShapeDtypeStruct((3, 4), f32)...  7 us
    pallas_call x1, Pallas kernels, surfaces(): pl.pallas_call(surface_kernel, out_shape=(jax.ShapeDtypeStruct((1024, 128...  5.98 us
    unnamed x3, local copies, waits for them, and re-layouts  1.87 us
    pad x1, local copies, waits for them, and re-layouts, local(): scl = jnp.pad(block_scales, ((0, 0), (0, 124)))  1.17 us

profile of v1, /device:TPU:1, one launch (start us, length us, event | category | flops | bytes accessed | tf_op | source)
XLA Modules:
  0.0 56.1 jit_solution(10432754775597763171)
XLA Ops:
  0.6 0.0 copy-start
  0.6 1.2 %pad.4.scl = f32[1,128]{1,0:T(1,128)} pad(f32[1,4]{1,0:T(1,128)} %param.15, f32[]{:T(128)} %constant.12.clone.1), padding=0_0x0_124 | pad | bytes 532 | tf_op jit(solution)/shard_map/jit(_pad)/pad | solution.py:587
  1.8 0.0 copy-done
  1.8 0.6 %reshape.32.raw = bf16[8,256]{1,0:T(8,128)(2,1)} reshape(bf16[1,2,1024]{2,1,0:T(2,128)(2,1)S(1)} %copy-done) | data formatting | bytes 8192 | tf_op jit(solution)/shard_map/reshape | solution.py:586
  2.4 19.7 %gather_samples.1 = (bf16[24,8,256]{2,1,0:T(8,128)(2,1)}, f32[24,1,128]{2,1,0:T(1,128)}) custom-call(bf16[8,256]{1,0:T(8,128)(2,1)} %reshape.32.raw, f32[1,128]{1,0:T(1,128)} %pad.4.scl), custom_call_target="tpu_custom_call" | custom-call | tf_op jit(solution)/shard_map/gather_samples/pallas_call | solution.py:109
  22.1 6.0 %surfaces.1 = (f32[1024,128]{1,0:T(8,128)}, f32[2,1,128]{2,1,0:T(1,128)}) custom-call(bf16[24,8,256]{2,1,0:T(8,128)(2,1)} %get-tuple-element.13.raw_ref, f32[24,1,128]{2,1,0:T(1,128)} %get-tuple-element.14.scl_ref, bf16[256,1024]{1,0:T(8,128)(2,1)} %constant.13.clone.fhi_ref, bf16[256,1024]{1,0:T(8,128)(2,1)} %constant.14.clone.flo_ref, ...), custom_call_target="tpu_custom_call" | custom-call | tf_op jit(solution)/shard_map/surfaces/pallas_call | solution.py:247
  28.1 19.1 %exchange.1 = (f32[4,8,32,128]{3,2,1,0:T(8,128)}, f32[8,2,32,1,128]{4,3,2,1,0:T(1,128)}) custom-call(f32[8,4,32,128]{3,2,1,0:T(8,128)} %bitcast.10, f32[2,1,128]{2,1,0:T(1,128)} %get-tuple-element.16.pay), custom_call_target="tpu_custom_call" | custom-call | tf_op jit(solution)/shard_map/exchange/pallas_call | solution.py:362
  47.2 7.0 %solve.1 = (f32[3,4]{1,0:T(4,128)}, f32[3,4]{1,0:T(4,128)}, f32[1,32]{1,0:T(1,128)}) custom-call(f32[8,2,32,128]{3,2,1,0:T(8,128)} %bitcast.12, f32[3,32]{1,0:T(4,128)} %rpos_ref.1), custom_call_target="tpu_custom_call" | custom-call | tf_op jit(solution)/shard_map/solve/pallas_call | solution.py:559
  54.2 1.9 %copy.20 = f32[4,16,2,1024]{3,2,1,0:T(2,128)} copy(f32[4,16,2,1024]{3,2,1,0:T(2,128)} %bitcast.11) | data formatting | bytes 1048576
Async XLA Ops:
  0.6 1.2 %copy-start = (bf16[1,2,1024]{2,1,0:T(2,128)(2,1)S(1)}, bf16[1,2,1024]{2,1,0:T(2,128)(2,1)}, u32[]{:S(2)}) copy-start(bf16[1,2,1024]{2,1,0:T(2,128)(2,1)} %param.14) | copy-start | bytes 12292

commit v2 on v1

v2 whole, which is shorter than its diff:
```python
import functools
import math

import jax
import jax.numpy as jnp
import numpy as np
from jax import lax
from jax.experimental import pallas as pl
from jax.experimental.pallas import tpu as pltpu
from jax.sharding import PartitionSpec as P

SEG = 256
DOPPLER_BINS = 32
LAG_COUNT = 1024
WL = 16
WD = 4
GN_MAX = 6
RX = 32
TB = 8
FFT = 512
SAMPLES = SEG * DOPPLER_BINS

MESH = pl.DeviceIdType.MESH
f32 = jnp.float32
bf16 = jnp.bfloat16
highest = lax.Precision.HIGHEST


def split_pair(table):
    high = table.astype(bf16)
    low = (table - high.astype(np.float64)).astype(bf16)
    return high, low


def tables():
    turn = 2.0 * np.pi / FFT
    t_f = np.arange(SEG)[:, None] * np.arange(FFT)[None, :] % FFT * turn
    forward = np.concatenate([np.cos(t_f), np.sin(t_f)], axis=1)
    backward = np.concatenate([np.cos(t_f.T), np.sin(t_f.T)], axis=1)
    d_m = (
        np.arange(DOPPLER_BINS)[:, None] * np.arange(DOPPLER_BINS)[None, :] % DOPPLER_BINS
    ) * (2.0 * np.pi / DOPPLER_BINS)
    mix = np.block([[np.cos(d_m), np.sin(d_m)], [-np.sin(d_m), np.cos(d_m)]])
    mix = mix / (FFT * math.sqrt(SAMPLES))
    return split_pair(forward) + split_pair(backward) + (mix.astype(np.float32),)


def iota(shape, dim):
    return lax.broadcasted_iota(jnp.int32, shape, dim)


def to_column(row, count):
    eye = iota((count, count), 0) == iota((count, count), 1)
    return jnp.sum(jnp.where(eye, row, 0.0), axis=1, keepdims=True)


def peer_lists(r, b):
    rows = [(lax.rem(r + d, RX), b) for d in range(1, RX)]
    blocks = [(r, lax.rem(b + d, TB)) for d in range(1, TB)]
    return rows, blocks


def remote(src, dst, send_sem, recv_sem, peer):
    return pltpu.make_async_remote_copy(
        src_ref=src,
        dst_ref=dst,
        send_sem=send_sem,
        recv_sem=recv_sem,
        device_id={"rx": peer[0], "tb": peer[1]},
        device_id_type=MESH,
    )


def front_kernel(
    raw_in, scl_in, lag_in, dop_in, own_in, em_in, start_in, steps_in,
    fhi_in, flo_in, bhi_in, blo_in, mix_in,
    amb, table,
    raw_ref, scl_ref, lag_ref, dop_ref, own_ref, em_ref, start_ref, steps_ref,
    fhi_ref, flo_ref, bhi_ref, blo_ref, mix_ref,
    block_ref, raw_all, scl_all, re_ref, im_ref, rr_ref, surf_ref, pay_ref,
    load_sem, raw_send, raw_recv, scl_send, scl_recv, code_send, code_recv,
    cfwd_send, cfwd_recv, pay_send, pay_recv, fwd_send, fwd_recv, surf_send, surf_recv, own_sem,
):
    r = lax.axis_index("rx")
    b = lax.axis_index("tb")
    barrier = pltpu.get_barrier_semaphore()
    rows, blocks = peer_lists(r, b)

    def signal(peer):
        pl.semaphore_signal(
            barrier, inc=1, device_id={"rx": peer[0], "tb": peer[1]}, device_id_type=MESH
        )

    sources = [
        (lax.rem(r + 2 * b + i, RX), lax.rem(b + d, TB)) for d in range(1, TB) for i in (1, 2)
    ]
    for peer in sources + rows + blocks:
        signal(peer)

    loads = [
        pltpu.make_async_copy(src, dst, load_sem.at[n])
        for n, (src, dst) in enumerate(
            (
                (raw_in, raw_ref), (scl_in, scl_ref), (own_in, own_ref), (em_in, em_ref),
                (start_in, start_ref), (steps_in, steps_ref), (lag_in, lag_ref),
                (dop_in, dop_ref), (fhi_in, fhi_ref), (flo_in, flo_ref), (bhi_in, bhi_ref),
                (blo_in, blo_ref), (mix_in, mix_ref),
            )
        )
    ]
    for copy in loads:
        copy.start()
    for copy in loads[:8]:
        copy.wait()
    own_raw = raw_ref[0].astype(f32)
    block_ref[...] = jnp.concatenate(
        [own_raw[k : k + 1, SEG * s : SEG * s + SEG] for k in range(2) for s in range(4)], axis=0
    ).astype(bf16)

    owner = jnp.concatenate(
        [to_column(own_ref[c : c + 1, :].astype(f32), 16) for c in range(2)], axis=0
    )
    code = jnp.concatenate(
        [to_column(em_ref[c : c + 1, :].astype(f32), 16) + (1.0 + 4.0 * c) for c in range(2)],
        axis=0,
    )
    p_row = iota((32, 32), 0)
    p_col = iota((32, 32), 1)
    owner_row = jnp.sum(jnp.where(p_row == p_col, owner, 0.0), axis=0, keepdims=True)
    same = (owner_row == owner) & (p_col < p_row)
    rank = jnp.sum(jnp.where(same, 1.0, 0.0), axis=1, keepdims=True)
    lane = iota((32, 128), 1)
    slot = lax.rem(lane, 64).astype(f32)
    placed = (rank * 32.0 + owner) == slot
    first = lane < 64
    codes = jnp.sum(jnp.where(placed & first, code, 0.0), axis=0, keepdims=True)
    lane1 = iota((1, 128), 1)
    for k in range(3):
        for e in range(4):
            codes = jnp.where(lane1 == 64 + 4 * k + e, start_ref[k : k + 1, e : e + 1], codes)
    for e in range(4):
        codes = jnp.where(lane1 == 76 + e, steps_ref[0:1, e : e + 1].astype(f32), codes)
    pay_ref[1] = codes
    raw_all[b] = block_ref[...]
    scl_all[b] = scl_ref[...]

    pl.semaphore_wait(barrier, len(sources) + len(rows) + len(blocks))

    targets = [(r, p, 0) for _, p in blocks]
    targets += [(lax.rem(r + RX - 2 * t - i, RX), t, i) for t in range(TB) for i in (1, 2)]
    sends = []
    for n, (to_r, to_b, i) in enumerate(targets):
        place = i * TB + b
        for src, dst, ss, rs in (
            (block_ref, raw_all, raw_send, raw_recv),
            (scl_ref, scl_all, scl_send, scl_recv),
        ):
            sends.append(remote(src, dst.at[place], ss.at[n], rs.at[place], (to_r, to_b)))
            sends[-1].start()
    own_code = pltpu.make_async_copy(pay_ref.at[1], table.at[b, 1, r], own_sem.at[0])
    own_code.start()
    for n, peer in enumerate(rows):
        sends.append(
            remote(pay_ref.at[1], table.at[b, 1, r], code_send.at[n], code_recv.at[r], peer)
        )
        sends[-1].start()

    places = [p for _, p in blocks] + [i * TB + t for i in (1, 2) for t in range(TB)]
    for place in places:
        remote(
            block_ref, raw_all.at[place], raw_send.at[0], raw_recv.at[place], blocks[0]
        ).wait_recv()
        remote(
            scl_ref, scl_all.at[place], scl_send.at[0], scl_recv.at[place], blocks[0]
        ).wait_recv()
    own_code.wait()
    for q, _ in rows:
        remote(
            pay_ref.at[1], table.at[b, 1, q], code_send.at[0], code_recv.at[q], rows[0]
        ).wait_recv()
    for n, peer in enumerate(blocks):
        sends.append(
            remote(table.at[b, 1], table.at[b, 1], cfwd_send.at[n], cfwd_recv.at[b], peer)
        )
        sends[-1].start()
    for copy in loads[8:]:
        copy.wait()

    raw = raw_all[...].astype(f32).reshape(3 * TB * 8, SEG).astype(bf16)
    spec = jnp.dot(raw, fhi_ref[...], preferred_element_type=f32)
    spec = spec + jnp.dot(raw, flo_ref[...], preferred_element_type=f32)
    cos_part = spec[:, :FFT].reshape(3 * TB, 8, FFT)
    sin_part = spec[:, FFT:].reshape(3 * TB, 8, FFT)
    sub = iota((1, 8, 1), 1)
    sign = jnp.where(sub < 4, 1.0, -1.0).astype(f32)
    pick = iota((1, 8, 4), 2) == lax.rem(iota((1, 8, 4), 1), 4)
    scale = jnp.sum(jnp.where(pick, scl_all[...], 0.0), axis=2, keepdims=True)
    pieces = (cos_part + sign * pltpu.roll(sin_part, 4, 1)) * scale
    for i in range(3):
        re_ref[i, 32:40, :] = jnp.zeros((8, FFT), f32)
        im_ref[i, 32:40, :] = jnp.zeros((8, FFT), f32)
        for t in range(TB):
            re_ref[i, 4 * t : 4 * t + 4, :] = pieces[i * TB + t, 0:4, :]
            im_ref[i, 4 * t : 4 * t + 4, :] = pieces[i * TB + t, 4:8, :]
    near_re = re_ref[0, 0:32, :]
    near_im = im_ref[0, 0:32, :]
    alt = jnp.where(lax.rem(iota((1, FFT), 1), 2) == 0, 1.0, -1.0).astype(f32)
    for c in range(2):
        for j in range(4):
            far_re = re_ref[c + 1, j : j + 32, :] + alt * re_ref[c + 1, j + 1 : j + 33, :]
            far_im = im_ref[c + 1, j : j + 32, :] + alt * im_ref[c + 1, j + 1 : j + 33, :]
            row = (c * 4 + j) * 32
            rr_ref[row : row + 32, :] = near_re * far_re + near_im * far_im
            rr_ref[256 + row : 288 + row, :] = near_im * far_re - near_re * far_im
    cross = rr_ref[...]
    high = cross.astype(bf16)
    low = (cross - high.astype(f32)).astype(bf16)
    lagged = jnp.dot(high, bhi_ref[...], preferred_element_type=f32)
    lagged = lagged + jnp.dot(low, bhi_ref[...], preferred_element_type=f32)
    lagged = lagged + jnp.dot(high, blo_ref[...], preferred_element_type=f32)
    lag_re = lagged[0:256, 0:256] + lagged[256:512, 256:512]
    lag_im = lagged[256:512, 0:256] - lagged[0:256, 256:512]

    lag_rows = lag_ref[pl.ds(2 * b, 2), :].astype(f32)
    dop_rows = dop_ref[pl.ds(2 * b, 2), :].astype(f32)
    tau_cols, nu_cols = [], []
    for c in range(2):
        top = jnp.concatenate(
            [lag_re[(c * 4 + j) * 32 : (c * 4 + j + 1) * 32] for j in range(4)], axis=1
        )
        low_half = jnp.concatenate(
            [lag_im[(c * 4 + j) * 32 : (c * 4 + j + 1) * 32] for j in range(4)], axis=1
        )
        stacked = jnp.concatenate([top, low_half], axis=0)
        surf = jnp.dot(mix_ref[...], stacked, precision=highest, preferred_element_type=f32)
        for comp in range(2):
            for lt in range(8):
                surf_ref[pl.ds(c * 16 + lt * 2 + comp, 32, stride=32), :] = surf[
                    comp * 32 : comp * 32 + 32, lt * 128 : lt * 128 + 128
                ]
        power = surf[0:32] * surf[0:32] + surf[32:64] * surf[32:64]
        lag0 = to_column(lag_rows[c : c + 1, :], 16)
        dop0 = to_column(dop_rows[c : c + 1, :], 16)
        offset = iota((16, DOPPLER_BINS), 1).astype(f32) - dop0
        offset = jnp.where(offset < 0.0, offset + DOPPLER_BINS, offset)
        inside = jnp.where(offset < WD, 1.0, 0.0).astype(f32)
        weights = jnp.concatenate([inside, inside * offset], axis=0)
        sums = jnp.dot(weights, power, precision=highest, preferred_element_type=f32)
        step = iota((16, LAG_COUNT), 1).astype(f32) - lag0
        within = (step >= 0.0) & (step < WL)
        plain = jnp.where(within, sums[0:16], 0.0)
        norm = 1.0 / (WL * WD)
        total = jnp.sum(plain, axis=1, keepdims=True) * norm + 1e-06
        lag_mean = jnp.sum(plain * step, axis=1, keepdims=True) * norm / total
        dop_mean = (
            jnp.sum(jnp.where(within, sums[16:32], 0.0), axis=1, keepdims=True) * norm / total
        )
        tau_cols.append((lag0 + lag_mean) * (16.0 / LAG_COUNT))
        nu_cols.append((dop0 + dop_mean) * (4.0 / DOPPLER_BINS))
    tau = jnp.concatenate(tau_cols, axis=0)
    nu = jnp.concatenate(nu_cols, axis=0)
    pay_ref[0] = jnp.sum(
        jnp.where(placed, jnp.where(first, tau, nu), 0.0), axis=0, keepdims=True
    )

    own_pay = pltpu.make_async_copy(pay_ref.at[0], table.at[b, 0, r], own_sem.at[0])
    own_pay.start()
    for n, peer in enumerate(rows):
        sends.append(
            remote(pay_ref.at[0], table.at[b, 0, r], pay_send.at[n], pay_recv.at[r], peer)
        )
        sends[-1].start()
    locals_ = []
    for d in range(4):
        locals_.append(
            pltpu.make_async_copy(
                surf_ref.at[pl.ds(pl.multiple_of(128 * b + 32 * d, 32), 32), :],
                amb.at[d, b],
                own_sem.at[1 + d],
            )
        )
        locals_[-1].start()
    for n, peer in enumerate(blocks):
        for d in range(4):
            sends.append(
                remote(
                    surf_ref.at[pl.ds(pl.multiple_of(128 * peer[1] + 32 * d, 32), 32), :],
                    amb.at[d, b],
                    surf_send.at[n, d],
                    surf_recv.at[b, d],
                    peer,
                )
            )
            sends[-1].start()
    own_pay.wait()
    plane = r // 4
    spot = lax.rem(r, 4)
    for count, dz in enumerate((0, 1, 7, 2, 6, 3, 5, 4)):
        there = lax.rem(plane + dz, 8)
        for dx in range(4):
            if dz == 0 and dx == 0:
                continue
            q = there * 4 + lax.rem(spot + dx, 4)
            remote(
                pay_ref.at[0], table.at[b, 0, q], pay_send.at[0], pay_recv.at[q], rows[0]
            ).wait_recv()
        chunk = table.at[b, 0, pl.ds(there * 4, 4)]
        for n, peer in enumerate(blocks):
            sends.append(
                remote(chunk, chunk, fwd_send.at[n, count], fwd_recv.at[b, there], peer)
            )
            sends[-1].start()
    for _, t in blocks:
        remote(
            table.at[t, 1], table.at[t, 1], cfwd_send.at[0], cfwd_recv.at[t], blocks[0]
        ).wait_recv()
        for z in range(8):
            chunk = table.at[t, 0, pl.ds(z * 4, 4)]
            remote(chunk, chunk, fwd_send.at[0, 0], fwd_recv.at[t, z], blocks[0]).wait_recv()
        for d in range(4):
            remote(
                surf_ref.at[pl.ds(0, 32), :],
                amb.at[d, t],
                surf_send.at[0, 0],
                surf_recv.at[t, d],
                blocks[0],
            ).wait_recv()
    for copy in locals_:
        copy.wait()
    for copy in sends:
        copy.wait_send()


def front(raw, scl, lag, dop, own, em, start, steps, consts):
    any_spec = pl.BlockSpec(memory_space=pl.ANY)
    dma = pltpu.SemaphoreType.DMA
    operands = (raw, scl, lag, dop, own, em, start, steps, *consts)
    n = 3 * TB - 1
    return pl.pallas_call(
        front_kernel,
        out_shape=(
            jax.ShapeDtypeStruct((4, TB, 32, 128), f32),
            jax.ShapeDtypeStruct((TB, 2, RX, 1, 128), f32),
        ),
        in_specs=[any_spec] * len(operands),
        out_specs=(any_spec, any_spec),
        scratch_shapes=[pltpu.VMEM(x.shape, x.dtype) for x in operands]
        + [
            pltpu.VMEM((8, SEG), bf16),
            pltpu.VMEM((3 * TB, 8, SEG), bf16),
            pltpu.VMEM((3 * TB,) + scl.shape, f32),
            pltpu.VMEM((3, 40, FFT), f32),
            pltpu.VMEM((3, 40, FFT), f32),
            pltpu.VMEM((512, FFT), f32),
            pltpu.VMEM((1024, 128), f32),
            pltpu.VMEM((2, 1, 128), f32),
            dma((len(operands),)),
            dma((n,)), dma((3 * TB,)), dma((n,)), dma((3 * TB,)),
            dma((RX - 1,)), dma((RX,)), dma((TB - 1,)), dma((TB,)),
            dma((RX - 1,)), dma((RX,)), dma((TB - 1, 8)), dma((TB, 8)),
            dma((TB - 1, 4)), dma((TB, 4)), dma((5,)),
        ],
        compiler_params=pltpu.CompilerParams(collective_id=0, has_side_effects=True),
        name="front",
    )(*operands)


def solve_three(normals, rhs, damp_term):
    entry_xx = normals[0] + damp_term
    entry_xy = normals[1]
    entry_xz = normals[2]
    entry_yy = normals[3] + damp_term
    entry_yz = normals[4]
    entry_zz = normals[5] + damp_term
    minor_xx = entry_yy * entry_zz - entry_yz * entry_yz
    minor_xy = entry_xz * entry_yz - entry_xy * entry_zz
    minor_xz = entry_xy * entry_yz - entry_xz * entry_yy
    minor_yy = entry_xx * entry_zz - entry_xz * entry_xz
    minor_yz = entry_xy * entry_xz - entry_xx * entry_yz
    minor_zz = entry_xx * entry_yy - entry_xy * entry_xy
    inverse = 1.0 / (entry_xx * minor_xx + entry_xy * minor_xy + entry_xz * minor_xz)
    step_x = minor_xx * rhs[0] + minor_xy * rhs[1] + minor_xz * rhs[2]
    step_y = minor_xy * rhs[0] + minor_yy * rhs[1] + minor_yz * rhs[2]
    step_z = minor_xz * rhs[0] + minor_yz * rhs[1] + minor_zz * rhs[2]
    return [step_x * inverse, step_y * inverse, step_z * inverse]


def per_receiver(x, shift):
    return pltpu.roll(x, (RX - shift) % RX, 0)


def solve_kernel(
    table_ref, rpos_ref, amb_in, pos_ref, vel_ref, bias_ref, amb_out,
    stage_ref, stage_sem, tau_ref, nu_ref, mask_ref, late_ref, fst_ref, snd_ref, spread_ref, jac_ref,
):
    stage_in = pltpu.make_async_copy(amb_in, stage_ref, stage_sem.at[0])
    stage_in.start()
    lane = iota((RX, 128), 1)
    low = lane < 64
    own_lane = iota((RX, 128), 0) == lax.rem(lane, RX)
    halves = []
    for k in range(4):
        a0, a1 = table_ref[k, 0], table_ref[k + 4, 0]
        tau_ref[k] = jnp.where(low, a0, pltpu.roll(a1, 64, 1))
        nu_ref[k] = jnp.where(low, pltpu.roll(a0, 64, 1), a1)
        code = jnp.where(low, table_ref[k, 1], pltpu.roll(table_ref[k + 4, 1], 64, 1))
        late = code > 4.5
        late_ref[k] = jnp.where(late, 1.0, 0.0)
        emitter = jnp.where(late, code - 4.0, code)
        for e in range(4):
            mask_ref[e, k] = jnp.where(emitter == e + 1.0, 1.0, 0.0)

    info = table_ref[0, 1]

    def owner_row(col):
        value = jnp.sum(jnp.where(lane == col, info, 0.0), axis=1, keepdims=True)
        return jnp.sum(jnp.where(own_lane, value, 0.0), axis=0, keepdims=True)

    def owner_rows(base):
        return jnp.concatenate([owner_row(base + e) for e in range(4)], axis=0)

    position = [owner_rows(64 + 4 * k) for k in range(3)]
    steps = owner_rows(76)

    def second_of(x, k):
        late = late_ref[k] > 0.5
        near_half = jnp.where(late, per_receiver(x, 2 * k + 2), per_receiver(x, 2 * k + 1))
        far_half = jnp.where(late, per_receiver(x, 2 * k + 10), per_receiver(x, 2 * k + 9))
        return jnp.where(low, near_half, far_half)

    eye = iota((RX, RX), 0) == iota((RX, RX), 1)
    for comp in range(3):
        column = jnp.sum(
            jnp.where(eye, rpos_ref[comp : comp + 1, :], 0.0), axis=1, keepdims=True
        )
        column = jnp.broadcast_to(column, (RX, 128))
        fst_ref[comp] = column
        for k in range(4):
            snd_ref[comp, k] = second_of(column, k)

    def sum_rows(parts):
        rows = jnp.concatenate([jnp.sum(p, axis=0, keepdims=True) for p in parts], axis=0)
        rows = rows + pltpu.roll(rows, 32, 1)
        return rows + pltpu.roll(rows, 64, 1)

    def add_to(acc, key, k, quantity):
        for e in range(4):
            term = mask_ref[e, k] * quantity
            term = term[0:8] + term[8:16] + term[16:24] + term[24:32]
            acc[key][e] = term if k == 0 else acc[key][e] + term

    def at_peaks(rows, k):
        value = mask_ref[0, k] * rows[0:1]
        for e in range(1, 4):
            value = value + mask_ref[e, k] * rows[e : e + 1]
        return value

    def ranges(position, k):
        sq_first = jnp.ones((RX, 128), f32)
        sq_second = sq_first
        firsts, seconds = [], []
        for comp in range(3):
            at = at_peaks(position[comp], k)
            d_first = at - fst_ref[comp]
            d_second = at - snd_ref[comp, k]
            sq_first = sq_first + d_first * d_first
            sq_second = sq_second + d_second * d_second
            firsts.append(d_first)
            seconds.append(d_second)
        inv_first = lax.rsqrt(sq_first)
        inv_second = lax.rsqrt(sq_second)
        spread = sq_second * inv_second - sq_first * inv_first
        spread_ref[k] = spread
        jac = [seconds[i] * inv_second - firsts[i] * inv_first for i in range(3)]
        for i in range(3):
            jac_ref[i, k] = jac[i]
        return spread, jac

    pairs = ((0, 0), (0, 1), (0, 2), (1, 1), (1, 2), (2, 2))
    acc = {key: [None] * 4 for key in range(7)}
    for k in range(4):
        _, jac = ranges(position, k)
        for key, (x, y) in enumerate(pairs):
            add_to(acc, key, k, jac[x] * jac[y])
        add_to(acc, 6, k, jnp.ones((RX, 128), f32))
    normals = [sum_rows(acc[key]) for key in range(6)]
    damp = 2.0 * (sum_rows(acc[6]) + 1.0)
    zero = jnp.zeros((4, 128), f32)

    def gn_step(step, carry):
        position, speed, bias, normals = carry
        moving = step.astype(f32) < steps
        acc = {key: [None] * 4 for key in range(3)}
        for k in range(4):
            delta = second_of(bias, k) - bias
            resid = tau_ref[k] - spread_ref[k] - delta
            for i in range(3):
                add_to(acc, i, k, jac_ref[i, k] * resid)
        moved = solve_three(normals, [sum_rows(acc[i]) for i in range(3)], damp)
        position = [position[i] + jnp.where(moving, moved[i], 0.0) for i in range(3)]
        acc = {key: [None] * 4 for key in range(9)}
        clock = None
        for k in range(4):
            spread, jac = ranges(position, k)
            for key, (x, y) in enumerate(pairs):
                add_to(acc, key, k, jac[x] * jac[y])
            rate = nu_ref[k]
            for i in range(3):
                rate = rate - at_peaks(speed[i], k) * jac[i]
            for i in range(3):
                add_to(acc, 6 + i, k, jac[i] * rate)
            live = mask_ref[0, k] + mask_ref[1, k] + mask_ref[2, k] + mask_ref[3, k]
            delta = second_of(bias, k) - bias
            cres = live * (tau_ref[k] - spread - delta)
            late = late_ref[k] * cres
            early = cres - late
            part = -cres
            for term, keep, shift in (
                (early, low, 2 * k + 1),
                (late, low, 2 * k + 2),
                (early, jnp.logical_not(low), 2 * k + 9),
                (late, jnp.logical_not(low), 2 * k + 10),
            ):
                part = part + pltpu.roll(jnp.where(keep, term, 0.0), shift, 0)
            clock = part if clock is None else clock + part
        normals = [sum_rows(acc[key]) for key in range(6)]
        turned = solve_three(normals, [sum_rows(acc[6 + i]) for i in range(3)], damp)
        speed = [speed[i] + jnp.where(moving, turned[i], 0.0) for i in range(3)]
        total = jnp.sum(clock, axis=1, keepdims=True)
        bias = bias + jnp.broadcast_to(total, (RX, 128)) / (3.0 * 16 * RX)
        return position, speed, bias, normals

    stage_in.wait()
    stage_out = [
        pltpu.make_async_copy(
            stage_ref.at[:, :, lt],
            amb_out.at[:, :, :, lt * 128 : lt * 128 + 128],
            stage_sem.at[1 + lt],
        )
        for lt in range(8)
    ]
    for copy in stage_out:
        copy.start()
    carry = (position, [zero, zero, zero], jnp.zeros((RX, 128), f32), normals)
    position, speed, bias, _ = lax.fori_loop(0, GN_MAX, gn_step, carry)
    r = lax.axis_index("rx")
    lane4 = iota((4, 128), 1)
    sub4 = iota((4, 128), 0)
    for out, value in ((pos_ref, position), (vel_ref, speed)):
        for i in range(3):
            column = jnp.sum(jnp.where(lane4 == r, value[i], 0.0), axis=1, keepdims=True)
            row = jnp.sum(jnp.where(lane4 == sub4, column, 0.0), axis=0, keepdims=True)
            out[i : i + 1, :] = row[:, 0:4]
    bias_row = jnp.sum(jnp.where(iota((RX, 128), 0) == lane, bias, 0.0), axis=0, keepdims=True)
    bias_ref[...] = bias_row[:, 0:RX]
    for copy in stage_out:
        copy.wait()


def solve(table, receiver_pos, amb):
    any_spec = pl.BlockSpec(memory_space=pl.ANY)
    vmem = pl.BlockSpec(memory_space=pltpu.VMEM)
    block = (4, RX, 128)
    return pl.pallas_call(
        solve_kernel,
        out_shape=(
            jax.ShapeDtypeStruct((3, 4), f32),
            jax.ShapeDtypeStruct((3, 4), f32),
            jax.ShapeDtypeStruct((1, RX), f32),
            jax.ShapeDtypeStruct((4, 16, 2, LAG_COUNT), f32),
        ),
        in_specs=[vmem, vmem, any_spec],
        out_specs=(vmem, vmem, vmem, any_spec),
        scratch_shapes=[
            pltpu.VMEM((4, 16, 8, 2, 128), f32),
            pltpu.SemaphoreType.DMA((9,)),
            pltpu.VMEM(block, f32),
            pltpu.VMEM(block, f32),
            pltpu.VMEM((4,) + block, f32),
            pltpu.VMEM(block, f32),
            pltpu.VMEM((3, RX, 128), f32),
            pltpu.VMEM((3,) + block, f32),
            pltpu.VMEM(block, f32),
            pltpu.VMEM((3,) + block, f32),
        ],
        name="solve",
    )(table, receiver_pos, amb)


def local(
    consts, raw_samples, block_scales, lag_window_start, doppler_window_start,
    peak_owner, peak_emitter, gn_steps, receiver_pos, emitter_start,
):
    amb, table = front(
        raw_samples, block_scales, lag_window_start, doppler_window_start,
        peak_owner.reshape(2, 16), peak_emitter, emitter_start, gn_steps.reshape(1, 4), consts,
    )
    position, speed, bias, amb = solve(
        table.reshape(TB, 2, RX, 128), receiver_pos, amb.reshape(4, 16, 8, 2, 128)
    )
    return amb, position, speed, bias.reshape(RX)


def solution(mesh):
    placed = (
        P("rx", None, "tb"),
        P("rx", "tb"),
        P("rx", None),
        P("rx", None),
        P(("rx", "tb"), None, None),
        P(("rx", "tb"), None),
        P("rx"),
        P(),
        P(None, "rx"),
    )
    return jax.shard_map(
        functools.partial(local, tables()),
        mesh=mesh,
        in_specs=placed,
        out_specs=(P("tb", "rx", None, None), P(None, "rx"), P(None, "rx"), P()),
        check_vma=False,
    )
```

time: 56.3 us -> 47.7 us (0.85)
  Pallas kernels: 51.8 us -> 46.9 us
  local copies, waits for them, and re-layouts: 3.65 us -> 0 us
    pallas_call x3 -> x1, Pallas kernels: 44.8 us -> 39.4 us  [front(): pl.pallas_call(front_kernel, out_shape=(jax.ShapeDtypeStruct((4, TB, 32,...]
    unnamed x3 -> x0, local copies, waits for them, and re-layouts: 1.87 us -> none
    pad x1 -> x0, local copies, waits for them, and re-layouts: 1.17 us -> none  [local(): scl = jnp.pad(block_scales, ((0, 0), (0, 124)))]
    reshape x1 -> x0, local copies, waits for them, and re-layouts: 0.6 us -> none  [local(): raw = raw_samples.reshape(8, SEG)]
where the time goes in v2:
time: 47.7 us; the launch traced here: 47.5 us
  Pallas kernels  46.9 us (98%)
  between operations  0.64 us (1%)
    pallas_call x1, Pallas kernels, front(): pl.pallas_call(front_kernel, out_shape=(jax.ShapeDtypeStruct((4, TB, 32,...  39.4 us
    pallas_call x1, Pallas kernels, solve(): pl.pallas_call(solve_kernel, out_shape=(jax.ShapeDtypeStruct((3, 4), f32)...  7.48 us

profile of v2, /device:TPU:1, one launch (start us, length us, event | category | flops | bytes accessed | tf_op | source)
XLA Modules:
  0.0 47.5 jit_solution(15779009139610040933)
XLA Ops:
  0.6 39.4 %front.1 = (f32[4,8,32,128]{3,2,1,0:T(8,128)}, f32[8,2,32,1,128]{4,3,2,1,0:T(1,128)}) custom-call(bf16[1,2,1024]{2,1,0:T(2,128)(2,1)} %raw_in.1, f32[1,4]{1,0:T(1,128)} %scl_in.1, s32[16,16]{1,0:T(8,128)} %lag_in.1, s32[16,16]{1,0:T(8,128)} %dop_in.1, s32[2,16]{1,0:T(2,128)} %bitcast.7, s32[2,16]{1,0:T(2,128)} %em_in.1, f32[3,4]{1,0:T(4,128)} %start_in.1, ...), custom_call_target="tpu_custom_call" | custom-call | tf_op jit(solution)/shard_map/front/pallas_call | solution.py:339
  40.0 7.5 %solve.1 = (f32[3,4]{1,0:T(4,128)}, f32[3,4]{1,0:T(4,128)}, f32[1,32]{1,0:T(1,128)}, f32[4,16,2,1024]{3,2,1,0:T(2,128)}) custom-call(f32[8,2,32,128]{3,2,1,0:T(8,128)} %bitcast.6, f32[3,32]{1,0:T(4,128)} %rpos_ref.1, f32[4,16,8,2,128]{4,3,2,1,0:T(2,128)} %bitcast.5), custom_call_target="tpu_custom_call" | custom-call | tf_op jit(solution)/shard_map/solve/pallas_call | solution.py:564

commit v3 on v2

--- a/solution.py
+++ b/solution.py
@@ -110,13 +110,31 @@
     ]
     for copy in loads:
         copy.start()
-    for copy in loads[:8]:
+    for copy in loads[:2]:
         copy.wait()
     own_raw = raw_ref[0].astype(f32)
     block_ref[...] = jnp.concatenate(
         [own_raw[k : k + 1, SEG * s : SEG * s + SEG] for k in range(2) for s in range(4)], axis=0
     ).astype(bf16)
 
+    raw_all[b] = block_ref[...]
+    scl_all[b] = scl_ref[...]
+
+    pl.semaphore_wait(barrier, len(sources) + len(rows) + len(blocks))
+
+    targets = [(r, p, 0) for _, p in blocks]
+    targets += [(lax.rem(r + RX - 2 * t - i, RX), t, i) for t in range(TB) for i in (1, 2)]
+    sends = []
+    for n, (to_r, to_b, i) in enumerate(targets):
+        place = i * TB + b
+        for src, dst, ss, rs in (
+            (block_ref, raw_all, raw_send, raw_recv),
+            (scl_ref, scl_all, scl_send, scl_recv),
+        ):
+            sends.append(remote(src, dst.at[place], ss.at[n], rs.at[place], (to_r, to_b)))
+            sends[-1].start()
+    for copy in loads[2:8]:
+        copy.wait()
     owner = jnp.concatenate(
         [to_column(own_ref[c : c + 1, :].astype(f32), 16) for c in range(2)], axis=0
     )
@@ -141,29 +159,14 @@
     for e in range(4):
         codes = jnp.where(lane1 == 76 + e, steps_ref[0:1, e : e + 1].astype(f32), codes)
     pay_ref[1] = codes
-    raw_all[b] = block_ref[...]
-    scl_all[b] = scl_ref[...]
-
-    pl.semaphore_wait(barrier, len(sources) + len(rows) + len(blocks))
-
-    targets = [(r, p, 0) for _, p in blocks]
-    targets += [(lax.rem(r + RX - 2 * t - i, RX), t, i) for t in range(TB) for i in (1, 2)]
-    sends = []
-    for n, (to_r, to_b, i) in enumerate(targets):
-        place = i * TB + b
-        for src, dst, ss, rs in (
-            (block_ref, raw_all, raw_send, raw_recv),
-            (scl_ref, scl_all, scl_send, scl_recv),
-        ):
-            sends.append(remote(src, dst.at[place], ss.at[n], rs.at[place], (to_r, to_b)))
-            sends[-1].start()
-    own_code = pltpu.make_async_copy(pay_ref.at[1], table.at[b, 1, r], own_sem.at[0])
+    own_code = pltpu.make_async_copy(pay_ref.at[1], table.at[b, 1, r], own_sem.at[5])
     own_code.start()
     for n, peer in enumerate(rows):
         sends.append(
             remote(pay_ref.at[1], table.at[b, 1, r], code_send.at[n], code_recv.at[r], peer)
         )
         sends[-1].start()
+
 
     places = [p for _, p in blocks] + [i * TB + t for i in (1, 2) for t in range(TB)]
     for place in places:
@@ -173,16 +176,6 @@
         remote(
             scl_ref, scl_all.at[place], scl_send.at[0], scl_recv.at[place], blocks[0]
         ).wait_recv()
-    own_code.wait()
-    for q, _ in rows:
-        remote(
-            pay_ref.at[1], table.at[b, 1, q], code_send.at[0], code_recv.at[q], rows[0]
-        ).wait_recv()
-    for n, peer in enumerate(blocks):
-        sends.append(
-            remote(table.at[b, 1], table.at[b, 1], cfwd_send.at[n], cfwd_recv.at[b], peer)
-        )
-        sends[-1].start()
     for copy in loads[8:]:
         copy.wait()
 
@@ -223,7 +216,7 @@
 
     lag_rows = lag_ref[pl.ds(2 * b, 2), :].astype(f32)
     dop_rows = dop_ref[pl.ds(2 * b, 2), :].astype(f32)
-    tau_cols, nu_cols = [], []
+    tau_cols, nu_cols, surfs = [], [], []
     for c in range(2):
         top = jnp.concatenate(
             [lag_re[(c * 4 + j) * 32 : (c * 4 + j + 1) * 32] for j in range(4)], axis=1
@@ -233,11 +226,7 @@
         )
         stacked = jnp.concatenate([top, low_half], axis=0)
         surf = jnp.dot(mix_ref[...], stacked, precision=highest, preferred_element_type=f32)
-        for comp in range(2):
-            for lt in range(8):
-                surf_ref[pl.ds(c * 16 + lt * 2 + comp, 32, stride=32), :] = surf[
-                    comp * 32 : comp * 32 + 32, lt * 128 : lt * 128 + 128
-                ]
+        surfs.append(surf)
         power = surf[0:32] * surf[0:32] + surf[32:64] * surf[32:64]
         lag0 = to_column(lag_rows[c : c + 1, :], 16)
         dop0 = to_column(dop_rows[c : c + 1, :], 16)
@@ -270,6 +259,22 @@
             remote(pay_ref.at[0], table.at[b, 0, r], pay_send.at[n], pay_recv.at[r], peer)
         )
         sends[-1].start()
+    own_code.wait()
+    for q, _ in rows:
+        remote(
+            pay_ref.at[1], table.at[b, 1, q], code_send.at[0], code_recv.at[q], rows[0]
+        ).wait_recv()
+    for n, peer in enumerate(blocks):
+        sends.append(
+            remote(table.at[b, 1], table.at[b, 1], cfwd_send.at[n], cfwd_recv.at[b], peer)
+        )
+        sends[-1].start()
+    for c in range(2):
+        for comp in range(2):
+            for lt in range(8):
+                surf_ref[pl.ds(c * 16 + lt * 2 + comp, 32, stride=32), :] = surfs[c][
+                    comp * 32 : comp * 32 + 32, lt * 128 : lt * 128 + 128
+                ]
     locals_ = []
     for d in range(4):
         locals_.append(
@@ -339,8 +344,8 @@
     return pl.pallas_call(
         front_kernel,
         out_shape=(
-            jax.ShapeDtypeStruct((4, TB, 32, 128), f32),
-            jax.ShapeDtypeStruct((TB, 2, RX, 1, 128), f32),
+            pltpu.VMEM((4, TB, 32, 128), f32),
+            pltpu.VMEM((TB, 2, RX, 1, 128), f32),
         ),
         in_specs=[any_spec] * len(operands),
         out_specs=(any_spec, any_spec),
@@ -358,7 +363,7 @@
             dma((n,)), dma((3 * TB,)), dma((n,)), dma((3 * TB,)),
             dma((RX - 1,)), dma((RX,)), dma((TB - 1,)), dma((TB,)),
             dma((RX - 1,)), dma((RX,)), dma((TB - 1, 8)), dma((TB, 8)),
-            dma((TB - 1, 4)), dma((TB, 4)), dma((5,)),
+            dma((TB - 1, 4)), dma((TB, 4)), dma((6,)),
         ],
         compiler_params=pltpu.CompilerParams(collective_id=0, has_side_effects=True),
         name="front",
@@ -390,11 +395,21 @@
 
 
 def solve_kernel(
-    table_ref, rpos_ref, amb_in, pos_ref, vel_ref, bias_ref, amb_out,
-    stage_ref, stage_sem, tau_ref, nu_ref, mask_ref, late_ref, fst_ref, snd_ref, spread_ref, jac_ref,
+    table_ref, rpos_in, amb_in, pos_ref, vel_ref, bias_ref, amb_out,
+    rpos_ref, stage_sem, tau_ref, nu_ref, mask_ref, late_ref, fst_ref, snd_ref, spread_ref, jac_ref,
 ):
-    stage_in = pltpu.make_async_copy(amb_in, stage_ref, stage_sem.at[0])
-    stage_in.start()
+    stage_out = [
+        pltpu.make_async_copy(
+            amb_in.at[:, :, lt],
+            amb_out.at[:, :, :, lt * 128 : lt * 128 + 128],
+            stage_sem.at[lt],
+        )
+        for lt in range(8)
+    ]
+    rpos_copy = pltpu.make_async_copy(rpos_in, rpos_ref, stage_sem.at[8])
+    rpos_copy.start()
+    for copy in stage_out:
+        copy.start()
     lane = iota((RX, 128), 1)
     low = lane < 64
     own_lane = iota((RX, 128), 0) == lax.rem(lane, RX)
@@ -428,6 +443,7 @@
         far_half = jnp.where(late, per_receiver(x, 2 * k + 10), per_receiver(x, 2 * k + 9))
         return jnp.where(low, near_half, far_half)
 
+    rpos_copy.wait()
     eye = iota((RX, RX), 0) == iota((RX, RX), 1)
     for comp in range(3):
         column = jnp.sum(
@@ -530,17 +546,6 @@
         bias = bias + jnp.broadcast_to(total, (RX, 128)) / (3.0 * 16 * RX)
         return position, speed, bias, normals
 
-    stage_in.wait()
-    stage_out = [
-        pltpu.make_async_copy(
-            stage_ref.at[:, :, lt],
-            amb_out.at[:, :, :, lt * 128 : lt * 128 + 128],
-            stage_sem.at[1 + lt],
-        )
-        for lt in range(8)
-    ]
-    for copy in stage_out:
-        copy.start()
     carry = (position, [zero, zero, zero], jnp.zeros((RX, 128), f32), normals)
     position, speed, bias, _ = lax.fori_loop(0, GN_MAX, gn_step, carry)
     r = lax.axis_index("rx")
@@ -569,10 +574,10 @@
             jax.ShapeDtypeStruct((1, RX), f32),
             jax.ShapeDtypeStruct((4, 16, 2, LAG_COUNT), f32),
         ),
-        in_specs=[vmem, vmem, any_spec],
+        in_specs=[vmem, pl.BlockSpec(memory_space=pltpu.HBM), any_spec],
         out_specs=(vmem, vmem, vmem, any_spec),
         scratch_shapes=[
-            pltpu.VMEM((4, 16, 8, 2, 128), f32),
+            pltpu.VMEM((3, RX), f32),
             pltpu.SemaphoreType.DMA((9,)),
             pltpu.VMEM(block, f32),
             pltpu.VMEM(block, f32),
@@ -583,6 +588,7 @@
             pltpu.VMEM(block, f32),
             pltpu.VMEM((3,) + block, f32),
         ],
+        compiler_params=pltpu.CompilerParams(vmem_limit_bytes=12 << 20),
         name="solve",
     )(table, receiver_pos, amb)
 

time: 47.7 us -> 46.8 us (0.981)
  Pallas kernels: 46.9 us -> 45.3 us
  local copies, waits for them, and re-layouts: 0 us -> 0.68 us
    pallas_call x1, Pallas kernels: 7.48 us -> 6.21 us  [solve(): pl.pallas_call(solve_kernel, out_shape=(jax.ShapeDtypeStruct((3, 4), f32)...]
    unnamed x0 -> x2, local copies, waits for them, and re-layouts: none -> 0.68 us
where the time goes in v3:
time: 46.8 us; the launch traced here: 46.6 us
  Pallas kernels  45.3 us (97%)
  local copies, waits for them, and re-layouts  0.68 us (1%)
  between operations  0.65 us (1%)
    pallas_call x1, Pallas kernels, front(): pl.pallas_call(front_kernel, out_shape=(pltpu.VMEM((4, TB, 32, 128), f32)...  39.1 us
    pallas_call x1, Pallas kernels, solve(): pl.pallas_call(solve_kernel, out_shape=(jax.ShapeDtypeStruct((3, 4), f32)...  6.21 us

profile of v3, /device:TPU:1, one launch (start us, length us, event | category | flops | bytes accessed | tf_op | source)
XLA Modules:
  0.0 46.6 jit_solution(10807589709886783571)
XLA Ops:
  0.6 39.1 %front.1 = (f32[4,8,32,128]{3,2,1,0:T(8,128)S(1)}, f32[8,2,32,1,128]{4,3,2,1,0:T(1,128)S(1)}) custom-call(bf16[1,2,1024]{2,1,0:T(2,128)(2,1)} %raw_in.1, f32[1,4]{1,0:T(1,128)} %scl_in.1, s32[16,16]{1,0:T(8,128)} %lag_in.1, s32[16,16]{1,0:T(8,128)} %dop_in.1, s32[2,16]{1,0:T(2,128)} %bitcast.7, s32[2,16]{1,0:T(2,128)} %em_in.1, f32[3,4]{1,0:T(4,128)} %start_in.1, ...), custom_call_target="tpu_custom_call" | custom-call | tf_op jit(solution)/shard_map/front/pallas_call | solution.py:344
  39.7 0.0 copy-start
  39.7 0.7 %copy-done = f32[3,32]{1,0:T(4,128)S(1)} copy-done((f32[3,32]{1,0:T(4,128)S(1)}, f32[3,32]{1,0:T(4,128)}, u32[]{:S(2)}) %copy-start) | copy-done | bytes 408
  40.4 6.2 %solve.1 = (f32[3,4]{1,0:T(4,128)}, f32[3,4]{1,0:T(4,128)}, f32[1,32]{1,0:T(1,128)}, f32[4,16,2,1024]{3,2,1,0:T(2,128)}) custom-call(f32[8,2,32,128]{3,2,1,0:T(8,128)S(1)} %bitcast.6, f32[3,32]{1,0:T(4,128)S(1)} %copy-done, f32[4,16,8,2,128]{4,3,2,1,0:T(2,128)S(1)} %bitcast.5), custom_call_target="tpu_custom_call" | custom-call | tf_op jit(solution)/shard_map/solve/pallas_call | solution.py:569
Async XLA Ops:
  39.7 0.7 %copy-start = (f32[3,32]{1,0:T(4,128)S(1)}, f32[3,32]{1,0:T(4,128)}, u32[]{:S(2)}) copy-start(f32[3,32]{1,0:T(4,128)} %rpos_in.1) | copy-start | bytes 1156

commit v4 on v3

--- a/solution.py
+++ b/solution.py
@@ -41,6 +41,7 @@
         np.arange(DOPPLER_BINS)[:, None] * np.arange(DOPPLER_BINS)[None, :] % DOPPLER_BINS
     ) * (2.0 * np.pi / DOPPLER_BINS)
     mix = np.block([[np.cos(d_m), np.sin(d_m)], [-np.sin(d_m), np.cos(d_m)]])
+    mix = mix.reshape(2, DOPPLER_BINS, -1).transpose(1, 0, 2).reshape(2 * DOPPLER_BINS, -1)
     mix = mix / (FFT * math.sqrt(SAMPLES))
     return split_pair(forward) + split_pair(backward) + (mix.astype(np.float32),)
 
@@ -73,8 +74,8 @@
 
 def front_kernel(
     raw_in, scl_in, lag_in, dop_in, own_in, em_in, start_in, steps_in,
-    fhi_in, flo_in, bhi_in, blo_in, mix_in,
-    amb, table,
+    fhi_in, flo_in, bhi_in, blo_in, mix_in, rpos_in,
+    amb, table, rpos_out,
     raw_ref, scl_ref, lag_ref, dop_ref, own_ref, em_ref, start_ref, steps_ref,
     fhi_ref, flo_ref, bhi_ref, blo_ref, mix_ref,
     block_ref, raw_all, scl_all, re_ref, im_ref, rr_ref, surf_ref, pay_ref,
@@ -110,6 +111,8 @@
     ]
     for copy in loads:
         copy.start()
+    rpos_copy = pltpu.make_async_copy(rpos_in, rpos_out, own_sem.at[2])
+    rpos_copy.start()
     for copy in loads[:2]:
         copy.wait()
     own_raw = raw_ref[0].astype(f32)
@@ -205,6 +208,16 @@
             row = (c * 4 + j) * 32
             rr_ref[row : row + 32, :] = near_re * far_re + near_im * far_im
             rr_ref[256 + row : 288 + row, :] = near_im * far_re - near_re * far_im
+    own_code.wait()
+    for q, _ in rows:
+        remote(
+            pay_ref.at[1], table.at[b, 1, q], code_send.at[0], code_recv.at[q], rows[0]
+        ).wait_recv()
+    for n, peer in enumerate(blocks):
+        sends.append(
+            remote(table.at[b, 1], table.at[b, 1], cfwd_send.at[n], cfwd_recv.at[b], peer)
+        )
+        sends[-1].start()
     cross = rr_ref[...]
     high = cross.astype(bf16)
     low = (cross - high.astype(f32)).astype(bf16)
@@ -227,10 +240,10 @@
         stacked = jnp.concatenate([top, low_half], axis=0)
         surf = jnp.dot(mix_ref[...], stacked, precision=highest, preferred_element_type=f32)
         surfs.append(surf)
-        power = surf[0:32] * surf[0:32] + surf[32:64] * surf[32:64]
+        power = surf * surf
         lag0 = to_column(lag_rows[c : c + 1, :], 16)
         dop0 = to_column(dop_rows[c : c + 1, :], 16)
-        offset = iota((16, DOPPLER_BINS), 1).astype(f32) - dop0
+        offset = (iota((16, 2 * DOPPLER_BINS), 1) // 2).astype(f32) - dop0
         offset = jnp.where(offset < 0.0, offset + DOPPLER_BINS, offset)
         inside = jnp.where(offset < WD, 1.0, 0.0).astype(f32)
         weights = jnp.concatenate([inside, inside * offset], axis=0)
@@ -259,44 +272,17 @@
             remote(pay_ref.at[0], table.at[b, 0, r], pay_send.at[n], pay_recv.at[r], peer)
         )
         sends[-1].start()
-    own_code.wait()
-    for q, _ in rows:
-        remote(
-            pay_ref.at[1], table.at[b, 1, q], code_send.at[0], code_recv.at[q], rows[0]
-        ).wait_recv()
+    for t in range(TB):
+        surf_ref[t] = jnp.concatenate(
+            [surfs[0][8 * t : 8 * t + 8], surfs[1][8 * t : 8 * t + 8]], axis=0
+        ).astype(bf16)
+    own_surf = pltpu.make_async_copy(surf_ref.at[b], amb.at[b], own_sem.at[1])
+    own_surf.start()
     for n, peer in enumerate(blocks):
         sends.append(
-            remote(table.at[b, 1], table.at[b, 1], cfwd_send.at[n], cfwd_recv.at[b], peer)
+            remote(surf_ref.at[peer[1]], amb.at[b], surf_send.at[n], surf_recv.at[b], peer)
         )
         sends[-1].start()
-    for c in range(2):
-        for comp in range(2):
-            for lt in range(8):
-                surf_ref[pl.ds(c * 16 + lt * 2 + comp, 32, stride=32), :] = surfs[c][
-                    comp * 32 : comp * 32 + 32, lt * 128 : lt * 128 + 128
-                ]
-    locals_ = []
-    for d in range(4):
-        locals_.append(
-            pltpu.make_async_copy(
-                surf_ref.at[pl.ds(pl.multiple_of(128 * b + 32 * d, 32), 32), :],
-                amb.at[d, b],
-                own_sem.at[1 + d],
-            )
-        )
-        locals_[-1].start()
-    for n, peer in enumerate(blocks):
-        for d in range(4):
-            sends.append(
-                remote(
-                    surf_ref.at[pl.ds(pl.multiple_of(128 * peer[1] + 32 * d, 32), 32), :],
-                    amb.at[d, b],
-                    surf_send.at[n, d],
-                    surf_recv.at[b, d],
-                    peer,
-                )
-            )
-            sends[-1].start()
     own_pay.wait()
     plane = r // 4
     spot = lax.rem(r, 4)
@@ -322,21 +308,16 @@
         for z in range(8):
             chunk = table.at[t, 0, pl.ds(z * 4, 4)]
             remote(chunk, chunk, fwd_send.at[0, 0], fwd_recv.at[t, z], blocks[0]).wait_recv()
-        for d in range(4):
-            remote(
-                surf_ref.at[pl.ds(0, 32), :],
-                amb.at[d, t],
-                surf_send.at[0, 0],
-                surf_recv.at[t, d],
-                blocks[0],
-            ).wait_recv()
-    for copy in locals_:
-        copy.wait()
+        remote(
+            surf_ref.at[t], amb.at[t], surf_send.at[0], surf_recv.at[t], blocks[0]
+        ).wait_recv()
+    own_surf.wait()
+    rpos_copy.wait()
     for copy in sends:
         copy.wait_send()
 
 
-def front(raw, scl, lag, dop, own, em, start, steps, consts):
+def front(raw, scl, lag, dop, own, em, start, steps, consts, rpos):
     any_spec = pl.BlockSpec(memory_space=pl.ANY)
     dma = pltpu.SemaphoreType.DMA
     operands = (raw, scl, lag, dop, own, em, start, steps, *consts)
@@ -344,11 +325,12 @@
     return pl.pallas_call(
         front_kernel,
         out_shape=(
-            pltpu.VMEM((4, TB, 32, 128), f32),
+            pltpu.VMEM((TB, 16, LAG_COUNT), bf16),
             pltpu.VMEM((TB, 2, RX, 1, 128), f32),
+            pltpu.VMEM(rpos.shape, f32),
         ),
-        in_specs=[any_spec] * len(operands),
-        out_specs=(any_spec, any_spec),
+        in_specs=[any_spec] * (len(operands) + 1),
+        out_specs=(any_spec, any_spec, any_spec),
         scratch_shapes=[pltpu.VMEM(x.shape, x.dtype) for x in operands]
         + [
             pltpu.VMEM((8, SEG), bf16),
@@ -357,17 +339,17 @@
             pltpu.VMEM((3, 40, FFT), f32),
             pltpu.VMEM((3, 40, FFT), f32),
             pltpu.VMEM((512, FFT), f32),
-            pltpu.VMEM((1024, 128), f32),
+            pltpu.VMEM((TB, 16, LAG_COUNT), bf16),
             pltpu.VMEM((2, 1, 128), f32),
             dma((len(operands),)),
             dma((n,)), dma((3 * TB,)), dma((n,)), dma((3 * TB,)),
             dma((RX - 1,)), dma((RX,)), dma((TB - 1,)), dma((TB,)),
             dma((RX - 1,)), dma((RX,)), dma((TB - 1, 8)), dma((TB, 8)),
-            dma((TB - 1, 4)), dma((TB, 4)), dma((6,)),
+            dma((TB - 1,)), dma((TB,)), dma((6,)),
         ],
         compiler_params=pltpu.CompilerParams(collective_id=0, has_side_effects=True),
         name="front",
-    )(*operands)
+    )(*operands, rpos)
 
 
 def solve_three(normals, rhs, damp_term):
@@ -395,21 +377,17 @@
 
 
 def solve_kernel(
-    table_ref, rpos_in, amb_in, pos_ref, vel_ref, bias_ref, amb_out,
-    rpos_ref, stage_sem, tau_ref, nu_ref, mask_ref, late_ref, fst_ref, snd_ref, spread_ref, jac_ref,
+    table_ref, rpos_ref, amb_in, pos_ref, vel_ref, bias_ref, amb_out,
+    stage_ref, stage_sem, tau_ref, nu_ref, mask_ref, late_ref, fst_ref, snd_ref, spread_ref, jac_ref,
 ):
-    stage_out = [
-        pltpu.make_async_copy(
-            amb_in.at[:, :, lt],
-            amb_out.at[:, :, :, lt * 128 : lt * 128 + 128],
-            stage_sem.at[lt],
-        )
-        for lt in range(8)
-    ]
-    rpos_copy = pltpu.make_async_copy(rpos_in, rpos_ref, stage_sem.at[8])
-    rpos_copy.start()
-    for copy in stage_out:
-        copy.start()
+    for t in range(TB):
+        value = amb_in[t].astype(f32)
+        for c in range(2):
+            for d in range(4):
+                row = 8 * c + 2 * d
+                stage_ref[d, 2 * t + c] = value[row : row + 2, :]
+    stage_out = pltpu.make_async_copy(stage_ref, amb_out, stage_sem.at[0])
+    stage_out.start()
     lane = iota((RX, 128), 1)
     low = lane < 64
     own_lane = iota((RX, 128), 0) == lax.rem(lane, RX)
@@ -443,7 +421,6 @@
         far_half = jnp.where(late, per_receiver(x, 2 * k + 10), per_receiver(x, 2 * k + 9))
         return jnp.where(low, near_half, far_half)
 
-    rpos_copy.wait()
     eye = iota((RX, RX), 0) == iota((RX, RX), 1)
     for comp in range(3):
         column = jnp.sum(
@@ -558,8 +535,7 @@
             out[i : i + 1, :] = row[:, 0:4]
     bias_row = jnp.sum(jnp.where(iota((RX, 128), 0) == lane, bias, 0.0), axis=0, keepdims=True)
     bias_ref[...] = bias_row[:, 0:RX]
-    for copy in stage_out:
-        copy.wait()
+    stage_out.wait()
 
 
 def solve(table, receiver_pos, amb):
@@ -574,11 +550,11 @@
             jax.ShapeDtypeStruct((1, RX), f32),
             jax.ShapeDtypeStruct((4, 16, 2, LAG_COUNT), f32),
         ),
-        in_specs=[vmem, pl.BlockSpec(memory_space=pltpu.HBM), any_spec],
+        in_specs=[vmem, vmem, vmem],
         out_specs=(vmem, vmem, vmem, any_spec),
         scratch_shapes=[
-            pltpu.VMEM((3, RX), f32),
-            pltpu.SemaphoreType.DMA((9,)),
+            pltpu.VMEM((4, 16, 2, LAG_COUNT), f32),
+            pltpu.SemaphoreType.DMA((1,)),
             pltpu.VMEM(block, f32),
             pltpu.VMEM(block, f32),
             pltpu.VMEM((4,) + block, f32),
@@ -597,12 +573,13 @@
     consts, raw_samples, block_scales, lag_window_start, doppler_window_start,
     peak_owner, peak_emitter, gn_steps, receiver_pos, emitter_start,
 ):
-    amb, table = front(
+    amb, table, rpos = front(
         raw_samples, block_scales, lag_window_start, doppler_window_start,
         peak_owner.reshape(2, 16), peak_emitter, emitter_start, gn_steps.reshape(1, 4), consts,
+        receiver_pos,
     )
     position, speed, bias, amb = solve(
-        table.reshape(TB, 2, RX, 128), receiver_pos, amb.reshape(4, 16, 8, 2, 128)
+        table.reshape(TB, 2, RX, 128), rpos, amb
     )
     return amb, position, speed, bias.reshape(RX)
 

time: 46.8 us -> 45.4 us (0.970)
  Pallas kernels: 45.3 us -> 44.6 us
  local copies, waits for them, and re-layouts: 0.68 us -> 0 us
    unnamed x2 -> x0, local copies, waits for them, and re-layouts: 0.68 us -> none
    pallas_call x1, Pallas kernels: 39.1 us -> 38.6 us  [front(): pl.pallas_call(front_kernel, out_shape=(pltpu.VMEM((TB, 16, LAG_COUNT), b...]
where the time goes in v4:
time: 45.4 us; the launch traced here: 45.3 us
  Pallas kernels  44.6 us (98%)
  between operations  0.64 us (1%)
    pallas_call x1, Pallas kernels, front(): pl.pallas_call(front_kernel, out_shape=(pltpu.VMEM((TB, 16, LAG_COUNT), b...  38.6 us
    pallas_call x1, Pallas kernels, solve(): pl.pallas_call(solve_kernel, out_shape=(jax.ShapeDtypeStruct((3, 4), f32)...  6.09 us

profile of v4, /device:TPU:1, one launch (start us, length us, event | category | flops | bytes accessed | tf_op | source)
XLA Modules:
  0.0 45.3 jit_solution(9631315345385610093)
XLA Ops:
  0.6 38.6 %front.1 = (bf16[8,16,1024]{2,1,0:T(8,128)(2,1)S(1)}, f32[8,2,32,1,128]{4,3,2,1,0:T(1,128)S(1)}, f32[3,32]{1,0:T(4,128)S(1)}) custom-call(bf16[1,2,1024]{2,1,0:T(2,128)(2,1)} %raw_in.1, f32[1,4]{1,0:T(1,128)} %scl_in.1, s32[16,16]{1,0:T(8,128)} %lag_in.1, s32[16,16]{1,0:T(8,128)} %dop_in.1, s32[2,16]{1,0:T(2,128)} %bitcast.5, s32[2,16]{1,0:T(2,128)} %em_in.1, ...), custom_call_target="tpu_custom_call" | custom-call | tf_op jit(solution)/shard_map/front/pallas_call | solution.py:325
  39.2 6.1 %solve.1 = (f32[3,4]{1,0:T(4,128)}, f32[3,4]{1,0:T(4,128)}, f32[1,32]{1,0:T(1,128)}, f32[4,16,2,1024]{3,2,1,0:T(2,128)}) custom-call(f32[8,2,32,128]{3,2,1,0:T(8,128)S(1)} %bitcast.4, f32[3,32]{1,0:T(4,128)S(1)} %get-tuple-element.12.rpos_ref, bf16[8,16,1024]{2,1,0:T(8,128)(2,1)S(1)} %get-tuple-element.13.amb_in), custom_call_target="tpu_custom_call" | custom-call | tf_op jit(solution)/shard_map/solve/pallas_call | solution.py:545

commit v5 on v4

--- a/solution.py
+++ b/solution.py
@@ -23,7 +23,6 @@
 MESH = pl.DeviceIdType.MESH
 f32 = jnp.float32
 bf16 = jnp.bfloat16
-highest = lax.Precision.HIGHEST
 
 
 def split_pair(table):
@@ -43,7 +42,9 @@
     mix = np.block([[np.cos(d_m), np.sin(d_m)], [-np.sin(d_m), np.cos(d_m)]])
     mix = mix.reshape(2, DOPPLER_BINS, -1).transpose(1, 0, 2).reshape(2 * DOPPLER_BINS, -1)
     mix = mix / (FFT * math.sqrt(SAMPLES))
-    return split_pair(forward) + split_pair(backward) + (mix.astype(np.float32),)
+    mix_high, mix_low = split_pair(mix)
+    deep_mix = np.concatenate([mix_high, mix_low, mix_high], axis=1)
+    return split_pair(forward) + split_pair(backward) + (deep_mix,)
 
 
 def iota(shape, dim):
@@ -238,7 +239,10 @@
             [lag_im[(c * 4 + j) * 32 : (c * 4 + j + 1) * 32] for j in range(4)], axis=1
         )
         stacked = jnp.concatenate([top, low_half], axis=0)
-        surf = jnp.dot(mix_ref[...], stacked, precision=highest, preferred_element_type=f32)
+        high = stacked.astype(bf16)
+        low = (stacked - high.astype(f32)).astype(bf16)
+        deep = jnp.concatenate([high, high, low], axis=0)
+        surf = jnp.dot(mix_ref[...], deep, preferred_element_type=f32)
         surfs.append(surf)
         power = surf * surf
         lag0 = to_column(lag_rows[c : c + 1, :], 16)
@@ -247,7 +251,14 @@
         offset = jnp.where(offset < 0.0, offset + DOPPLER_BINS, offset)
         inside = jnp.where(offset < WD, 1.0, 0.0).astype(f32)
         weights = jnp.concatenate([inside, inside * offset], axis=0)
-        sums = jnp.dot(weights, power, precision=highest, preferred_element_type=f32)
+        weights = weights.astype(bf16)
+        high = power.astype(bf16)
+        low = (power - high.astype(f32)).astype(bf16)
+        sums = jnp.dot(
+            jnp.concatenate([weights, weights], axis=1),
+            jnp.concatenate([high, low], axis=0),
+            preferred_element_type=f32,
+        )
         step = iota((16, LAG_COUNT), 1).astype(f32) - lag0
         within = (step >= 0.0) & (step < WL)
         plain = jnp.where(within, sums[0:16], 0.0)
@@ -284,18 +295,21 @@
         )
         sends[-1].start()
     own_pay.wait()
-    plane = r // 4
-    spot = lax.rem(r, 4)
-    for count, dz in enumerate((0, 1, 7, 2, 6, 3, 5, 4)):
-        there = lax.rem(plane + dz, 8)
-        for dx in range(4):
-            if dz == 0 and dx == 0:
+    for copy in sends[: -len(blocks)]:
+        copy.wait_send()
+    sends = sends[-len(blocks) :]
+    part = r // 8
+    spot = lax.rem(r, 8)
+    for count, dp in enumerate((0, 1, 3, 2)):
+        there = lax.rem(part + dp, 4)
+        for dx in range(8):
+            if dp == 0 and dx == 0:
                 continue
-            q = there * 4 + lax.rem(spot + dx, 4)
+            q = there * 8 + lax.rem(spot + dx, 8)
             remote(
                 pay_ref.at[0], table.at[b, 0, q], pay_send.at[0], pay_recv.at[q], rows[0]
             ).wait_recv()
-        chunk = table.at[b, 0, pl.ds(there * 4, 4)]
+        chunk = table.at[b, 0, pl.ds(there * 8, 8)]
         for n, peer in enumerate(blocks):
             sends.append(
                 remote(chunk, chunk, fwd_send.at[n, count], fwd_recv.at[b, there], peer)
@@ -305,8 +319,8 @@
         remote(
             table.at[t, 1], table.at[t, 1], cfwd_send.at[0], cfwd_recv.at[t], blocks[0]
         ).wait_recv()
-        for z in range(8):
-            chunk = table.at[t, 0, pl.ds(z * 4, 4)]
+        for z in range(4):
+            chunk = table.at[t, 0, pl.ds(z * 8, 8)]
             remote(chunk, chunk, fwd_send.at[0, 0], fwd_recv.at[t, z], blocks[0]).wait_recv()
         remote(
             surf_ref.at[t], amb.at[t], surf_send.at[0], surf_recv.at[t], blocks[0]
@@ -344,7 +358,7 @@
             dma((len(operands),)),
             dma((n,)), dma((3 * TB,)), dma((n,)), dma((3 * TB,)),
             dma((RX - 1,)), dma((RX,)), dma((TB - 1,)), dma((TB,)),
-            dma((RX - 1,)), dma((RX,)), dma((TB - 1, 8)), dma((TB, 8)),
+            dma((RX - 1,)), dma((RX,)), dma((TB - 1, 4)), dma((TB, 4)),
             dma((TB - 1,)), dma((TB,)), dma((6,)),
         ],
         compiler_params=pltpu.CompilerParams(collective_id=0, has_side_effects=True),

time: 45.4 us -> 43.5 us (0.958)
  Pallas kernels: 44.6 us -> 42.7 us
    pallas_call x1, Pallas kernels: 38.6 us -> 36.6 us  [front(): pl.pallas_call(front_kernel, out_shape=(pltpu.VMEM((TB, 16, LAG_COUNT), b...]
where the time goes in v5:
time: 43.5 us; the launch traced here: 43.4 us
  Pallas kernels  42.7 us (98%)
  between operations  0.64 us (1%)
    pallas_call x1, Pallas kernels, front(): pl.pallas_call(front_kernel, out_shape=(pltpu.VMEM((TB, 16, LAG_COUNT), b...  36.6 us
    pallas_call x1, Pallas kernels, solve(): pl.pallas_call(solve_kernel, out_shape=(jax.ShapeDtypeStruct((3, 4), f32)...  6.09 us

profile of v5, /device:TPU:1, one launch (start us, length us, event | category | flops | bytes accessed | tf_op | source)
XLA Modules:
  0.0 43.4 jit_solution(8167348473001400779)
XLA Ops:
  0.6 36.6 %front.1 = (bf16[8,16,1024]{2,1,0:T(8,128)(2,1)S(1)}, f32[8,2,32,1,128]{4,3,2,1,0:T(1,128)S(1)}, f32[3,32]{1,0:T(4,128)S(1)}) custom-call(bf16[1,2,1024]{2,1,0:T(2,128)(2,1)} %raw_in.1, f32[1,4]{1,0:T(1,128)} %scl_in.1, s32[16,16]{1,0:T(8,128)} %lag_in.1, s32[16,16]{1,0:T(8,128)} %dop_in.1, s32[2,16]{1,0:T(2,128)} %bitcast.5, s32[2,16]{1,0:T(2,128)} %em_in.1, ...), custom_call_target="tpu_custom_call" | custom-call | tf_op jit(solution)/shard_map/front/pallas_call | solution.py:339
  37.3 6.1 %solve.1 = (f32[3,4]{1,0:T(4,128)}, f32[3,4]{1,0:T(4,128)}, f32[1,32]{1,0:T(1,128)}, f32[4,16,2,1024]{3,2,1,0:T(2,128)}) custom-call(f32[8,2,32,128]{3,2,1,0:T(8,128)S(1)} %bitcast.4, f32[3,32]{1,0:T(4,128)S(1)} %get-tuple-element.12.rpos_ref, bf16[8,16,1024]{2,1,0:T(8,128)(2,1)S(1)} %get-tuple-element.13.amb_in), custom_call_target="tpu_custom_call" | custom-call | tf_op jit(solution)/shard_map/solve/pallas_call | solution.py:559

commit v6 on v5

--- a/solution.py
+++ b/solution.py
@@ -76,10 +76,11 @@
 def front_kernel(
     raw_in, scl_in, lag_in, dop_in, own_in, em_in, start_in, steps_in,
     fhi_in, flo_in, bhi_in, blo_in, mix_in, rpos_in,
-    amb, table, rpos_out,
+    amb, table, prep, small,
     raw_ref, scl_ref, lag_ref, dop_ref, own_ref, em_ref, start_ref, steps_ref,
     fhi_ref, flo_ref, bhi_ref, blo_ref, mix_ref,
-    block_ref, raw_all, scl_all, re_ref, im_ref, rr_ref, surf_ref, pay_ref,
+    rpos_ref, block_ref, raw_all, scl_all, re_ref, im_ref, rr_ref, surf_ref, pay_ref,
+    code_tab, code_ref, prep_ref, small_ref, land_ref, wide_ref,
     load_sem, raw_send, raw_recv, scl_send, scl_recv, code_send, code_recv,
     cfwd_send, cfwd_recv, pay_send, pay_recv, fwd_send, fwd_recv, surf_send, surf_recv, own_sem,
 ):
@@ -112,7 +113,7 @@
     ]
     for copy in loads:
         copy.start()
-    rpos_copy = pltpu.make_async_copy(rpos_in, rpos_out, own_sem.at[2])
+    rpos_copy = pltpu.make_async_copy(rpos_in, rpos_ref, own_sem.at[2])
     rpos_copy.start()
     for copy in loads[:2]:
         copy.wait()
@@ -163,11 +164,11 @@
     for e in range(4):
         codes = jnp.where(lane1 == 76 + e, steps_ref[0:1, e : e + 1].astype(f32), codes)
     pay_ref[1] = codes
-    own_code = pltpu.make_async_copy(pay_ref.at[1], table.at[b, 1, r], own_sem.at[5])
+    own_code = pltpu.make_async_copy(pay_ref.at[1], code_tab.at[b, r], own_sem.at[5])
     own_code.start()
     for n, peer in enumerate(rows):
         sends.append(
-            remote(pay_ref.at[1], table.at[b, 1, r], code_send.at[n], code_recv.at[r], peer)
+            remote(pay_ref.at[1], code_tab.at[b, r], code_send.at[n], code_recv.at[r], peer)
         )
         sends[-1].start()
 
@@ -212,11 +213,11 @@
     own_code.wait()
     for q, _ in rows:
         remote(
-            pay_ref.at[1], table.at[b, 1, q], code_send.at[0], code_recv.at[q], rows[0]
+            pay_ref.at[1], code_tab.at[b, q], code_send.at[0], code_recv.at[q], rows[0]
         ).wait_recv()
     for n, peer in enumerate(blocks):
         sends.append(
-            remote(table.at[b, 1], table.at[b, 1], cfwd_send.at[n], cfwd_recv.at[b], peer)
+            remote(code_tab.at[b], code_tab.at[b], cfwd_send.at[n], cfwd_recv.at[b], peer)
         )
         sends[-1].start()
     cross = rr_ref[...]
@@ -276,28 +277,44 @@
         jnp.where(placed, jnp.where(first, tau, nu), 0.0), axis=0, keepdims=True
     )
 
-    own_pay = pltpu.make_async_copy(pay_ref.at[0], table.at[b, 0, r], own_sem.at[0])
+    own_pay = pltpu.make_async_copy(pay_ref.at[0], table.at[b, r], own_sem.at[0])
     own_pay.start()
     for n, peer in enumerate(rows):
         sends.append(
-            remote(pay_ref.at[0], table.at[b, 0, r], pay_send.at[n], pay_recv.at[r], peer)
+            remote(pay_ref.at[0], table.at[b, r], pay_send.at[n], pay_recv.at[r], peer)
         )
         sends[-1].start()
     for t in range(TB):
         surf_ref[t] = jnp.concatenate(
             [surfs[0][8 * t : 8 * t + 8], surfs[1][8 * t : 8 * t + 8]], axis=0
         ).astype(bf16)
-    own_surf = pltpu.make_async_copy(surf_ref.at[b], amb.at[b], own_sem.at[1])
+    own_surf = pltpu.make_async_copy(surf_ref.at[b], land_ref.at[b], own_sem.at[1])
     own_surf.start()
     for n, peer in enumerate(blocks):
         sends.append(
-            remote(surf_ref.at[peer[1]], amb.at[b], surf_send.at[n], surf_recv.at[b], peer)
+            remote(surf_ref.at[peer[1]], land_ref.at[b], surf_send.at[n], surf_recv.at[b], peer)
         )
         sends[-1].start()
     own_pay.wait()
     for copy in sends[: -len(blocks)]:
         copy.wait_send()
     sends = sends[-len(blocks) :]
+    for _, t in blocks:
+        remote(
+            code_tab.at[t], code_tab.at[t], cfwd_send.at[0], cfwd_recv.at[t], blocks[0]
+        ).wait_recv()
+    rpos_copy.wait()
+    for k in range(TB):
+        for q in range(RX):
+            code_ref[k, q : q + 1, :] = code_tab[k, q]
+    prepare(code_ref, rpos_ref, prep_ref, small_ref)
+    outs = [
+        pltpu.make_async_copy(prep_ref, prep, own_sem.at[2]),
+        pltpu.make_async_copy(small_ref, small, own_sem.at[3]),
+        pltpu.make_async_copy(wide_ref, amb, own_sem.at[4]),
+    ]
+    outs[0].start()
+    outs[1].start()
     part = r // 8
     spot = lax.rem(r, 8)
     for count, dp in enumerate((0, 1, 3, 2)):
@@ -307,26 +324,32 @@
                 continue
             q = there * 8 + lax.rem(spot + dx, 8)
             remote(
-                pay_ref.at[0], table.at[b, 0, q], pay_send.at[0], pay_recv.at[q], rows[0]
+                pay_ref.at[0], table.at[b, q], pay_send.at[0], pay_recv.at[q], rows[0]
             ).wait_recv()
-        chunk = table.at[b, 0, pl.ds(there * 8, 8)]
+        chunk = table.at[b, pl.ds(there * 8, 8)]
         for n, peer in enumerate(blocks):
             sends.append(
                 remote(chunk, chunk, fwd_send.at[n, count], fwd_recv.at[b, there], peer)
             )
             sends[-1].start()
+    own_surf.wait()
     for _, t in blocks:
         remote(
-            table.at[t, 1], table.at[t, 1], cfwd_send.at[0], cfwd_recv.at[t], blocks[0]
+            surf_ref.at[t], land_ref.at[t], surf_send.at[0], surf_recv.at[t], blocks[0]
         ).wait_recv()
+    for t in range(TB):
+        value = land_ref[t].astype(f32)
+        for c in range(2):
+            for d in range(4):
+                row = 8 * c + 2 * d
+                wide_ref[d, 2 * t + c] = value[row : row + 2, :]
+    outs[2].start()
+    for _, t in blocks:
         for z in range(4):
-            chunk = table.at[t, 0, pl.ds(z * 8, 8)]
+            chunk = table.at[t, pl.ds(z * 8, 8)]
             remote(chunk, chunk, fwd_send.at[0, 0], fwd_recv.at[t, z], blocks[0]).wait_recv()
-        remote(
-            surf_ref.at[t], amb.at[t], surf_send.at[0], surf_recv.at[t], blocks[0]
-        ).wait_recv()
-    own_surf.wait()
-    rpos_copy.wait()
+    for copy in outs:
+        copy.wait()
     for copy in sends:
         copy.wait_send()
 
@@ -339,14 +362,16 @@
     return pl.pallas_call(
         front_kernel,
         out_shape=(
-            pltpu.VMEM((TB, 16, LAG_COUNT), bf16),
-            pltpu.VMEM((TB, 2, RX, 1, 128), f32),
-            pltpu.VMEM(rpos.shape, f32),
+            pltpu.VMEM((4, 16, 2, LAG_COUNT), f32),
+            pltpu.VMEM((TB, RX, 1, 128), f32),
+            pltpu.VMEM((51, RX, 128), f32),
+            pltpu.VMEM((11, 8, 128), f32),
         ),
         in_specs=[any_spec] * (len(operands) + 1),
-        out_specs=(any_spec, any_spec, any_spec),
+        out_specs=(any_spec,) * 4,
         scratch_shapes=[pltpu.VMEM(x.shape, x.dtype) for x in operands]
         + [
+            pltpu.VMEM(rpos.shape, f32),
             pltpu.VMEM((8, SEG), bf16),
             pltpu.VMEM((3 * TB, 8, SEG), bf16),
             pltpu.VMEM((3 * TB,) + scl.shape, f32),
@@ -355,6 +380,12 @@
             pltpu.VMEM((512, FFT), f32),
             pltpu.VMEM((TB, 16, LAG_COUNT), bf16),
             pltpu.VMEM((2, 1, 128), f32),
+            pltpu.VMEM((TB, RX, 1, 128), f32),
+            pltpu.VMEM((TB, RX, 128), f32),
+            pltpu.VMEM((51, RX, 128), f32),
+            pltpu.VMEM((11, 8, 128), f32),
+            pltpu.VMEM((TB, 16, LAG_COUNT), bf16),
+            pltpu.VMEM((4, 16, 2, LAG_COUNT), f32),
             dma((len(operands),)),
             dma((n,)), dma((3 * TB,)), dma((n,)), dma((3 * TB,)),
             dma((RX - 1,)), dma((RX,)), dma((TB - 1,)), dma((TB,)),
@@ -390,136 +421,169 @@
     return pltpu.roll(x, (RX - shift) % RX, 0)
 
 
-def solve_kernel(
-    table_ref, rpos_ref, amb_in, pos_ref, vel_ref, bias_ref, amb_out,
-    stage_ref, stage_sem, tau_ref, nu_ref, mask_ref, late_ref, fst_ref, snd_ref, spread_ref, jac_ref,
-):
-    for t in range(TB):
-        value = amb_in[t].astype(f32)
-        for c in range(2):
-            for d in range(4):
-                row = 8 * c + 2 * d
-                stage_ref[d, 2 * t + c] = value[row : row + 2, :]
-    stage_out = pltpu.make_async_copy(stage_ref, amb_out, stage_sem.at[0])
-    stage_out.start()
+ROW_OF = (0, 4, 2, 6)
+OWNER_AT = (0, 0, 2, 2, 1, 1, 3, 3)
+PAIRS = ((0, 0), (0, 1), (0, 2), (1, 1), (1, 2), (2, 2))
+MASK, LATE, FIRST, SECOND, SPREAD, JAC = 0, 16, 20, 23, 35, 39
+START, STEPS, DAMP, NORMAL = 0, 3, 4, 5
+
+
+def fold(parts):
+    sub = iota((8, 128), 0)
+    upper = sub < 4
+    early = lax.rem(sub, 4) < 2
+
+    def halves(x, y):
+        return jnp.where(upper, x, y) + pltpu.roll(jnp.where(upper, y, x), 4, 0)
+
+    one = halves(parts[0], parts[1])
+    two = halves(parts[2], parts[3])
+    rows = jnp.where(early, one + pltpu.roll(one, 6, 0), two + pltpu.roll(two, 2, 0))
+    rows = rows + pltpu.roll(rows, 7, 0)
+    rows = rows + pltpu.roll(rows, 32, 1)
+    return rows + pltpu.roll(rows, 64, 1)
+
+
+def add_to(prep_ref, acc, key, k, quantity):
+    for e in range(4):
+        term = prep_ref[MASK + 4 * e + k] * quantity
+        term = (term[0:8] + term[8:16]) + (term[16:24] + term[24:32])
+        acc[key][e] = term if k == 0 else acc[key][e] + term
+
+
+def at_peaks(prep_ref, rows, k):
+    value = prep_ref[MASK + k] * rows[0:1]
+    for e in range(1, 4):
+        value = value + prep_ref[MASK + 4 * e + k] * rows[ROW_OF[e] : ROW_OF[e] + 1]
+    return value
+
+
+def second_of(x, late, k):
+    low = iota((RX, 128), 1) < 64
+    near_half = jnp.where(late, per_receiver(x, 2 * k + 2), per_receiver(x, 2 * k + 1))
+    far_half = jnp.where(late, per_receiver(x, 2 * k + 10), per_receiver(x, 2 * k + 9))
+    return jnp.where(low, near_half, far_half)
+
+
+def ranges(prep_ref, position, k):
+    sq_first = jnp.ones((RX, 128), f32)
+    sq_second = sq_first
+    firsts, seconds = [], []
+    for comp in range(3):
+        at = at_peaks(prep_ref, position[comp], k)
+        d_first = at - prep_ref[FIRST + comp]
+        d_second = at - prep_ref[SECOND + 4 * comp + k]
+        sq_first = sq_first + d_first * d_first
+        sq_second = sq_second + d_second * d_second
+        firsts.append(d_first)
+        seconds.append(d_second)
+    inv_first = lax.rsqrt(sq_first)
+    inv_second = lax.rsqrt(sq_second)
+    spread = sq_second * inv_second - sq_first * inv_first
+    return spread, [seconds[i] * inv_second - firsts[i] * inv_first for i in range(3)]
+
+
+def prepare(code_ref, rpos_ref, prep_ref, small_ref):
     lane = iota((RX, 128), 1)
     low = lane < 64
     own_lane = iota((RX, 128), 0) == lax.rem(lane, RX)
-    halves = []
     for k in range(4):
-        a0, a1 = table_ref[k, 0], table_ref[k + 4, 0]
-        tau_ref[k] = jnp.where(low, a0, pltpu.roll(a1, 64, 1))
-        nu_ref[k] = jnp.where(low, pltpu.roll(a0, 64, 1), a1)
-        code = jnp.where(low, table_ref[k, 1], pltpu.roll(table_ref[k + 4, 1], 64, 1))
+        code = jnp.where(low, code_ref[k], pltpu.roll(code_ref[k + 4], 64, 1))
         late = code > 4.5
-        late_ref[k] = jnp.where(late, 1.0, 0.0)
+        prep_ref[LATE + k] = jnp.where(late, 1.0, 0.0)
         emitter = jnp.where(late, code - 4.0, code)
         for e in range(4):
-            mask_ref[e, k] = jnp.where(emitter == e + 1.0, 1.0, 0.0)
-
-    info = table_ref[0, 1]
+            prep_ref[MASK + 4 * e + k] = jnp.where(emitter == e + 1.0, 1.0, 0.0)
+    info = code_ref[0]
 
     def owner_row(col):
         value = jnp.sum(jnp.where(lane == col, info, 0.0), axis=1, keepdims=True)
         return jnp.sum(jnp.where(own_lane, value, 0.0), axis=0, keepdims=True)
 
     def owner_rows(base):
-        return jnp.concatenate([owner_row(base + e) for e in range(4)], axis=0)
+        made = [owner_row(base + e) for e in range(4)]
+        return jnp.concatenate([made[e] for e in OWNER_AT], axis=0)
 
     position = [owner_rows(64 + 4 * k) for k in range(3)]
-    steps = owner_rows(76)
-
-    def second_of(x, k):
-        late = late_ref[k] > 0.5
-        near_half = jnp.where(late, per_receiver(x, 2 * k + 2), per_receiver(x, 2 * k + 1))
-        far_half = jnp.where(late, per_receiver(x, 2 * k + 10), per_receiver(x, 2 * k + 9))
-        return jnp.where(low, near_half, far_half)
-
+    for k in range(3):
+        small_ref[START + k] = position[k]
+    small_ref[STEPS] = owner_rows(76)
     eye = iota((RX, RX), 0) == iota((RX, RX), 1)
     for comp in range(3):
         column = jnp.sum(
             jnp.where(eye, rpos_ref[comp : comp + 1, :], 0.0), axis=1, keepdims=True
         )
         column = jnp.broadcast_to(column, (RX, 128))
-        fst_ref[comp] = column
+        prep_ref[FIRST + comp] = column
         for k in range(4):
-            snd_ref[comp, k] = second_of(column, k)
-
-    def sum_rows(parts):
-        rows = jnp.concatenate([jnp.sum(p, axis=0, keepdims=True) for p in parts], axis=0)
-        rows = rows + pltpu.roll(rows, 32, 1)
-        return rows + pltpu.roll(rows, 64, 1)
-
-    def add_to(acc, key, k, quantity):
-        for e in range(4):
-            term = mask_ref[e, k] * quantity
-            term = term[0:8] + term[8:16] + term[16:24] + term[24:32]
-            acc[key][e] = term if k == 0 else acc[key][e] + term
-
-    def at_peaks(rows, k):
-        value = mask_ref[0, k] * rows[0:1]
-        for e in range(1, 4):
-            value = value + mask_ref[e, k] * rows[e : e + 1]
-        return value
-
-    def ranges(position, k):
-        sq_first = jnp.ones((RX, 128), f32)
-        sq_second = sq_first
-        firsts, seconds = [], []
-        for comp in range(3):
-            at = at_peaks(position[comp], k)
-            d_first = at - fst_ref[comp]
-            d_second = at - snd_ref[comp, k]
-            sq_first = sq_first + d_first * d_first
-            sq_second = sq_second + d_second * d_second
-            firsts.append(d_first)
-            seconds.append(d_second)
-        inv_first = lax.rsqrt(sq_first)
-        inv_second = lax.rsqrt(sq_second)
-        spread = sq_second * inv_second - sq_first * inv_first
-        spread_ref[k] = spread
-        jac = [seconds[i] * inv_second - firsts[i] * inv_first for i in range(3)]
-        for i in range(3):
-            jac_ref[i, k] = jac[i]
-        return spread, jac
-
-    pairs = ((0, 0), (0, 1), (0, 2), (1, 1), (1, 2), (2, 2))
+            prep_ref[SECOND + 4 * comp + k] = second_of(column, prep_ref[LATE + k] > 0.5, k)
     acc = {key: [None] * 4 for key in range(7)}
     for k in range(4):
-        _, jac = ranges(position, k)
-        for key, (x, y) in enumerate(pairs):
-            add_to(acc, key, k, jac[x] * jac[y])
-        add_to(acc, 6, k, jnp.ones((RX, 128), f32))
-    normals = [sum_rows(acc[key]) for key in range(6)]
-    damp = 2.0 * (sum_rows(acc[6]) + 1.0)
-    zero = jnp.zeros((4, 128), f32)
+        spread, jac = ranges(prep_ref, position, k)
+        prep_ref[SPREAD + k] = spread
+        for i in range(3):
+            prep_ref[JAC + 4 * i + k] = jac[i]
+        for key, (x, y) in enumerate(PAIRS):
+            add_to(prep_ref, acc, key, k, jac[x] * jac[y])
+        add_to(prep_ref, acc, 6, k, jnp.ones((RX, 128), f32))
+    for key in range(6):
+        small_ref[NORMAL + key] = fold(acc[key])
+    small_ref[DAMP] = 2.0 * (fold(acc[6]) + 1.0)
+
+
+def solve_kernel(
+    table_ref, prep_ref, small_ref, amb_in, pos_ref, vel_ref, bias_ref, amb_out,
+    out_sem, tau_ref, nu_ref, spread_ref, jac_ref,
+):
+    amb_copy = pltpu.make_async_copy(amb_in, amb_out, out_sem.at[0])
+    amb_copy.start()
+    lane = iota((RX, 128), 1)
+    low = lane < 64
+    for k in range(4):
+        a0, a1 = table_ref[k], table_ref[k + 4]
+        tau_ref[k] = jnp.where(low, a0, pltpu.roll(a1, 64, 1))
+        nu_ref[k] = jnp.where(low, pltpu.roll(a0, 64, 1), a1)
+        spread_ref[k] = prep_ref[SPREAD + k]
+        for i in range(3):
+            jac_ref[i, k] = prep_ref[JAC + 4 * i + k]
+    position = [small_ref[START + k] for k in range(3)]
+    steps = small_ref[STEPS]
+    damp = small_ref[DAMP]
+    normals = [small_ref[NORMAL + key] for key in range(6)]
+    zero = jnp.zeros((8, 128), f32)
 
     def gn_step(step, carry):
         position, speed, bias, normals = carry
         moving = step.astype(f32) < steps
         acc = {key: [None] * 4 for key in range(3)}
         for k in range(4):
-            delta = second_of(bias, k) - bias
+            delta = second_of(bias, prep_ref[LATE + k] > 0.5, k) - bias
             resid = tau_ref[k] - spread_ref[k] - delta
             for i in range(3):
-                add_to(acc, i, k, jac_ref[i, k] * resid)
-        moved = solve_three(normals, [sum_rows(acc[i]) for i in range(3)], damp)
+                add_to(prep_ref, acc, i, k, jac_ref[i, k] * resid)
+        moved = solve_three(normals, [fold(acc[i]) for i in range(3)], damp)
         position = [position[i] + jnp.where(moving, moved[i], 0.0) for i in range(3)]
         acc = {key: [None] * 4 for key in range(9)}
         clock = None
         for k in range(4):
-            spread, jac = ranges(position, k)
-            for key, (x, y) in enumerate(pairs):
-                add_to(acc, key, k, jac[x] * jac[y])
+            spread, jac = ranges(prep_ref, position, k)
+            spread_ref[k] = spread
+            for i in range(3):
+                jac_ref[i, k] = jac[i]
+            for key, (x, y) in enumerate(PAIRS):
+                add_to(prep_ref, acc, key, k, jac[x] * jac[y])
             rate = nu_ref[k]
             for i in range(3):
-                rate = rate - at_peaks(speed[i], k) * jac[i]
+                rate = rate - at_peaks(prep_ref, speed[i], k) * jac[i]
             for i in range(3):
-                add_to(acc, 6 + i, k, jac[i] * rate)
-            live = mask_ref[0, k] + mask_ref[1, k] + mask_ref[2, k] + mask_ref[3, k]
-            delta = second_of(bias, k) - bias
+                add_to(prep_ref, acc, 6 + i, k, jac[i] * rate)
+            late_k = prep_ref[LATE + k]
+            live = (prep_ref[MASK + k] + prep_ref[MASK + 4 + k]) + (
+                prep_ref[MASK + 8 + k] + prep_ref[MASK + 12 + k]
+            )
+            delta = second_of(bias, late_k > 0.5, k) - bias
             cres = live * (tau_ref[k] - spread - delta)
-            late = late_ref[k] * cres
+            late = late_k * cres
             early = cres - late
             part = -cres
             for term, keep, shift in (
@@ -530,8 +594,8 @@
             ):
                 part = part + pltpu.roll(jnp.where(keep, term, 0.0), shift, 0)
             clock = part if clock is None else clock + part
-        normals = [sum_rows(acc[key]) for key in range(6)]
-        turned = solve_three(normals, [sum_rows(acc[6 + i]) for i in range(3)], damp)
+        normals = [fold(acc[key]) for key in range(6)]
+        turned = solve_three(normals, [fold(acc[6 + i]) for i in range(3)], damp)
         speed = [speed[i] + jnp.where(moving, turned[i], 0.0) for i in range(3)]
         total = jnp.sum(clock, axis=1, keepdims=True)
         bias = bias + jnp.broadcast_to(total, (RX, 128)) / (3.0 * 16 * RX)
@@ -540,19 +604,21 @@
     carry = (position, [zero, zero, zero], jnp.zeros((RX, 128), f32), normals)
     position, speed, bias, _ = lax.fori_loop(0, GN_MAX, gn_step, carry)
     r = lax.axis_index("rx")
-    lane4 = iota((4, 128), 1)
-    sub4 = iota((4, 128), 0)
+    lane8 = iota((8, 128), 1)
+    sub8 = iota((8, 128), 0)
+    spot = lax.rem(sub8, 4) + jnp.where(sub8 >= 4, 1, 0)
+    used = (lax.rem(sub8, 2) == 0) & (lane8 == spot)
     for out, value in ((pos_ref, position), (vel_ref, speed)):
         for i in range(3):
-            column = jnp.sum(jnp.where(lane4 == r, value[i], 0.0), axis=1, keepdims=True)
-            row = jnp.sum(jnp.where(lane4 == sub4, column, 0.0), axis=0, keepdims=True)
+            column = jnp.sum(jnp.where(lane8 == r, value[i], 0.0), axis=1, keepdims=True)
+            row = jnp.sum(jnp.where(used, column, 0.0), axis=0, keepdims=True)
             out[i : i + 1, :] = row[:, 0:4]
     bias_row = jnp.sum(jnp.where(iota((RX, 128), 0) == lane, bias, 0.0), axis=0, keepdims=True)
     bias_ref[...] = bias_row[:, 0:RX]
-    stage_out.wait()
-
-
-def solve(table, receiver_pos, amb):
+    amb_copy.wait()
+
+
+def solve(table, prep, small, amb):
     any_spec = pl.BlockSpec(memory_space=pl.ANY)
     vmem = pl.BlockSpec(memory_space=pltpu.VMEM)
     block = (4, RX, 128)
@@ -564,36 +630,31 @@
             jax.ShapeDtypeStruct((1, RX), f32),
             jax.ShapeDtypeStruct((4, 16, 2, LAG_COUNT), f32),
         ),
-        in_specs=[vmem, vmem, vmem],
+        in_specs=[vmem, vmem, vmem, any_spec],
         out_specs=(vmem, vmem, vmem, any_spec),
         scratch_shapes=[
-            pltpu.VMEM((4, 16, 2, LAG_COUNT), f32),
             pltpu.SemaphoreType.DMA((1,)),
             pltpu.VMEM(block, f32),
             pltpu.VMEM(block, f32),
-            pltpu.VMEM((4,) + block, f32),
-            pltpu.VMEM(block, f32),
-            pltpu.VMEM((3, RX, 128), f32),
-            pltpu.VMEM((3,) + block, f32),
             pltpu.VMEM(block, f32),
             pltpu.VMEM((3,) + block, f32),
         ],
         compiler_params=pltpu.CompilerParams(vmem_limit_bytes=12 << 20),
         name="solve",
-    )(table, receiver_pos, amb)
+    )(table, prep, small, amb)
 
 
 def local(
     consts, raw_samples, block_scales, lag_window_start, doppler_window_start,
     peak_owner, peak_emitter, gn_steps, receiver_pos, emitter_start,
 ):
-    amb, table, rpos = front(
+    amb, table, prep, small = front(
         raw_samples, block_scales, lag_window_start, doppler_window_start,
         peak_owner.reshape(2, 16), peak_emitter, emitter_start, gn_steps.reshape(1, 4), consts,
         receiver_pos,
     )
     position, speed, bias, amb = solve(
-        table.reshape(TB, 2, RX, 128), rpos, amb
+        table.reshape(TB, RX, 128), prep, small, amb
     )
     return amb, position, speed, bias.reshape(RX)
 

time: 43.5 us -> 42.8 us (0.984)
  Pallas kernels: 42.7 us -> 42.1 us
    pallas_call x1, Pallas kernels: 6.09 us -> 5.46 us  [solve(): pl.pallas_call(solve_kernel, out_shape=(jax.ShapeDtypeStruct((3, 4), f32)...]
where the time goes in v6:
time: 42.8 us; the launch traced here: 42.7 us
  Pallas kernels  42.1 us (98%)
  between operations  0.64 us (1%)
    pallas_call x1, Pallas kernels, front(): pl.pallas_call(front_kernel, out_shape=(pltpu.VMEM((4, 16, 2, LAG_COUNT),...  36.6 us
    pallas_call x1, Pallas kernels, solve(): pl.pallas_call(solve_kernel, out_shape=(jax.ShapeDtypeStruct((3, 4), f32)...  5.46 us

profile of v6, /device:TPU:1, one launch (start us, length us, event | category | flops | bytes accessed | tf_op | source)
XLA Modules:
  0.0 42.7 jit_solution(11051791373012274943)
XLA Ops:
  0.6 36.6 %front.1 = (f32[4,16,2,1024]{3,2,1,0:T(2,128)S(1)}, f32[8,32,1,128]{3,2,1,0:T(1,128)S(1)}, f32[51,32,128]{2,1,0:T(8,128)S(1)}, f32[11,8,128]{2,1,0:T(8,128)S(1)}) custom-call(bf16[1,2,1024]{2,1,0:T(2,128)(2,1)} %raw_in.1, f32[1,4]{1,0:T(1,128)} %scl_in.1, s32[16,16]{1,0:T(8,128)} %lag_in.1, s32[16,16]{1,0:T(8,128)} %dop_in.1, s32[2,16]{1,0:T(2,128)} %bitcast.5, ...), custom_call_target="tpu_custom_call" | custom-call | tf_op jit(solution)/shard_map/front/pallas_call | solution.py:362
  37.3 5.5 %solve.1 = (f32[3,4]{1,0:T(4,128)}, f32[3,4]{1,0:T(4,128)}, f32[1,32]{1,0:T(1,128)}, f32[4,16,2,1024]{3,2,1,0:T(2,128)}) custom-call(f32[8,32,128]{2,1,0:T(8,128)S(1)} %bitcast.4, f32[51,32,128]{2,1,0:T(8,128)S(1)} %get-tuple-element.13.prep_ref, f32[11,8,128]{2,1,0:T(8,128)S(1)} %get-tuple-element.14.small_ref, f32[4,16,2,1024]{3,2,1,0:T(2,128)S(1)} %get-tuple-element.15.amb_in), custom_call_target="tpu_custom_call" | custom-call | tf_op jit(solution)/shard_map/solve/pallas_call | solution.py:625

commit v7 on v6

--- a/solution.py
+++ b/solution.py
@@ -364,7 +364,7 @@
         out_shape=(
             pltpu.VMEM((4, 16, 2, LAG_COUNT), f32),
             pltpu.VMEM((TB, RX, 1, 128), f32),
-            pltpu.VMEM((51, RX, 128), f32),
+            pltpu.VMEM((PLANES, RX, 128), f32),
             pltpu.VMEM((11, 8, 128), f32),
         ),
         in_specs=[any_spec] * (len(operands) + 1),
@@ -382,7 +382,7 @@
             pltpu.VMEM((2, 1, 128), f32),
             pltpu.VMEM((TB, RX, 1, 128), f32),
             pltpu.VMEM((TB, RX, 128), f32),
-            pltpu.VMEM((51, RX, 128), f32),
+            pltpu.VMEM((PLANES, RX, 128), f32),
             pltpu.VMEM((11, 8, 128), f32),
             pltpu.VMEM((TB, 16, LAG_COUNT), bf16),
             pltpu.VMEM((4, 16, 2, LAG_COUNT), f32),
@@ -424,11 +424,13 @@
 ROW_OF = (0, 4, 2, 6)
 OWNER_AT = (0, 0, 2, 2, 1, 1, 3, 3)
 PAIRS = ((0, 0), (0, 1), (0, 2), (1, 1), (1, 2), (2, 2))
-MASK, LATE, FIRST, SECOND, SPREAD, JAC = 0, 16, 20, 23, 35, 39
+EMIT, MASK, LIVE, LATE, FIRST, SECOND, SPREAD, JAC, PLANES = 0, 4, 16, 20, 24, 27, 39, 43, 55
 START, STEPS, DAMP, NORMAL = 0, 3, 4, 5
 
 
 def fold(parts):
+    total, second, third, fourth = parts
+    first = total - second - third - fourth
     sub = iota((8, 128), 0)
     upper = sub < 4
     early = lax.rem(sub, 4) < 2
@@ -436,51 +438,69 @@
     def halves(x, y):
         return jnp.where(upper, x, y) + pltpu.roll(jnp.where(upper, y, x), 4, 0)
 
-    one = halves(parts[0], parts[1])
-    two = halves(parts[2], parts[3])
+    one = halves(first, second)
+    two = halves(third, fourth)
     rows = jnp.where(early, one + pltpu.roll(one, 6, 0), two + pltpu.roll(two, 2, 0))
     rows = rows + pltpu.roll(rows, 7, 0)
     rows = rows + pltpu.roll(rows, 32, 1)
     return rows + pltpu.roll(rows, 64, 1)
 
 
-def add_to(prep_ref, acc, key, k, quantity):
-    for e in range(4):
-        term = prep_ref[MASK + 4 * e + k] * quantity
-        term = (term[0:8] + term[8:16]) + (term[16:24] + term[24:32])
-        acc[key][e] = term if k == 0 else acc[key][e] + term
-
-
-def at_peaks(prep_ref, rows, k):
-    value = prep_ref[MASK + k] * rows[0:1]
-    for e in range(1, 4):
-        value = value + prep_ref[MASK + 4 * e + k] * rows[ROW_OF[e] : ROW_OF[e] + 1]
+def add_to(acc, key, masks, quantity):
+    terms = [quantity] + [mask * quantity for mask in masks]
+    old = acc[key]
+    acc[key] = terms if old is None else [x + y for x, y in zip(old, terms)]
+
+
+def spread_rows(rows):
+    return [jnp.broadcast_to(rows[at : at + 1], (8, 128)) for at in ROW_OF]
+
+
+def tile_of(k, h):
+    return k, slice(8 * h, 8 * h + 8)
+
+
+def at_peak(which, rows):
+    value = rows[0]
+    for is_it, row in zip(which, rows[1:]):
+        value = jnp.where(is_it, row, value)
     return value
 
 
-def second_of(x, late, k):
-    low = iota((RX, 128), 1) < 64
-    near_half = jnp.where(late, per_receiver(x, 2 * k + 2), per_receiver(x, 2 * k + 1))
-    far_half = jnp.where(late, per_receiver(x, 2 * k + 10), per_receiver(x, 2 * k + 9))
-    return jnp.where(low, near_half, far_half)
-
-
-def ranges(prep_ref, position, k):
-    sq_first = jnp.ones((RX, 128), f32)
-    sq_second = sq_first
+def tile_ranges(prep_ref, which, position, k, part):
+    sq_first = None
     firsts, seconds = [], []
     for comp in range(3):
-        at = at_peaks(prep_ref, position[comp], k)
-        d_first = at - prep_ref[FIRST + comp]
-        d_second = at - prep_ref[SECOND + 4 * comp + k]
-        sq_first = sq_first + d_first * d_first
-        sq_second = sq_second + d_second * d_second
+        at = at_peak(which, position[comp])
+        d_first = at - prep_ref[FIRST + comp, part, :]
+        d_second = at - prep_ref[SECOND + 4 * comp + k, part, :]
+        if sq_first is None:
+            sq_first = 1.0 + d_first * d_first
+            sq_second = 1.0 + d_second * d_second
+        else:
+            sq_first = sq_first + d_first * d_first
+            sq_second = sq_second + d_second * d_second
         firsts.append(d_first)
         seconds.append(d_second)
     inv_first = lax.rsqrt(sq_first)
     inv_second = lax.rsqrt(sq_second)
     spread = sq_second * inv_second - sq_first * inv_first
+    live = prep_ref[LIVE + k, part, :]
+    inv_first = inv_first * live
+    inv_second = inv_second * live
     return spread, [seconds[i] * inv_second - firsts[i] * inv_first for i in range(3)]
+
+
+def tile_masks(prep_ref, k, part):
+    emit = prep_ref[EMIT + k, part, :]
+    which = [emit == float(e) for e in (1, 2, 3)]
+    return which, [prep_ref[MASK + 4 * e + k, part, :] for e in range(3)]
+
+
+def turned_by_slot(x):
+    low = iota((RX, 128), 1) < 64
+    base = jnp.where(low, x, jnp.concatenate([x[8:], x[:8]], axis=0))
+    return [per_receiver(base, shift) for shift in range(1, 9)]
 
 
 def prepare(code_ref, rpos_ref, prep_ref, small_ref):
@@ -491,8 +511,10 @@
         code = jnp.where(low, code_ref[k], pltpu.roll(code_ref[k + 4], 64, 1))
         late = code > 4.5
         prep_ref[LATE + k] = jnp.where(late, 1.0, 0.0)
-        emitter = jnp.where(late, code - 4.0, code)
-        for e in range(4):
+        emitter = jnp.where(late, code - 5.0, code - 1.0)
+        prep_ref[EMIT + k] = emitter
+        prep_ref[LIVE + k] = jnp.where(code > 0.5, 1.0, 0.0)
+        for e in range(3):
             prep_ref[MASK + 4 * e + k] = jnp.where(emitter == e + 1.0, 1.0, 0.0)
     info = code_ref[0]
 
@@ -515,17 +537,22 @@
         )
         column = jnp.broadcast_to(column, (RX, 128))
         prep_ref[FIRST + comp] = column
+        turned = turned_by_slot(column)
         for k in range(4):
-            prep_ref[SECOND + 4 * comp + k] = second_of(column, prep_ref[LATE + k] > 0.5, k)
-    acc = {key: [None] * 4 for key in range(7)}
-    for k in range(4):
-        spread, jac = ranges(prep_ref, position, k)
-        prep_ref[SPREAD + k] = spread
+            prep_ref[SECOND + 4 * comp + k] = jnp.where(
+                prep_ref[LATE + k] > 0.5, turned[2 * k + 1], turned[2 * k]
+            )
+    acc = {key: None for key in range(7)}
+    position = [spread_rows(rows) for rows in position]
+    for k, part in [tile_of(k, h) for k in range(4) for h in range(4)]:
+        which, masks = tile_masks(prep_ref, k, part)
+        spread, jac = tile_ranges(prep_ref, which, position, k, part)
+        prep_ref[SPREAD + k, part, :] = spread
         for i in range(3):
-            prep_ref[JAC + 4 * i + k] = jac[i]
+            prep_ref[JAC + 4 * i + k, part, :] = jac[i]
         for key, (x, y) in enumerate(PAIRS):
-            add_to(prep_ref, acc, key, k, jac[x] * jac[y])
-        add_to(prep_ref, acc, 6, k, jnp.ones((RX, 128), f32))
+            add_to(acc, key, masks, jac[x] * jac[y])
+        add_to(acc, 6, masks, prep_ref[LIVE + k, part, :])
     for key in range(6):
         small_ref[NORMAL + key] = fold(acc[key])
     small_ref[DAMP] = 2.0 * (fold(acc[6]) + 1.0)
@@ -533,7 +560,7 @@
 
 def solve_kernel(
     table_ref, prep_ref, small_ref, amb_in, pos_ref, vel_ref, bias_ref, amb_out,
-    out_sem, tau_ref, nu_ref, spread_ref, jac_ref,
+    out_sem, tau_ref, nu_ref, spread_ref, jac_ref, left_ref,
 ):
     amb_copy = pltpu.make_async_copy(amb_in, amb_out, out_sem.at[0])
     amb_copy.start()
@@ -547,57 +574,56 @@
         for i in range(3):
             jac_ref[i, k] = prep_ref[JAC + 4 * i + k]
     position = [small_ref[START + k] for k in range(3)]
-    steps = small_ref[STEPS]
-    damp = small_ref[DAMP]
     normals = [small_ref[NORMAL + key] for key in range(6)]
     zero = jnp.zeros((8, 128), f32)
+    tiles = [tile_of(k, h) for k in range(4) for h in range(4)]
 
     def gn_step(step, carry):
         position, speed, bias, normals = carry
-        moving = step.astype(f32) < steps
-        acc = {key: [None] * 4 for key in range(3)}
+        moving = step.astype(f32) < small_ref[STEPS]
+        damp = small_ref[DAMP]
+        turned = turned_by_slot(bias)
+        acc = {key: None for key in range(3)}
         for k in range(4):
-            delta = second_of(bias, prep_ref[LATE + k] > 0.5, k) - bias
-            resid = tau_ref[k] - spread_ref[k] - delta
+            late = prep_ref[LATE + k] > 0.5
+            left_ref[k] = tau_ref[k] + bias - jnp.where(late, turned[2 * k + 1], turned[2 * k])
+        for k, part in tiles:
+            masks = [prep_ref[MASK + 4 * e + k, part, :] for e in range(3)]
+            resid = left_ref[k, part, :] - spread_ref[k, part, :]
             for i in range(3):
-                add_to(prep_ref, acc, i, k, jac_ref[i, k] * resid)
+                add_to(acc, i, masks, jac_ref[i, k, part, :] * resid)
         moved = solve_three(normals, [fold(acc[i]) for i in range(3)], damp)
         position = [position[i] + jnp.where(moving, moved[i], 0.0) for i in range(3)]
-        acc = {key: [None] * 4 for key in range(9)}
-        clock = None
-        for k in range(4):
-            spread, jac = ranges(prep_ref, position, k)
-            spread_ref[k] = spread
+        at_rows = [spread_rows(rows) for rows in position]
+        speed_rows = [spread_rows(rows) for rows in speed]
+        acc = {key: None for key in range(9)}
+        for k, part in tiles:
+            which, masks = tile_masks(prep_ref, k, part)
+            spread, jac = tile_ranges(prep_ref, which, at_rows, k, part)
+            spread_ref[k, part, :] = spread
             for i in range(3):
-                jac_ref[i, k] = jac[i]
+                jac_ref[i, k, part, :] = jac[i]
+            rate = nu_ref[k, part, :]
+            for i in range(3):
+                rate = rate - at_peak(which, speed_rows[i]) * jac[i]
             for key, (x, y) in enumerate(PAIRS):
-                add_to(prep_ref, acc, key, k, jac[x] * jac[y])
-            rate = nu_ref[k]
+                add_to(acc, key, masks, jac[x] * jac[y])
             for i in range(3):
-                rate = rate - at_peaks(prep_ref, speed[i], k) * jac[i]
-            for i in range(3):
-                add_to(prep_ref, acc, 6 + i, k, jac[i] * rate)
-            late_k = prep_ref[LATE + k]
-            live = (prep_ref[MASK + k] + prep_ref[MASK + 4 + k]) + (
-                prep_ref[MASK + 8 + k] + prep_ref[MASK + 12 + k]
-            )
-            delta = second_of(bias, late_k > 0.5, k) - bias
-            cres = live * (tau_ref[k] - spread - delta)
-            late = late_k * cres
-            early = cres - late
-            part = -cres
-            for term, keep, shift in (
-                (early, low, 2 * k + 1),
-                (late, low, 2 * k + 2),
-                (early, jnp.logical_not(low), 2 * k + 9),
-                (late, jnp.logical_not(low), 2 * k + 10),
-            ):
-                part = part + pltpu.roll(jnp.where(keep, term, 0.0), shift, 0)
-            clock = part if clock is None else clock + part
+                add_to(acc, 6 + i, masks, jac[i] * rate)
+        nested, whole = None, None
+        for k in (3, 2, 1, 0):
+            gap = left_ref[k] - spread_ref[k]
+            every = prep_ref[LIVE + k] * gap
+            late = prep_ref[LATE + k] * gap
+            term = every - late + pltpu.roll(late, 1, 0)
+            nested = term if nested is None else term + pltpu.roll(nested, 2, 0)
+            whole = every if whole is None else whole + every
+        nested = pltpu.roll(nested, 1, 0)
+        shifted = jnp.concatenate([nested[24:], nested[:24]], axis=0)
+        total = jnp.sum(jnp.where(low, nested, shifted) - whole, axis=1, keepdims=True)
         normals = [fold(acc[key]) for key in range(6)]
-        turned = solve_three(normals, [fold(acc[6 + i]) for i in range(3)], damp)
-        speed = [speed[i] + jnp.where(moving, turned[i], 0.0) for i in range(3)]
-        total = jnp.sum(clock, axis=1, keepdims=True)
+        swung = solve_three(normals, [fold(acc[6 + i]) for i in range(3)], damp)
+        speed = [speed[i] + jnp.where(moving, swung[i], 0.0) for i in range(3)]
         bias = bias + jnp.broadcast_to(total, (RX, 128)) / (3.0 * 16 * RX)
         return position, speed, bias, normals
 
@@ -638,6 +664,7 @@
             pltpu.VMEM(block, f32),
             pltpu.VMEM(block, f32),
             pltpu.VMEM((3,) + block, f32),
+            pltpu.VMEM(block, f32),
         ],
         compiler_params=pltpu.CompilerParams(vmem_limit_bytes=12 << 20),
         name="solve",

time: 42.8 us -> 42.5 us (level)
  no operation moved by 1% of the time
where the time goes in v7:
time: 42.5 us; the launch traced here: 42.4 us
  Pallas kernels  41.7 us (98%)
  between operations  0.64 us (2%)
    pallas_call x1, Pallas kernels, front(): pl.pallas_call(front_kernel, out_shape=(pltpu.VMEM((4, 16, 2, LAG_COUNT),...  36.6 us
    pallas_call x1, Pallas kernels, solve(): pl.pallas_call(solve_kernel, out_shape=(jax.ShapeDtypeStruct((3, 4), f32)...  5.1 us

profile of v7, /device:TPU:1, one launch (start us, length us, event | category | flops | bytes accessed | tf_op | source)
XLA Modules:
  0.0 42.4 jit_solution(15229088900920383520)
XLA Ops:
  0.6 36.6 %front.1 = (f32[4,16,2,1024]{3,2,1,0:T(2,128)S(1)}, f32[8,32,1,128]{3,2,1,0:T(1,128)S(1)}, f32[55,32,128]{2,1,0:T(8,128)S(1)}, f32[11,8,128]{2,1,0:T(8,128)S(1)}) custom-call(bf16[1,2,1024]{2,1,0:T(2,128)(2,1)} %raw_in.1, f32[1,4]{1,0:T(1,128)} %scl_in.1, s32[16,16]{1,0:T(8,128)} %lag_in.1, s32[16,16]{1,0:T(8,128)} %dop_in.1, s32[2,16]{1,0:T(2,128)} %bitcast.5, ...), custom_call_target="tpu_custom_call" | custom-call | tf_op jit(solution)/shard_map/front/pallas_call | solution.py:362
  37.3 5.1 %solve.1 = (f32[3,4]{1,0:T(4,128)}, f32[3,4]{1,0:T(4,128)}, f32[1,32]{1,0:T(1,128)}, f32[4,16,2,1024]{3,2,1,0:T(2,128)}) custom-call(f32[8,32,128]{2,1,0:T(8,128)S(1)} %bitcast.4, f32[55,32,128]{2,1,0:T(8,128)S(1)} %get-tuple-element.13.prep_ref, f32[11,8,128]{2,1,0:T(8,128)S(1)} %get-tuple-element.14.small_ref, f32[4,16,2,1024]{3,2,1,0:T(2,128)S(1)} %get-tuple-element.15.amb_in), custom_call_target="tpu_custom_call" | custom-call | tf_op jit(solution)/shard_map/solve/pallas_call | solution.py:651

commit v8 on v7

--- a/solution.py
+++ b/solution.py
@@ -79,7 +79,7 @@
     amb, table, prep, small,
     raw_ref, scl_ref, lag_ref, dop_ref, own_ref, em_ref, start_ref, steps_ref,
     fhi_ref, flo_ref, bhi_ref, blo_ref, mix_ref,
-    rpos_ref, block_ref, raw_all, scl_all, re_ref, im_ref, rr_ref, surf_ref, pay_ref,
+    rpos_ref, pad_ref, block_ref, raw_all, scl_all, re_ref, im_ref, rr_ref, surf_ref, pay_ref,
     code_tab, code_ref, prep_ref, small_ref, land_ref, wide_ref,
     load_sem, raw_send, raw_recv, scl_send, scl_recv, code_send, code_recv,
     cfwd_send, cfwd_recv, pay_send, pay_recv, fwd_send, fwd_recv, surf_send, surf_recv, own_sem,
@@ -121,23 +121,23 @@
     block_ref[...] = jnp.concatenate(
         [own_raw[k : k + 1, SEG * s : SEG * s + SEG] for k in range(2) for s in range(4)], axis=0
     ).astype(bf16)
-
-    raw_all[b] = block_ref[...]
-    scl_all[b] = scl_ref[...]
+    pad_ref[...] = jnp.zeros((1, 128), f32)
+    pad_ref[:, 0:4] = scl_ref[...]
+
 
     pl.semaphore_wait(barrier, len(sources) + len(rows) + len(blocks))
 
     targets = [(r, p, 0) for _, p in blocks]
     targets += [(lax.rem(r + RX - 2 * t - i, RX), t, i) for t in range(TB) for i in (1, 2)]
-    sends = []
-    for n, (to_r, to_b, i) in enumerate(targets):
+    for to_r, to_b, i in targets:
         place = i * TB + b
         for src, dst, ss, rs in (
             (block_ref, raw_all, raw_send, raw_recv),
-            (scl_ref, scl_all, scl_send, scl_recv),
+            (pad_ref, scl_all, scl_send, scl_recv),
         ):
-            sends.append(remote(src, dst.at[place], ss.at[n], rs.at[place], (to_r, to_b)))
-            sends[-1].start()
+            remote(src, dst.at[place], ss, rs, (to_r, to_b)).start()
+    pltpu.make_async_copy(block_ref, raw_all.at[b], raw_recv).start()
+    pltpu.make_async_copy(pad_ref, scl_all.at[b], scl_recv).start()
     for copy in loads[2:8]:
         copy.wait()
     owner = jnp.concatenate(
@@ -164,23 +164,12 @@
     for e in range(4):
         codes = jnp.where(lane1 == 76 + e, steps_ref[0:1, e : e + 1].astype(f32), codes)
     pay_ref[1] = codes
-    own_code = pltpu.make_async_copy(pay_ref.at[1], code_tab.at[b, r], own_sem.at[5])
-    own_code.start()
-    for n, peer in enumerate(rows):
-        sends.append(
-            remote(pay_ref.at[1], code_tab.at[b, r], code_send.at[n], code_recv.at[r], peer)
-        )
-        sends[-1].start()
-
-
-    places = [p for _, p in blocks] + [i * TB + t for i in (1, 2) for t in range(TB)]
-    for place in places:
-        remote(
-            block_ref, raw_all.at[place], raw_send.at[0], raw_recv.at[place], blocks[0]
-        ).wait_recv()
-        remote(
-            scl_ref, scl_all.at[place], scl_send.at[0], scl_recv.at[place], blocks[0]
-        ).wait_recv()
+    pltpu.make_async_copy(pay_ref.at[1], code_tab.at[b, r], code_recv).start()
+    for peer in rows:
+        remote(pay_ref.at[1], code_tab.at[b, r], code_send, code_recv, peer).start()
+    peer = blocks[0]
+    remote(raw_all, raw_all, raw_send, raw_recv, peer).wait_recv()
+    remote(scl_all, scl_all, scl_send, scl_recv, peer).wait_recv()
     for copy in loads[8:]:
         copy.wait()
 
@@ -191,7 +180,7 @@
     sin_part = spec[:, FFT:].reshape(3 * TB, 8, FFT)
     sub = iota((1, 8, 1), 1)
     sign = jnp.where(sub < 4, 1.0, -1.0).astype(f32)
-    pick = iota((1, 8, 4), 2) == lax.rem(iota((1, 8, 4), 1), 4)
+    pick = iota((1, 8, 128), 2) == lax.rem(iota((1, 8, 128), 1), 4)
     scale = jnp.sum(jnp.where(pick, scl_all[...], 0.0), axis=2, keepdims=True)
     pieces = (cos_part + sign * pltpu.roll(sin_part, 4, 1)) * scale
     for i in range(3):
@@ -210,16 +199,9 @@
             row = (c * 4 + j) * 32
             rr_ref[row : row + 32, :] = near_re * far_re + near_im * far_im
             rr_ref[256 + row : 288 + row, :] = near_im * far_re - near_re * far_im
-    own_code.wait()
-    for q, _ in rows:
-        remote(
-            pay_ref.at[1], code_tab.at[b, q], code_send.at[0], code_recv.at[q], rows[0]
-        ).wait_recv()
-    for n, peer in enumerate(blocks):
-        sends.append(
-            remote(code_tab.at[b], code_tab.at[b], cfwd_send.at[n], cfwd_recv.at[b], peer)
-        )
-        sends[-1].start()
+    remote(code_tab.at[b], code_tab.at[b], code_send, code_recv, blocks[0]).wait_recv()
+    for peer in blocks:
+        remote(code_tab.at[b], code_tab.at[b], cfwd_send, cfwd_recv.at[b], peer).start()
     cross = rr_ref[...]
     high = cross.astype(bf16)
     low = (cross - high.astype(f32)).astype(bf16)
@@ -277,32 +259,25 @@
         jnp.where(placed, jnp.where(first, tau, nu), 0.0), axis=0, keepdims=True
     )
 
-    own_pay = pltpu.make_async_copy(pay_ref.at[0], table.at[b, r], own_sem.at[0])
-    own_pay.start()
-    for n, peer in enumerate(rows):
-        sends.append(
-            remote(pay_ref.at[0], table.at[b, r], pay_send.at[n], pay_recv.at[r], peer)
-        )
-        sends[-1].start()
+    part = r // 8
+    pltpu.make_async_copy(pay_ref.at[0], table.at[b, r], pay_recv.at[part]).start()
+    for peer in rows:
+        remote(pay_ref.at[0], table.at[b, r], pay_send, pay_recv.at[part], peer).start()
     for t in range(TB):
         surf_ref[t] = jnp.concatenate(
             [surfs[0][8 * t : 8 * t + 8], surfs[1][8 * t : 8 * t + 8]], axis=0
         ).astype(bf16)
     own_surf = pltpu.make_async_copy(surf_ref.at[b], land_ref.at[b], own_sem.at[1])
     own_surf.start()
-    for n, peer in enumerate(blocks):
-        sends.append(
-            remote(surf_ref.at[peer[1]], land_ref.at[b], surf_send.at[n], surf_recv.at[b], peer)
-        )
-        sends[-1].start()
-    own_pay.wait()
-    for copy in sends[: -len(blocks)]:
-        copy.wait_send()
-    sends = sends[-len(blocks) :]
+    for peer in blocks:
+        remote(surf_ref.at[peer[1]], land_ref.at[b], surf_send, surf_recv.at[b], peer).start()
+    some = blocks[0]
+    near = (raw_all.at[pl.ds(0, 3 * TB - 1)], raw_send), (scl_all.at[pl.ds(0, 3 * TB - 1)], scl_send)
+    row_set = code_tab.at[0, pl.ds(0, RX - 1)]
+    for ref, sem in near + ((row_set, code_send), (row_set, pay_send)):
+        remote(ref, ref, sem, raw_recv, some).wait_send()
     for _, t in blocks:
-        remote(
-            code_tab.at[t], code_tab.at[t], cfwd_send.at[0], cfwd_recv.at[t], blocks[0]
-        ).wait_recv()
+        remote(code_tab.at[t], code_tab.at[t], cfwd_send, cfwd_recv.at[t], some).wait_recv()
     rpos_copy.wait()
     for k in range(TB):
         for q in range(RX):
@@ -315,28 +290,15 @@
     ]
     outs[0].start()
     outs[1].start()
-    part = r // 8
-    spot = lax.rem(r, 8)
-    for count, dp in enumerate((0, 1, 3, 2)):
+    for dp in (0, 1, 3, 2):
         there = lax.rem(part + dp, 4)
-        for dx in range(8):
-            if dp == 0 and dx == 0:
-                continue
-            q = there * 8 + lax.rem(spot + dx, 8)
-            remote(
-                pay_ref.at[0], table.at[b, q], pay_send.at[0], pay_recv.at[q], rows[0]
-            ).wait_recv()
         chunk = table.at[b, pl.ds(there * 8, 8)]
-        for n, peer in enumerate(blocks):
-            sends.append(
-                remote(chunk, chunk, fwd_send.at[n, count], fwd_recv.at[b, there], peer)
-            )
-            sends[-1].start()
+        remote(chunk, chunk, pay_send, pay_recv.at[there], some).wait_recv()
+        for peer in blocks:
+            remote(chunk, chunk, fwd_send, fwd_recv.at[b], peer).start()
     own_surf.wait()
     for _, t in blocks:
-        remote(
-            surf_ref.at[t], land_ref.at[t], surf_send.at[0], surf_recv.at[t], blocks[0]
-        ).wait_recv()
+        remote(surf_ref.at[t], land_ref.at[t], surf_send, surf_recv.at[t], some).wait_recv()
     for t in range(TB):
         value = land_ref[t].astype(f32)
         for c in range(2):
@@ -344,21 +306,21 @@
                 row = 8 * c + 2 * d
                 wide_ref[d, 2 * t + c] = value[row : row + 2, :]
     outs[2].start()
+    for ref, sem in ((code_tab, cfwd_send), (surf_ref, surf_send)):
+        ref = ref.at[pl.ds(0, TB - 1)]
+        remote(ref, ref, sem, raw_recv, some).wait_send()
     for _, t in blocks:
-        for z in range(4):
-            chunk = table.at[t, pl.ds(z * 8, 8)]
-            remote(chunk, chunk, fwd_send.at[0, 0], fwd_recv.at[t, z], blocks[0]).wait_recv()
+        remote(table.at[t], table.at[t], fwd_send, fwd_recv.at[t], some).wait_recv()
     for copy in outs:
         copy.wait()
-    for copy in sends:
-        copy.wait_send()
+    ref = table.at[pl.ds(0, TB - 1)]
+    remote(ref, ref, fwd_send, raw_recv, some).wait_send()
 
 
 def front(raw, scl, lag, dop, own, em, start, steps, consts, rpos):
     any_spec = pl.BlockSpec(memory_space=pl.ANY)
     dma = pltpu.SemaphoreType.DMA
     operands = (raw, scl, lag, dop, own, em, start, steps, *consts)
-    n = 3 * TB - 1
     return pl.pallas_call(
         front_kernel,
         out_shape=(
@@ -372,9 +334,10 @@
         scratch_shapes=[pltpu.VMEM(x.shape, x.dtype) for x in operands]
         + [
             pltpu.VMEM(rpos.shape, f32),
+            pltpu.VMEM((1, 128), f32),
             pltpu.VMEM((8, SEG), bf16),
             pltpu.VMEM((3 * TB, 8, SEG), bf16),
-            pltpu.VMEM((3 * TB,) + scl.shape, f32),
+            pltpu.VMEM((3 * TB, 1, 128), f32),
             pltpu.VMEM((3, 40, FFT), f32),
             pltpu.VMEM((3, 40, FFT), f32),
             pltpu.VMEM((512, FFT), f32),
@@ -387,10 +350,8 @@
             pltpu.VMEM((TB, 16, LAG_COUNT), bf16),
             pltpu.VMEM((4, 16, 2, LAG_COUNT), f32),
             dma((len(operands),)),
-            dma((n,)), dma((3 * TB,)), dma((n,)), dma((3 * TB,)),
-            dma((RX - 1,)), dma((RX,)), dma((TB - 1,)), dma((TB,)),
-            dma((RX - 1,)), dma((RX,)), dma((TB - 1, 4)), dma((TB, 4)),
-            dma((TB - 1,)), dma((TB,)), dma((6,)),
+            dma, dma, dma, dma, dma, dma, dma, dma((TB,)), dma, dma((4,)), dma, dma((TB,)),
+            dma, dma((TB,)), dma((6,)),
         ],
         compiler_params=pltpu.CompilerParams(collective_id=0, has_side_effects=True),
         name="front",

time: 42.5 us -> 39.8 us (0.936)
  Pallas kernels: 41.7 us -> 39.1 us
    pallas_call x1, Pallas kernels: 36.6 us -> 34 us  [front(): pl.pallas_call(front_kernel, out_shape=(pltpu.VMEM((4, 16, 2, LAG_COUNT),...]
where the time goes in v8:
time: 39.8 us; the launch traced here: 39.7 us
  Pallas kernels  39.1 us (98%)
  between operations  0.64 us (2%)
    pallas_call x1, Pallas kernels, front(): pl.pallas_call(front_kernel, out_shape=(pltpu.VMEM((4, 16, 2, LAG_COUNT),...  34 us
    pallas_call x1, Pallas kernels, solve(): pl.pallas_call(solve_kernel, out_shape=(jax.ShapeDtypeStruct((3, 4), f32)...  5.1 us

profile of v8, /device:TPU:1, one launch (start us, length us, event | category | flops | bytes accessed | tf_op | source)
XLA Modules:
  0.0 39.7 jit_solution(16431233207322953458)
XLA Ops:
  0.6 34.0 %front.1 = (f32[4,16,2,1024]{3,2,1,0:T(2,128)S(1)}, f32[8,32,1,128]{3,2,1,0:T(1,128)S(1)}, f32[55,32,128]{2,1,0:T(8,128)S(1)}, f32[11,8,128]{2,1,0:T(8,128)S(1)}) custom-call(bf16[1,2,1024]{2,1,0:T(2,128)(2,1)} %raw_in.1, f32[1,4]{1,0:T(1,128)} %scl_in.1, s32[16,16]{1,0:T(8,128)} %lag_in.1, s32[16,16]{1,0:T(8,128)} %dop_in.1, s32[2,16]{1,0:T(2,128)} %bitcast.5, ...), custom_call_target="tpu_custom_call" | custom-call | tf_op jit(solution)/shard_map/front/pallas_call | solution.py:324
  34.6 5.1 %solve.1 = (f32[3,4]{1,0:T(4,128)}, f32[3,4]{1,0:T(4,128)}, f32[1,32]{1,0:T(1,128)}, f32[4,16,2,1024]{3,2,1,0:T(2,128)}) custom-call(f32[8,32,128]{2,1,0:T(8,128)S(1)} %bitcast.4, f32[55,32,128]{2,1,0:T(8,128)S(1)} %get-tuple-element.13.prep_ref, f32[11,8,128]{2,1,0:T(8,128)S(1)} %get-tuple-element.14.small_ref, f32[4,16,2,1024]{3,2,1,0:T(2,128)S(1)} %get-tuple-element.15.amb_in), custom_call_target="tpu_custom_call" | custom-call | tf_op jit(solution)/shard_map/solve/pallas_call | solution.py:612

commit v9 on v8

--- a/solution.py
+++ b/solution.py
@@ -44,7 +44,10 @@
     mix = mix / (FFT * math.sqrt(SAMPLES))
     mix_high, mix_low = split_pair(mix)
     deep_mix = np.concatenate([mix_high, mix_low, mix_high], axis=1)
-    return split_pair(forward) + split_pair(backward) + (deep_mix,)
+    deep_forward = np.concatenate(split_pair(forward), axis=0)
+    back_high, back_low = split_pair(backward)
+    deep_backward = np.concatenate([back_high, back_low], axis=0)
+    return deep_forward, deep_backward, deep_mix
 
 
 def iota(shape, dim):
@@ -75,10 +78,10 @@
 
 def front_kernel(
     raw_in, scl_in, lag_in, dop_in, own_in, em_in, start_in, steps_in,
-    fhi_in, flo_in, bhi_in, blo_in, mix_in, rpos_in,
+    fwd_in, back_in, mix_in, rpos_in,
     amb, table, prep, small,
     raw_ref, scl_ref, lag_ref, dop_ref, own_ref, em_ref, start_ref, steps_ref,
-    fhi_ref, flo_ref, bhi_ref, blo_ref, mix_ref,
+    fwd_ref, back_ref, mix_ref,
     rpos_ref, pad_ref, block_ref, raw_all, scl_all, re_ref, im_ref, rr_ref, surf_ref, pay_ref,
     code_tab, code_ref, prep_ref, small_ref, land_ref, wide_ref,
     load_sem, raw_send, raw_recv, scl_send, scl_recv, code_send, code_recv,
@@ -106,8 +109,7 @@
             (
                 (raw_in, raw_ref), (scl_in, scl_ref), (own_in, own_ref), (em_in, em_ref),
                 (start_in, start_ref), (steps_in, steps_ref), (lag_in, lag_ref),
-                (dop_in, dop_ref), (fhi_in, fhi_ref), (flo_in, flo_ref), (bhi_in, bhi_ref),
-                (blo_in, blo_ref), (mix_in, mix_ref),
+                (dop_in, dop_ref), (fwd_in, fwd_ref), (back_in, back_ref), (mix_in, mix_ref),
             )
         )
     ]
@@ -174,8 +176,8 @@
         copy.wait()
 
     raw = raw_all[...].astype(f32).reshape(3 * TB * 8, SEG).astype(bf16)
-    spec = jnp.dot(raw, fhi_ref[...], preferred_element_type=f32)
-    spec = spec + jnp.dot(raw, flo_ref[...], preferred_element_type=f32)
+    spec = jnp.dot(raw, fwd_ref[0:256, :], preferred_element_type=f32)
+    spec = spec + jnp.dot(raw, fwd_ref[256:512, :], preferred_element_type=f32)
     cos_part = spec[:, :FFT].reshape(3 * TB, 8, FFT)
     sin_part = spec[:, FFT:].reshape(3 * TB, 8, FFT)
     sub = iota((1, 8, 1), 1)
@@ -201,13 +203,13 @@
             rr_ref[256 + row : 288 + row, :] = near_im * far_re - near_re * far_im
     remote(code_tab.at[b], code_tab.at[b], code_send, code_recv, blocks[0]).wait_recv()
     for peer in blocks:
-        remote(code_tab.at[b], code_tab.at[b], cfwd_send, cfwd_recv.at[b], peer).start()
+        remote(code_tab.at[b], code_tab.at[b], cfwd_send, cfwd_recv, peer).start()
     cross = rr_ref[...]
     high = cross.astype(bf16)
     low = (cross - high.astype(f32)).astype(bf16)
-    lagged = jnp.dot(high, bhi_ref[...], preferred_element_type=f32)
-    lagged = lagged + jnp.dot(low, bhi_ref[...], preferred_element_type=f32)
-    lagged = lagged + jnp.dot(high, blo_ref[...], preferred_element_type=f32)
+    lagged = jnp.dot(high, back_ref[0:512, :], preferred_element_type=f32)
+    lagged = lagged + jnp.dot(low, back_ref[0:512, :], preferred_element_type=f32)
+    lagged = lagged + jnp.dot(high, back_ref[512:1024, :], preferred_element_type=f32)
     lag_re = lagged[0:256, 0:256] + lagged[256:512, 256:512]
     lag_im = lagged[256:512, 0:256] - lagged[0:256, 256:512]
 
@@ -267,17 +269,16 @@
         surf_ref[t] = jnp.concatenate(
             [surfs[0][8 * t : 8 * t + 8], surfs[1][8 * t : 8 * t + 8]], axis=0
         ).astype(bf16)
-    own_surf = pltpu.make_async_copy(surf_ref.at[b], land_ref.at[b], own_sem.at[1])
-    own_surf.start()
+    pltpu.make_async_copy(surf_ref.at[b], land_ref.at[b], surf_recv).start()
     for peer in blocks:
-        remote(surf_ref.at[peer[1]], land_ref.at[b], surf_send, surf_recv.at[b], peer).start()
+        remote(surf_ref.at[peer[1]], land_ref.at[b], surf_send, surf_recv, peer).start()
     some = blocks[0]
     near = (raw_all.at[pl.ds(0, 3 * TB - 1)], raw_send), (scl_all.at[pl.ds(0, 3 * TB - 1)], scl_send)
     row_set = code_tab.at[0, pl.ds(0, RX - 1)]
     for ref, sem in near + ((row_set, code_send), (row_set, pay_send)):
         remote(ref, ref, sem, raw_recv, some).wait_send()
-    for _, t in blocks:
-        remote(code_tab.at[t], code_tab.at[t], cfwd_send, cfwd_recv.at[t], some).wait_recv()
+    ref = code_tab.at[pl.ds(0, TB - 1)]
+    remote(ref, ref, cfwd_send, cfwd_recv, some).wait_recv()
     rpos_copy.wait()
     for k in range(TB):
         for q in range(RX):
@@ -295,10 +296,8 @@
         chunk = table.at[b, pl.ds(there * 8, 8)]
         remote(chunk, chunk, pay_send, pay_recv.at[there], some).wait_recv()
         for peer in blocks:
-            remote(chunk, chunk, fwd_send, fwd_recv.at[b], peer).start()
-    own_surf.wait()
-    for _, t in blocks:
-        remote(surf_ref.at[t], land_ref.at[t], surf_send, surf_recv.at[t], some).wait_recv()
+            remote(chunk, chunk, fwd_send, fwd_recv, peer).start()
+    remote(surf_ref, land_ref, surf_send, surf_recv, some).wait_recv()
     for t in range(TB):
         value = land_ref[t].astype(f32)
         for c in range(2):
@@ -309,12 +308,10 @@
     for ref, sem in ((code_tab, cfwd_send), (surf_ref, surf_send)):
         ref = ref.at[pl.ds(0, TB - 1)]
         remote(ref, ref, sem, raw_recv, some).wait_send()
-    for _, t in blocks:
-        remote(table.at[t], table.at[t], fwd_send, fwd_recv.at[t], some).wait_recv()
     for copy in outs:
         copy.wait()
     ref = table.at[pl.ds(0, TB - 1)]
-    remote(ref, ref, fwd_send, raw_recv, some).wait_send()
+    remote(ref, ref, fwd_send, fwd_recv, some).wait()
 
 
 def front(raw, scl, lag, dop, own, em, start, steps, consts, rpos):
@@ -350,8 +347,7 @@
             pltpu.VMEM((TB, 16, LAG_COUNT), bf16),
             pltpu.VMEM((4, 16, 2, LAG_COUNT), f32),
             dma((len(operands),)),
-            dma, dma, dma, dma, dma, dma, dma, dma((TB,)), dma, dma((4,)), dma, dma((TB,)),
-            dma, dma((TB,)), dma((6,)),
+            dma, dma, dma, dma, dma, dma, dma, dma, dma, dma((4,)), dma, dma, dma, dma, dma((5,)),
         ],
         compiler_params=pltpu.CompilerParams(collective_id=0, has_side_effects=True),
         name="front",
@@ -384,6 +380,7 @@
 
 ROW_OF = (0, 4, 2, 6)
 OWNER_AT = (0, 0, 2, 2, 1, 1, 3, 3)
+FULL = ((0, 1, 2), (1, 3, 4), (2, 4, 5))
 PAIRS = ((0, 0), (0, 1), (0, 2), (1, 1), (1, 2), (2, 2))
 EMIT, MASK, LIVE, LATE, FIRST, SECOND, SPREAD, JAC, PLANES = 0, 4, 16, 20, 24, 27, 39, 43, 55
 START, STEPS, DAMP, NORMAL = 0, 3, 4, 5
@@ -556,7 +553,6 @@
         moved = solve_three(normals, [fold(acc[i]) for i in range(3)], damp)
         position = [position[i] + jnp.where(moving, moved[i], 0.0) for i in range(3)]
         at_rows = [spread_rows(rows) for rows in position]
-        speed_rows = [spread_rows(rows) for rows in speed]
         acc = {key: None for key in range(9)}
         for k, part in tiles:
             which, masks = tile_masks(prep_ref, k, part)
@@ -565,8 +561,6 @@
             for i in range(3):
                 jac_ref[i, k, part, :] = jac[i]
             rate = nu_ref[k, part, :]
-            for i in range(3):
-                rate = rate - at_peak(which, speed_rows[i]) * jac[i]
             for key, (x, y) in enumerate(PAIRS):
                 add_to(acc, key, masks, jac[x] * jac[y])
             for i in range(3):
@@ -583,7 +577,19 @@
         shifted = jnp.concatenate([nested[24:], nested[:24]], axis=0)
         total = jnp.sum(jnp.where(low, nested, shifted) - whole, axis=1, keepdims=True)
         normals = [fold(acc[key]) for key in range(6)]
-        swung = solve_three(normals, [fold(acc[6 + i]) for i in range(3)], damp)
+        swung = solve_three(
+            normals,
+            [
+                fold(acc[6 + i])
+                - (
+                    normals[FULL[i][0]] * speed[0]
+                    + normals[FULL[i][1]] * speed[1]
+                    + normals[FULL[i][2]] * speed[2]
+                )
+                for i in range(3)
+            ],
+            damp,
+        )
         speed = [speed[i] + jnp.where(moving, swung[i], 0.0) for i in range(3)]
         bias = bias + jnp.broadcast_to(total, (RX, 128)) / (3.0 * 16 * RX)
         return position, speed, bias, normals

time: 39.8 us -> 39.3 us (0.987)
  Pallas kernels: 39.1 us -> 38.6 us
where the time goes in v9:
time: 39.3 us; the launch traced here: 39.2 us
  Pallas kernels  38.6 us (98%)
  between operations  0.64 us (2%)
    pallas_call x1, Pallas kernels, front(): pl.pallas_call(front_kernel, out_shape=(pltpu.VMEM((4, 16, 2, LAG_COUNT),...  33.7 us
    pallas_call x1, Pallas kernels, solve(): pl.pallas_call(solve_kernel, out_shape=(jax.ShapeDtypeStruct((3, 4), f32)...  4.85 us

profile of v9, /device:TPU:1, one launch (start us, length us, event | category | flops | bytes accessed | tf_op | source)
XLA Modules:
  0.0 39.2 jit_solution(6512068163647580373)
XLA Ops:
  0.6 33.7 %front.1 = (f32[4,16,2,1024]{3,2,1,0:T(2,128)S(1)}, f32[8,32,1,128]{3,2,1,0:T(1,128)S(1)}, f32[55,32,128]{2,1,0:T(8,128)S(1)}, f32[11,8,128]{2,1,0:T(8,128)S(1)}) custom-call(bf16[1,2,1024]{2,1,0:T(2,128)(2,1)} %raw_in.1, f32[1,4]{1,0:T(1,128)} %scl_in.1, s32[16,16]{1,0:T(8,128)} %lag_in.1, s32[16,16]{1,0:T(8,128)} %dop_in.1, s32[2,16]{1,0:T(2,128)} %bitcast.5, ...), custom_call_target="tpu_custom_call" | custom-call | tf_op jit(solution)/shard_map/front/pallas_call | solution.py:321
  34.4 4.8 %solve.1 = (f32[3,4]{1,0:T(4,128)}, f32[3,4]{1,0:T(4,128)}, f32[1,32]{1,0:T(1,128)}, f32[4,16,2,1024]{3,2,1,0:T(2,128)}) custom-call(f32[8,32,128]{2,1,0:T(8,128)S(1)} %bitcast.4, f32[55,32,128]{2,1,0:T(8,128)S(1)} %get-tuple-element.13.prep_ref, f32[11,8,128]{2,1,0:T(8,128)S(1)} %get-tuple-element.14.small_ref, f32[4,16,2,1024]{3,2,1,0:T(2,128)S(1)} %get-tuple-element.15.amb_in), custom_call_target="tpu_custom_call" | custom-call | tf_op jit(solution)/shard_map/solve/pallas_call | solution.py:618

commit v10 on v9

--- a/solution.py
+++ b/solution.py
@@ -131,13 +131,12 @@
 
     targets = [(r, p, 0) for _, p in blocks]
     targets += [(lax.rem(r + RX - 2 * t - i, RX), t, i) for t in range(TB) for i in (1, 2)]
-    for to_r, to_b, i in targets:
-        place = i * TB + b
-        for src, dst, ss, rs in (
-            (block_ref, raw_all, raw_send, raw_recv),
-            (pad_ref, scl_all, scl_send, scl_recv),
-        ):
-            remote(src, dst.at[place], ss, rs, (to_r, to_b)).start()
+    for src, dst, ss, rs in (
+        (block_ref, raw_all, raw_send, raw_recv),
+        (pad_ref, scl_all, scl_send, scl_recv),
+    ):
+        for to_r, to_b, i in targets:
+            remote(src, dst.at[i * TB + b], ss, rs, (to_r, to_b)).start()
     pltpu.make_async_copy(block_ref, raw_all.at[b], raw_recv).start()
     pltpu.make_async_copy(pad_ref, scl_all.at[b], scl_recv).start()
     for copy in loads[2:8]:
@@ -171,7 +170,6 @@
         remote(pay_ref.at[1], code_tab.at[b, r], code_send, code_recv, peer).start()
     peer = blocks[0]
     remote(raw_all, raw_all, raw_send, raw_recv, peer).wait_recv()
-    remote(scl_all, scl_all, scl_send, scl_recv, peer).wait_recv()
     for copy in loads[8:]:
         copy.wait()
 
@@ -180,6 +178,7 @@
     spec = spec + jnp.dot(raw, fwd_ref[256:512, :], preferred_element_type=f32)
     cos_part = spec[:, :FFT].reshape(3 * TB, 8, FFT)
     sin_part = spec[:, FFT:].reshape(3 * TB, 8, FFT)
+    remote(scl_all, scl_all, scl_send, scl_recv, blocks[0]).wait_recv()
     sub = iota((1, 8, 1), 1)
     sign = jnp.where(sub < 4, 1.0, -1.0).astype(f32)
     pick = iota((1, 8, 128), 2) == lax.rem(iota((1, 8, 128), 1), 4)

time: 39.3 us -> 39.9 us (1.015)
  Pallas kernels: 38.6 us -> 39.2 us
    pallas_call x1, Pallas kernels: 33.7 us -> 34.3 us  [front(): pl.pallas_call(front_kernel, out_shape=(pltpu.VMEM((4, 16, 2, LAG_COUNT),...]
where the time goes in v10:
time: 39.9 us; the launch traced here: 39.8 us
  Pallas kernels  39.2 us (98%)
  between operations  0.64 us (2%)
    pallas_call x1, Pallas kernels, front(): pl.pallas_call(front_kernel, out_shape=(pltpu.VMEM((4, 16, 2, LAG_COUNT),...  34.3 us
    pallas_call x1, Pallas kernels, solve(): pl.pallas_call(solve_kernel, out_shape=(jax.ShapeDtypeStruct((3, 4), f32)...  4.85 us

profile of v10, /device:TPU:1, one launch (start us, length us, event | category | flops | bytes accessed | tf_op | source)
XLA Modules:
  0.0 39.8 jit_solution(5600154026881935933)
XLA Ops:
  0.6 34.3 %front.1 = (f32[4,16,2,1024]{3,2,1,0:T(2,128)S(1)}, f32[8,32,1,128]{3,2,1,0:T(1,128)S(1)}, f32[55,32,128]{2,1,0:T(8,128)S(1)}, f32[11,8,128]{2,1,0:T(8,128)S(1)}) custom-call(bf16[1,2,1024]{2,1,0:T(2,128)(2,1)} %raw_in.1, f32[1,4]{1,0:T(1,128)} %scl_in.1, s32[16,16]{1,0:T(8,128)} %lag_in.1, s32[16,16]{1,0:T(8,128)} %dop_in.1, s32[2,16]{1,0:T(2,128)} %bitcast.5, ...), custom_call_target="tpu_custom_call" | custom-call | tf_op jit(solution)/shard_map/front/pallas_call | solution.py:320
  35.0 4.8 %solve.1 = (f32[3,4]{1,0:T(4,128)}, f32[3,4]{1,0:T(4,128)}, f32[1,32]{1,0:T(1,128)}, f32[4,16,2,1024]{3,2,1,0:T(2,128)}) custom-call(f32[8,32,128]{2,1,0:T(8,128)S(1)} %bitcast.4, f32[55,32,128]{2,1,0:T(8,128)S(1)} %get-tuple-element.13.prep_ref, f32[11,8,128]{2,1,0:T(8,128)S(1)} %get-tuple-element.14.small_ref, f32[4,16,2,1024]{3,2,1,0:T(2,128)S(1)} %get-tuple-element.15.amb_in), custom_call_target="tpu_custom_call" | custom-call | tf_op jit(solution)/shard_map/solve/pallas_call | solution.py:617
